TPU v7x, 128 devices: a whole 4x4x4 slice. The times are simulated.
128 devices in a mesh: gene: 16 (over y, x), samp: 8 (over z, core).
Axes of the slice: x: 4, y: 4, z: 4, core: 2. Of those that a mesh axis runs over, the one named last changes fastest.
Arguments:
- dosage: bfloat16 [12288, 10240], P('gene', 'samp'), may hold values from 0 to 2
- expression: float32 [10240, 32], P('samp', 'gene'), may hold values from -6 to 6
- perms: int32 [128, 10240], P(None, 'samp'), may hold values from 0 to 10239, each once within a row
- windows: int32 [32, 2], P('gene'), may hold values from 0 to 12288, as said below
- order: int32 [32], replicated, may hold values from 0 to 31, each once
Outputs:
- observed: float32 [32], P('gene')
- successive: float32 [32, 128], P('gene')
Inputs may be any that keep to these rules, and one draw needn't show every extreme that they name: `windows`: gene i's window [start, end) starts within the 768 variants before the block of variants i // 2 * 768 to (i // 2 + 1) * 768 - 1, or at 0, and ends within the 768 variants after that block, or at 12288; start < end.
All inputs are finite; a program needn't handle non-finite values.
Results may differ from a plain program's by a relative error of at most 0.0015.
Values may be sent and summed in bfloat16 or wider, within the bound.
No kernel may reach another device: no remote copies, remote signals or barrier semaphores. Data moves between devices by JAX's collectives and lax.ppermute only.
A program may use at most 128 MiB of HBM per device.

v0:
```python
import math

import jax
import jax.numpy as jnp
from jax import lax
from jax.sharding import PartitionSpec as P

epsilon = 1e-06


def joined_along(tiles, dim):
    dims = list(tiles.shape[1:])
    dims[dim] *= tiles.shape[0]
    return jnp.moveaxis(tiles, 0, dim).reshape(dims)


def from_everyone(shard, axis):
    copies = jnp.broadcast_to(shard, (lax.axis_size(axis), *shard.shape))
    return lax.all_to_all(copies, axis, split_axis=0, concat_axis=0, tiled=True)


def gather_directly(shard, axis, dim):
    return joined_along(from_everyone(shard, axis), dim)


def padded(block, sides, width):
    for axis, dim in sides:
        count = lax.axis_size(axis)
        forward = [(i, i + 1) for i in range(count - 1)]
        backward = [(target, source) for source, target in forward]
        low = lax.ppermute(
            lax.slice_in_dim(block, block.shape[dim] - width, None, axis=dim), axis, forward
        )
        high = lax.ppermute(lax.slice_in_dim(block, 0, width, axis=dim), axis, backward)
        block = jnp.concatenate([low, block, high], axis=dim)
    return block


def in_blocks(shard, dim, size):
    dims = shard.shape
    tiles = shard.reshape(*dims[:dim], size, dims[dim] // size, *dims[dim + 1 :])
    return jnp.moveaxis(tiles, dim, 0)


def sum_at_owner(shard, axis, dim):
    size = lax.axis_size(axis)
    tiles = lax.all_to_all(in_blocks(shard, dim, size), axis, 0, 0, tiled=True)
    return jnp.sum(tiles, axis=0)


def sent_together(arrays, axis, dim, along):
    widths = [math.prod(a.shape[along:]) for a in arrays]
    both = jnp.concatenate(
        [a.reshape(*a.shape[:along], w) for a, w in zip(arrays, widths)], axis=along
    )
    whole = sum_at_owner(both, axis, dim)
    tiles = jnp.split(whole, [sum(widths[:k]) for k in range(1, len(widths))], axis=along)
    return tuple((b.reshape(*whole.shape[:along], *a.shape[along:]) for a, b in zip(arrays, tiles)))


def taken_together(shard, axis):
    return from_everyone(shard, axis).max(axis=0)


def together(arrays, axis):
    ends = [0]
    for a in arrays:
        ends.append(ends[-1] + a.size)
    subtotal = taken_together(jnp.concatenate([a.ravel() for a in arrays]), axis)
    return tuple((subtotal[b:e].reshape(a.shape) for a, b, e in zip(arrays, ends, ends[1:])))


def permute_rows(wide, perms):
    permutations, samp_dev = perms.shape
    gene_cols = wide.shape[1]
    picked = jnp.take(wide, perms, axis=0)
    return jnp.transpose(picked, (1, 2, 0)).reshape(samp_dev, gene_cols * permutations)


def pick_rows(index, table):
    choose = (index[:, None] == jnp.arange(table.shape[0], dtype=jnp.int32)[None, :]).astype(
        jnp.float32
    )
    return jnp.dot(
        choose, table, precision=lax.Precision.HIGHEST, preferred_element_type=jnp.float32
    )


def on_device(dosage, expression, perms, windows, order):
    var_dev, samp_dev = dosage.shape
    gene_dev = expression.shape[1]
    permutations = perms.shape[0]
    samples = samp_dev * lax.axis_size("samp")
    gene_place = lax.axis_index("gene")
    samp_place = lax.axis_index("samp")
    every_sample = gather_directly(expression, "samp", 0)
    center = every_sample - jnp.mean(every_sample, axis=0, keepdims=True)
    scaled = center * lax.rsqrt(jnp.mean(center * center, axis=0, keepdims=True) + epsilon)
    standard = scaled.astype(jnp.bfloat16)
    wide = padded(standard, (("gene", 1),), gene_dev)
    bounds = padded(windows, (("gene", 0),), gene_dev)
    row_index = gene_place * var_dev + jnp.arange(var_dev, dtype=jnp.int32)
    gene_cols = wide.shape[1]
    row_count = dosage.shape[0]
    columns = lax.dynamic_slice_in_dim(wide, samp_place * samp_dev, samp_dev, 0)
    shuffled = permute_rows(wide, perms)
    totals = jnp.sum(dosage.astype(jnp.float32), axis=1)
    squares = jnp.sum(jnp.square(dosage.astype(jnp.float32)), axis=1)
    direct = jnp.dot(dosage, columns, preferred_element_type=jnp.float32)
    share_rows = row_count // lax.axis_size("samp")
    partial_value = sum_at_owner(
        jnp.dot(dosage, shuffled, preferred_element_type=jnp.float32), "samp", 0
    )
    direct, totals, squares = sent_together((direct, totals, squares), "samp", 0, 1)
    row_index = lax.dynamic_slice_in_dim(row_index, samp_place * share_rows, share_rows, 0)
    row_mean = totals / samples
    row_var = squares / samples - row_mean * row_mean + epsilon
    row_scale = lax.rsqrt(row_var * samples)
    inside = (row_index[:, None] >= bounds[None, :, 0]) & (row_index[:, None] < bounds[None, :, 1])
    values = (
        jnp.abs(partial_value).reshape(partial_value.shape[0], gene_cols, permutations)
        * row_scale[:, None, None]
    )
    maxima = jnp.max(jnp.where(inside[:, :, None], values, jnp.float32(0.0)), axis=0)
    observed = jnp.max(
        jnp.where(inside, jnp.abs(direct) * row_scale[:, None], jnp.float32(0.0)), axis=0
    )
    maxima, observed = together((maxima, observed), "samp")
    width = gene_dev * permutations
    left_part = jnp.concatenate([maxima[:gene_dev].reshape(width), observed[:gene_dev]])
    right_part = jnp.concatenate([maxima[2 * gene_dev :].reshape(width), observed[2 * gene_dev :]])
    packed = jnp.stack([left_part, right_part], axis=0)
    arrived = padded(packed, (("gene", 0),), 1)
    from_left = arrived[0]
    from_right = arrived[3]
    maxima = jnp.maximum(
        maxima[gene_dev : 2 * gene_dev],
        jnp.maximum(from_left[:width], from_right[:width]).reshape(gene_dev, permutations),
    )
    observed = jnp.maximum(
        observed[gene_dev : 2 * gene_dev], jnp.maximum(from_left[width:], from_right[width:])
    )
    everyone = gather_directly(maxima, "gene", 0)
    whole_suffix = lax.cummax(pick_rows(order, everyone), axis=0, reverse=True)
    successive = lax.dynamic_slice_in_dim(whole_suffix, gene_place * gene_dev, gene_dev, 0)
    return (observed, successive)


def solution(mesh):
    placed = (P("gene", "samp"), P("samp", "gene"), P(None, "samp"), P("gene", None), P())
    return jax.shard_map(
        on_device,
        mesh=mesh,
        in_specs=placed,
        out_specs=(P("gene"), P("gene", None)),
        check_vma=False,
    )
```

profile of v0, /device:TPU:0, one launch (start us, length us, event | category | flops | bytes accessed | tf_op | source)
XLA Modules:
  0.0 703.2 jit_solution(18379537026737769378)
XLA Ops:
  0.6 1.3 broadcast_in_dim.51
  2.0 5.4 all-to-all-start
  7.4 0.0 copy-start.2
  7.4 1.2 compare_select_fusion
  8.6 0.0 copy-start
  8.6 0.9 reshape.183
  9.5 1.2 broadcast_clamp_fusion
  10.7 0.0 copy-done.2
  10.7 0.8 and_bitcast_fusion
  11.6 1.6 all-to-all-done
  13.1 0.2 reduce_sum.54
  13.3 0.3 multiply_reduce_fusion
  13.6 0.1 multiply_convert_fusion
  13.7 1.3 collective-permute-start.3
  15.0 4.5 collective-permute-start.2
  19.6 0.0 copy-done
  19.6 0.6 convert_reduce_fusion
  20.2 0.1 concatenate.29
  20.3 0.1 concatenate.28
  20.4 0.0 collective-permute-done.3
  20.4 0.8 collective-permute-done.2
  21.2 0.1 pad_maximum_fusion
  21.4 1.3 copy.30
  22.6 2.2 convolution_bitcast_fusion
  24.8 0.1 concatenate.27
  24.9 0.6 pad_maximum_fusion.1
  25.6 3.3 all-to-all-start.2
  28.9 567.2 %gather_fusion = bf16[163840,6]{1,0:T(8,128)(2,1)} fusion(bf16[10240,6]{1,0:T(8,128)(2,1)S(1)} %copy.30, s32[163840]{0:T(1024)S(1)} %broadcast_clamp_fusion), kind=kCustom, calls=%fused_computation | custom fusion | bytes 4587520 | tf_op jit(solution)/shard_map/jit(_take)/gather | solution.py:76
  596.1 30.8 %copy.31 = bf16[128,1280,6]{1,0,2:T(8,128)(2,1)S(1)} copy(bf16[128,1280,6]{2,1,0:T(8,128)(2,1)} %bitcast.33) | data formatting | bytes 3932160 | tf_op jit(solution)/shard_map/jit(_take)/gather | solution.py:76
  626.9 0.0 copy-done.3
  626.9 0.0 copy-start.1
  626.9 0.3 bitcast_select_fusion
  627.2 1.2 copy-done.1
  628.4 3.1 fusion.9
  631.6 0.0 all-to-all-done.2
  631.6 4.9 all-to-all-start.1
  636.4 0.0 copy-done.4
  636.4 0.1 copy.26
  636.5 1.3 collective-permute-start.1
  637.8 4.8 collective-permute-start
  642.7 0.1 dynamic_slice.9
  642.8 0.0 collective-permute-done.1
  642.8 1.2 collective-permute-done
  644.0 0.1 pad_add_fusion
  644.1 0.2 select_reduce_fusion.1
  644.2 0.1 copy.29
  644.4 0.0 copy-start.5
  644.4 22.0 %all-to-all-done.1 = f32[8,96,768]{2,1,0:T(8,128)S(1)} async-done(((f32[8,96,768]{2,1,0:T(8,128)}), f32[8,96,768]{2,1,0:T(8,128)S(1)}, u32[]{:S(2)}, u32[]{:S(2)}) %all-to-all-start.1) | async-done | bytes 2359328 | tf_op jit(solution)/shard_map/all_to_all | solution.py:47
  666.4 0.1 reduce_sum.56
  666.6 0.3 select_reduce_fusion
  667.0 7.8 %all_to_all.26 = f32[8,1,774]{2,1,0:T(1,128)S(1)} all-to-all(f32[8,1,774]{2,1,0:T(1,128)S(1)} %broadcast_in_dim.56), channel_id=1, replica_groups=mesh['gene'=16,'samp'=8] {'samp'}, dimensions={0} | all-to-all | bytes 49536 | tf_op jit(solution)/shard_map/all_to_all | solution.py:19
  674.8 0.1 fusion.8
  674.9 1.3 collective-permute-start.5
  676.2 4.8 collective-permute-start.4
  681.0 0.0 collective-permute-done.5
  681.1 1.3 collective-permute-done.4
  682.3 0.6 broadcast_in_dim.57
  682.9 11.8 %all-to-all-start.4 = ((f32[16,2,128]{2,1,0:T(2,128)}), f32[16,2,128]{2,1,0:T(2,128)S(1)}, u32[]{:S(2)}, u32[]{:S(2)}) async-start(f32[16,2,128]{2,1,0:T(2,128)} %broadcast_in_dim.57), calls=%async_computation.4 | async-start | bytes 32768 | tf_op jit(solution)/shard_map/all_to_all | solution.py:19
  694.8 0.6 fusion.5
  695.4 7.0 all-to-all-done.4
  702.4 0.0 copy-done.5
  702.4 0.2 fusion.2
  702.5 0.1 reduce_window_max.10
  702.7 0.6 constant_dynamic-slice_fusion
  (21 shorter events, 0.2 us)
Async XLA Ops:
  2.0 11.1 %all-to-all-start = ((f32[8,1280,2]{1,2,0:T(2,128)}), f32[8,1280,2]{1,2,0:T(2,128)S(1)}, u32[]{:S(2)}, u32[]{:S(2)}) async-start(f32[8,1280,2]{1,2,0:T(2,128)} %broadcast_in_dim.51), calls=%async_computation | async-start | bytes 163840 | tf_op jit(solution)/shard_map/all_to_all | solution.py:19
  7.4 3.3 copy-start.2
  8.6 10.9 %copy-start = (bf16[768,1280]{1,0:T(8,128)(2,1)S(1)}, bf16[768,1280]{1,0:T(8,128)(2,1)}, u32[]{:S(2)}) copy-start(bf16[768,1280]{1,0:T(8,128)(2,1)} %param.5) | copy-start | bytes 5898244
  13.7 6.7 collective-permute-start.3
  15.0 6.2 collective-permute-start.2
  25.6 606.0 %all-to-all-start.2 = ((f32[8,96,8]{1,2,0:T(8,128)}), f32[8,96,8]{1,2,0:T(8,128)S(1)}, u32[]{:S(2)}, u32[]{:S(2)}) async-start(f32[8,96,8]{1,2,0:T(8,128)} %pad_maximum_fusion.1), calls=%async_computation.2 | async-start | bytes 65536 | tf_op jit(solution)/shard_map/all_to_all | solution.py:47
  596.0 30.8 %copy-start.3 = (pred[1280,128]{0,1:T(8,128)(4,1)S(1)}, pred[1280,128]{0,1:T(8,128)(4,1)}, u32[]{:S(2)}) copy-start(pred[1280,128]{0,1:T(8,128)(4,1)} %and_bitcast_fusion) | copy-start | bytes 491524
  626.9 1.5 copy-start.1
  631.6 4.9 copy-start.4
  631.6 34.8 %all-to-all-start.1 = ((f32[8,96,768]{2,1,0:T(8,128)}), f32[8,96,768]{2,1,0:T(8,128)S(1)}, u32[]{:S(2)}, u32[]{:S(2)}) async-start(f32[8,96,768]{2,1,0:T(8,128)} %bitcast.34), calls=%async_computation.1 | async-start | bytes 4718592 | tf_op jit(solution)/shard_map/all_to_all | solution.py:47
  636.5 6.2 collective-permute-start.1
  637.8 6.1 collective-permute-start
  644.4 58.0 %copy-start.5 = (s32[32]{0:T(128)S(1)}, s32[32]{0:T(128)}, u32[]{:S(2)}) copy-start(s32[32]{0:T(128)} %param.9) | copy-start | bytes 388
  674.9 6.2 collective-permute-start.5
  676.2 6.1 collective-permute-start.4
  682.9 19.4 %all-to-all-start.4 = ((f32[16,2,128]{2,1,0:T(2,128)}), f32[16,2,128]{2,1,0:T(2,128)S(1)}, u32[]{:S(2)}, u32[]{:S(2)}) async-start(f32[16,2,128]{2,1,0:T(2,128)} %broadcast_in_dim.57), calls=%async_computation.4 | async-start | bytes 32768 | tf_op jit(solution)/shard_map/all_to_all | solution.py:19
where the time goes:
time: 705 us; the launch traced here: 703 us
  local copies, waits for them, and re-layouts  605 us (86%)
  starting transfers between devices  43.5 us (6%)
  waiting for transfers between devices  33.9 us (5%)
  blocking collectives  7.78 us (1%)
    gather x2, local copies, waits for them, and re-layouts, permute_rows(): picked = jnp.take(wide, perms, axis=0)  598 us
    all_to_all x2, waiting for transfers between devices, sum_at_owner(): tiles = lax.all_to_all(in_blocks(shard, dim, size), axis, 0, 0, tiled=True)  22 us
    all_to_all x2, starting transfers between devices, from_everyone(): return lax.all_to_all(copies, axis, split_axis=0, concat_axis=0, tiled=True)  17.2 us
    ppermute x3, starting transfers between devices, padded(): lax.ppermute(lax.slice_in_dim(block, block.shape[dim] - width, None, axis...  14.2 us
  transfers between devices with their start and end apart: 10, of which 6 were waited for; matrix products, arithmetic and copies ran while one was open for 86% of the time, Pallas kernels for 0%

commit v1 on v0

v1 whole, which is shorter than its diff:
```python
import functools

import jax
import jax.numpy as jnp
from jax import lax
from jax.experimental import pallas as pl
from jax.experimental.pallas import tpu as pltpu
from jax.sharding import Mesh
from jax.sharding import PartitionSpec as P

epsilon = 1e-06
LANES = 128
TILE = 16
HALF = 8
CHUNKS = 2

VM = pl.BlockSpec(memory_space=pltpu.VMEM)
SM = pl.BlockSpec(memory_space=pltpu.SMEM)


def lane_gather(table, index):
    dims = lax.GatherDimensionNumbers(
        offset_dims=(),
        collapsed_slice_dims=(1,),
        start_index_map=(1,),
        operand_batching_dims=(0,),
        start_indices_batching_dims=(0,),
    )
    return lax.gather(
        table,
        index[..., None],
        dims,
        slice_sizes=(1, 1),
        mode=lax.GatherScatterMode.PROMISE_IN_BOUNDS,
    )


def gather_chunk(chunk, place, perms, table, out):
    z, c = place[1], place[2]
    table_rows = table.shape[1]
    tiles = perms.shape[1] // LANES
    group = 5

    def step(t, carry):
        block, part = t // (tiles // group), t % (tiles // group)
        kc, pair = block // 2, block % 2
        first = []
        for k in range(2):
            zz = lax.rem(z + pair * 2 + k, 4)
            cc = lax.rem(c + kc, 2)
            first.append(pl.multiple_of((zz * 2 + cc) * 2 * HALF + chunk * HALF, HALF))
        for u in range(group):
            lane = pl.ds(pl.multiple_of((part * group + u) * LANES, LANES), LANES)
            index = jnp.concatenate([perms[pl.ds(f, HALF), lane] for f in first], axis=0)
            low = (index & (LANES - 1)).astype(jnp.int16)
            high = (index >> 7).astype(jnp.int16)
            found = [jnp.zeros((TILE, LANES), jnp.bfloat16) for _ in range(2)]
            for r in range(table_rows):
                here = high == jnp.int16(r)
                for j in range(2):
                    found[j] = jnp.where(here, lane_gather(table[j, r], low), found[j])
            for j in range(2):
                row = pl.multiple_of(block * 2 * TILE + j * TILE, TILE)
                out[pl.ds(row, TILE), lane] = found[j]
        return carry

    lax.fori_loop(0, 4 * (tiles // group), step, 0)


def first_kernel(place, windows, every, perms, out, table):
    z, c = place[1], place[2]
    shards, genes, width = every.shape
    samples = shards * width
    own = every[z * 2 + c]
    direct = []
    for j in range(genes):
        x = every[:, j, :]
        mean = jnp.sum(x, keepdims=True) / samples
        center = x - mean
        scale = lax.rsqrt(jnp.sum(center * center, keepdims=True) / samples + epsilon)
        scaled = center * scale
        for k in range(shards):
            for i in range(width // LANES):
                piece = scaled[k : k + 1, i * LANES : (i + 1) * LANES]
                table[j, k * (width // LANES) + i] = jnp.broadcast_to(piece, (TILE, LANES)).astype(
                    jnp.bfloat16
                )
        direct.append((own[j : j + 1] - mean) * scale)
    row = lax.broadcasted_iota(jnp.int32, (TILE, width), 0)
    lane = lax.broadcasted_iota(jnp.int32, (TILE, width), 1)
    extra = jnp.where(row == 0, direct[0], jnp.where(row == 1, direct[1], 0.0))
    for j in range(genes):
        for b in range(2):
            w = windows[j, b]
            digits = ((w >> 7).astype(jnp.float32), (w & 127).astype(jnp.float32))
            for d in range(2):
                extra = jnp.where((row == 2 + d) & (lane == j * 2 + b), digits[d], extra)
    extra = jnp.where(row == 4, 1.0, extra)
    out[8 * TILE : 9 * TILE, :] = extra.astype(jnp.bfloat16)
    gather_chunk(0, place, perms, table, out)


def later_kernel(chunk, place, perms, table, out):
    gather_chunk(chunk, place, perms, table, out)


def times(rows, dosage):
    return lax.dot_general(
        rows, dosage, (((1,), (1,)), ((), ())), preferred_element_type=jnp.float32
    )


def product_kernel(with_stats, left, own, right, dosage, keep, send, *win):
    weights = dosage[...]
    small = []
    for o, ref in enumerate((left, own, right)):
        got = times(ref[: 8 * TILE, :], weights)
        for kc, dst in ((0, keep), (1, send)):
            for kz in range(4):
                for j in range(2):
                    src = kc * 64 + (kz // 2) * 32 + j * TILE + (kz % 2) * HALF
                    to = kz * 48 + (o * 2 + j) * HALF
                    dst[to : to + HALF, :] = got[src : src + HALF]
        if with_stats:
            small.append(times(ref[8 * TILE :, :], weights))
    if with_stats:
        variants, width = dosage.shape
        total = jnp.zeros((variants, LANES), jnp.float32)
        for i in range(width // LANES):
            d = dosage[:, i * LANES : (i + 1) * LANES].astype(jnp.float32)
            total = total + d * d
        squares = lax.dot_general(
            jnp.ones((8, LANES), jnp.float32),
            total,
            (((1,), (1,)), ((), ())),
            precision=lax.Precision.HIGHEST,
            preferred_element_type=jnp.float32,
        )
        stats = jnp.concatenate(
            [small[0][:2], small[1][:2], small[2][:2], small[1][4:5], squares[:1]], axis=0
        )
        keep[192:200, :] = stats
        send[192:200, :] = stats
        win_ref = win[0]
        win_ref[...] = jnp.zeros_like(win_ref)
        for o, ref in enumerate((left, own, right)):
            e = ref[8 * TILE :, :LANES].astype(jnp.float32)
            win_ref[o : o + 1, :] = e[2:3] * 128.0 + e[3:4]


def split_kernel(keep, got, *outs):
    for kz, out in enumerate(outs):
        out[:48, :] = keep[kz * 48 : kz * 48 + 48, :] + got[kz * 48 : kz * 48 + 48, :]
        if out.shape[0] > 48:
            out[48:, :] = keep[192:200, :] + got[192:200, :]


def maxima_kernel(samples, place, win, *refs):
    refs, out = refs[:-1], refs[-1]
    chunks = []
    for h in range(CHUNKS):
        part = refs[4 * h : 4 * h + 4]
        chunks.append((part[0][...] + part[1][...]) + (part[2][...] + part[3][...]))
    stats = chunks[0][48:56]
    mean = stats[6:7] / samples
    spread = stats[7:8] / samples - mean * mean + epsilon
    scale = lax.rsqrt(spread * samples)
    variants = scale.shape[1]
    index = lax.broadcasted_iota(jnp.int32, (1, variants), 1) + place[0] * variants
    index = index.astype(jnp.float32)
    lane = lax.broadcasted_iota(jnp.int32, (HALF, LANES), 1)
    tile = jnp.zeros((HALF, LANES), jnp.float32)
    direct = jnp.abs(stats) * scale
    for o in range(3):
        for j in range(2):
            n = o * 2 + j
            lo = win[o : o + 1, j * 2 : j * 2 + 1]
            hi = win[o : o + 1, j * 2 + 1 : j * 2 + 2]
            factor = (index >= lo) & (index < hi)
            for h in range(CHUNKS):
                v = jnp.abs(chunks[h][n * HALF : n * HALF + HALF]) * scale
                best = jnp.max(jnp.where(factor, v, 0.0), axis=1, keepdims=True)
                tile = jnp.where(lane == h * 6 + n, best, tile)
            best = jnp.max(jnp.where(factor, direct[n : n + 1], 0.0), axis=1, keepdims=True)
            tile = jnp.where(lane == 12 + n, best, tile)
    for i in range(out.shape[0]):
        out[i] = tile


def rank_kernel(place, order, blocks, out, observed, store):
    owners = blocks.shape[0]
    for o in range(owners):
        best = blocks[o]
        if o > 0:
            best = jnp.maximum(best, pltpu.roll(blocks[o - 1], LANES - 2, 1))
        if o < owners - 1:
            best = jnp.maximum(best, pltpu.roll(blocks[o + 1], 2, 1))
        store[2 * o] = best
        store[2 * o + 1] = pltpu.roll(best, LANES - 1, 1)
    g = place[0]
    zero = jnp.zeros((HALF, LANES), jnp.float32)
    tails = [zero, zero]
    for i in range(2 * owners):
        value = store[order[i]]
        for k in range(2):
            tails[k] = jnp.where(i >= 2 * g + k, jnp.maximum(tails[k], value), tails[k])
    lane = lax.broadcasted_iota(jnp.int32, (HALF, LANES), 1)
    tile = zero
    for k in range(2):
        for h in range(CHUNKS):
            tile = jnp.where(lane == 2 * k + h, tails[k][:, h * 6 + 2 : h * 6 + 3], tile)
    for i in range(out.shape[0]):
        out[i] = tile
    own = store[2 * g]
    observed[...] = jnp.concatenate([own[:1, 14:15], own[:1, 15:16]], axis=1)


def final_kernel(parts, out):
    lane = lax.broadcasted_iota(jnp.int32, (HALF, LANES), 1)
    row = lax.broadcasted_iota(jnp.int32, (HALF, LANES), 0)
    for k in range(2):
        spread = jnp.zeros((HALF, LANES), jnp.float32)
        for d in range(parts.shape[0]):
            for h in range(CHUNKS):
                column = parts[d, :, 2 * k + h : 2 * k + h + 1]
                spread = jnp.where(lane // HALF == d * 2 + h, column, spread)
        out[k : k + 1, :] = jnp.sum(
            jnp.where(lane % HALF == row, spread, 0.0), axis=0, keepdims=True
        )


def shape(dims, kind=jnp.float32):
    return jax.ShapeDtypeStruct(dims, kind)


def on_device(dosage, expression, perms, windows, order):
    variants, width = dosage.shape
    owners = lax.axis_size("gene")
    shards = 8
    samples = width * shards
    g, z, c = lax.axis_index("gene"), lax.axis_index("z"), lax.axis_index("core")
    place = jnp.stack([g, z, c]).astype(jnp.int32)
    copies = jnp.broadcast_to(expression.T[None], (shards, 2, width))
    every = lax.all_to_all(copies, ("z", "core"), 0, 0, tiled=True)

    table_shape = shape((2, samples // LANES, TILE, LANES), jnp.bfloat16)
    first, table = pl.pallas_call(
        first_kernel,
        out_shape=(shape((9 * TILE, width), jnp.bfloat16), table_shape),
        in_specs=[SM, SM, VM, VM],
        out_specs=(VM, VM),
        name="first_gather",
    )(place, windows, every, perms)
    shuffled = [first]
    for h in range(1, CHUNKS):
        shuffled.append(
            pl.pallas_call(
                functools.partial(later_kernel, h),
                out_shape=shape((8 * TILE, width), jnp.bfloat16),
                in_specs=[SM, VM, VM],
                out_specs=VM,
                name="later_gather",
            )(place, perms, table)
        )
    ahead = [(i, (i + 1) % owners) for i in range(owners)]
    back = [(b, a) for a, b in ahead]
    sums = []
    for h, own in enumerate(shuffled):
        left = lax.ppermute(own, "gene", ahead)
        right = lax.ppermute(own, "gene", back)
        rows = 200 if h == 0 else 192
        outs = [shape((rows, variants)), shape((rows, variants))]
        if h == 0:
            outs.append(shape((8, LANES)))
        made = pl.pallas_call(
            functools.partial(product_kernel, h == 0),
            out_shape=tuple(outs),
            in_specs=[VM] * 4,
            out_specs=tuple([VM] * len(outs)),
            name="products",
        )(left, own, right, dosage)
        if h == 0:
            win = made[2]
        keep, send = made[:2]
        got = lax.ppermute(send, "core", [(0, 1), (1, 0)])
        depth = 56 if h == 0 else 48
        parts = pl.pallas_call(
            split_kernel,
            out_shape=tuple([shape((depth, variants))] * 4),
            in_specs=[VM] * 2,
            out_specs=tuple([VM] * 4),
            name="split",
        )(keep, got)
        sums.append(parts[0])
        for k in range(1, 4):
            sums.append(lax.ppermute(parts[k], "z", [(i, (i + k) % 4) for i in range(4)]))
    tiles = pl.pallas_call(
        functools.partial(maxima_kernel, samples),
        out_shape=shape((owners, HALF, LANES)),
        in_specs=[SM] + [VM] * (1 + len(sums)),
        out_specs=VM,
        name="maxima",
    )(place, win, *sums)
    tiles = lax.all_to_all(tiles, "gene", 0, 0, tiled=True)
    tails, observed = pl.pallas_call(
        rank_kernel,
        out_shape=(shape((shards, HALF, LANES)), shape((1, 2))),
        in_specs=[SM, SM, VM],
        out_specs=(VM, VM),
        scratch_shapes=[pltpu.VMEM((2 * owners, HALF, LANES), jnp.float32)],
        name="rank",
    )(place, order, tiles)
    tails = lax.all_to_all(tails, ("z", "core"), 0, 0, tiled=True)
    successive = pl.pallas_call(
        final_kernel, out_shape=shape((2, LANES)), in_specs=[VM], out_specs=VM, name="final"
    )(tails)
    return observed.reshape(2), successive


def solution(mesh):
    split = Mesh(mesh.devices.reshape(16, 4, 2), ("gene", "z", "core"))
    samp = ("z", "core")
    placed = (P("gene", samp), P(samp, "gene"), P(None, samp), P("gene", None), P())
    return jax.shard_map(
        on_device,
        mesh=split,
        in_specs=placed,
        out_specs=(P("gene"), P("gene", None)),
        check_vma=False,
    )
```

time: 705 us -> 116 us (0.16)
  local copies, waits for them, and re-layouts: 605 us -> 7.46 us
  Pallas kernels: 0 us -> 41 us
  starting transfers between devices: 43.5 us -> 24.3 us
  waiting for transfers between devices: 33.9 us -> 17.1 us
  blocking collectives: 7.78 us -> 23 us
    gather x2 -> x0, local copies, waits for them, and re-layouts: 598 us -> none  [permute_rows(): picked = jnp.take(wide, perms, axis=0)]
    pallas_call x0 -> x9, Pallas kernels: none -> 41 us  [the longest x2 11.8 us: on_device(): pl.pallas_call(functools.partial(product_kernel, h == 0), out_shape=tuple...]
    all_to_all x4 -> x1, waiting for transfers between devices: 30.6 us -> 5.06 us  [on_device(): every = lax.all_to_all(copies, ('z', 'core'), 0, 0, tiled=True)]
    all_to_all x4 -> x1, starting transfers between devices: 25.4 us -> 5.43 us  [on_device(): every = lax.all_to_all(copies, ('z', 'core'), 0, 0, tiled=True)]
    all_to_all x1 -> x2, blocking collectives: 7.78 us -> 23 us  [the longest x1 13.5 us: on_device(): tiles = lax.all_to_all(tiles, 'gene', 0, 0, tiled=True)]
    ppermute x6 -> x12, waiting for transfers between devices: 3.3 us -> 12 us  [the longest x6 8.09 us: on_device(): lax.ppermute(parts[k], 'z', [(i, (i + k) % 4) for i in range(4)])]
    ppermute x6 -> x12, starting transfers between devices: 18.1 us -> 18.9 us  [the longest x2 9.2 us: on_device(): right = lax.ppermute(own, 'gene', back)]
  transfers between devices with their start and end apart: 10 -> 13, of which waited for: 6 -> 4; matrix products, arithmetic and copies ran while one was open for 86% -> 1% of each run, Pallas kernels for 0% -> 14%
where the time goes in v1:
time: 116 us; the launch traced here: 114 us
  Pallas kernels  41 us (35%)
  starting transfers between devices  24.3 us (21%)
  blocking collectives  23 us (20%)
  waiting for transfers between devices  17.1 us (15%)
  local copies, waits for them, and re-layouts  7.46 us (6%)
    all_to_all x1, blocking collectives, on_device(): tiles = lax.all_to_all(tiles, 'gene', 0, 0, tiled=True)  13.5 us
    pallas_call x2, Pallas kernels, on_device(): pl.pallas_call(functools.partial(product_kernel, h == 0), out_shape=tuple...  11.8 us
    pallas_call x1, Pallas kernels, on_device(): pl.pallas_call(first_kernel, out_shape=(shape((9 * TILE, width), jnp.bflo...  9.94 us
    pallas_call x1, Pallas kernels, on_device(): pl.pallas_call(functools.partial(later_kernel, h), out_shape=shape((8 * T...  9.62 us
    all_to_all x1, blocking collectives, on_device(): tails = lax.all_to_all(tails, ('z', 'core'), 0, 0, tiled=True)  9.5 us
    ppermute x2, starting transfers between devices, on_device(): right = lax.ppermute(own, 'gene', back)  9.2 us
    ppermute x6, starting transfers between devices, on_device(): lax.ppermute(parts[k], 'z', [(i, (i + k) % 4) for i in range(4)])  8.19 us
    ppermute x6, waiting for transfers between devices, on_device(): lax.ppermute(parts[k], 'z', [(i, (i + k) % 4) for i in range(4)])  8.09 us
  transfers between devices with their start and end apart: 13, of which 4 were waited for; matrix products, arithmetic and copies ran while one was open for 1% of the time, Pallas kernels for 14%

profile of v1, /device:TPU:0, one launch (start us, length us, event | category | flops | bytes accessed | tf_op | source)
XLA Modules:
  0.0 114.2 jit_solution(576044158211235292)
XLA Ops:
  0.6 1.4 %broadcast_in_dim.2 = f32[8,2,1280]{2,1,0:T(2,128)} broadcast(f32[2,1280]{1,0:T(2,128)} %bitcast.5), dimensions={1,2} | broadcast | bytes 92160 | tf_op jit(solution)/shard_map/broadcast_in_dim | solution.py:243
  2.0 5.4 %all-to-all-start = ((f32[8,2,1280]{2,1,0:T(2,128)}), f32[8,2,1280]{2,1,0:T(2,128)S(1)}, u32[]{:S(2)}, u32[]{:S(2)}) async-start(f32[8,2,1280]{2,1,0:T(2,128)} %broadcast_in_dim.2), calls=%async_computation | async-start | bytes 163840 | tf_op jit(solution)/shard_map/all_to_all | solution.py:244
  7.4 0.6 pad_add_fusion.place
  8.1 5.1 %all-to-all-done.every = f32[8,2,1280]{2,1,0:T(2,128)S(1)} async-done(((f32[8,2,1280]{2,1,0:T(2,128)}), f32[8,2,1280]{2,1,0:T(2,128)S(1)}, u32[]{:S(2)}, u32[]{:S(2)}) %all-to-all-start) | async-done | bytes 81952 | tf_op jit(solution)/shard_map/all_to_all | solution.py:244
  13.1 0.0 copy-start.4
  13.1 0.6 copy-done.4
  13.8 9.9 %first_gather.1 = (bf16[144,1280]{1,0:T(8,128)(2,1)}, bf16[2,80,16,128]{3,2,1,0:T(8,128)(2,1)}) custom-call(s32[3]{0:T(128)} %pad_add_fusion.place, s32[2,2]{1,0:T(2,128)} %windows.1, f32[8,2,1280]{2,1,0:T(2,128)} %copy-done.4, s32[128,1280]{1,0:T(8,128)} %perms.3), custom_call_target="tpu_custom_call" | custom-call | tf_op jit(solution)/shard_map/first_gather/pallas_call | solution.py:247
  23.7 9.6 %later_gather.1.own = bf16[128,1280]{1,0:T(8,128)(2,1)} custom-call(s32[3]{0:T(128)} %pad_add_fusion.place, s32[128,1280]{1,0:T(8,128)} %perms.3, bf16[2,80,16,128]{3,2,1,0:T(8,128)(2,1)} %get-tuple-element.27.table), custom_call_target="tpu_custom_call" | custom-call | tf_op jit(solution)/shard_map/later_gather/pallas_call | solution.py:257
  33.3 1.5 %collective-permute-start.6 = (bf16[128,1280]{1,0:T(8,128)(2,1)}, bf16[128,1280]{1,0:T(8,128)(2,1)S(1)}, u32[]{:S(2)}, u32[]{:S(2)}) collective-permute-start(bf16[128,1280]{1,0:T(8,128)(2,1)} %later_gather.1.own), channel_id=1, source_target_pairs={{0,8},{8,16},{16,24},{24,32},{32,40},{40,48},{48,56},{56,64},{64,7... | collective-permute-start | bytes 983048 | tf_op jit(solution)/shard_map/ppermute | solution.py:269
  34.8 3.9 %collective-permute-start.7 = (bf16[128,1280]{1,0:T(8,128)(2,1)}, bf16[128,1280]{1,0:T(8,128)(2,1)S(1)}, u32[]{:S(2)}, u32[]{:S(2)}) collective-permute-start(bf16[128,1280]{1,0:T(8,128)(2,1)} %later_gather.1.own), channel_id=1, source_target_pairs={{8,0},{16,8},{24,16},{32,24},{40,32},{48,40},{56,48},{64,56},{72,6... | collective-permute-start | bytes 983048 | tf_op jit(solution)/shard_map/ppermute | solution.py:270
  38.7 0.0 collective-permute-start
  38.7 5.3 %collective-permute-start.1 = (bf16[144,1280]{1,0:T(8,128)(2,1)}, bf16[144,1280]{1,0:T(8,128)(2,1)S(1)}, u32[]{:S(2)}, u32[]{:S(2)}) collective-permute-start(bf16[144,1280]{1,0:T(8,128)(2,1)} %get-tuple-element.19.own), channel_id=1, source_target_pairs={{8,0},{16,8},{24,16},{32,24},{40,32},{48,40},{56,48},{64,56},{72,6... | collective-permute-start | bytes 1105928 | tf_op jit(solution)/shard_map/ppermute | solution.py:270
  44.0 3.4 %collective-permute-done.6.left = bf16[128,1280]{1,0:T(8,128)(2,1)S(1)} collective-permute-done((bf16[128,1280]{1,0:T(8,128)(2,1)}, bf16[128,1280]{1,0:T(8,128)(2,1)S(1)}, u32[]{:S(2)}, u32[]{:S(2)}) %collective-permute-start.6) | collective-permute-done | bytes 327712 | tf_op jit(solution)/shard_map/ppermute | solution.py:269
  47.4 0.0 copy-start.5
  47.4 0.0 collective-permute-done.7.right
  47.4 0.7 copy-done.5
  48.1 0.0 copy-start.6
  48.1 0.7 copy-done.6
  48.9 4.9 %products.3 = (f32[192,768]{1,0:T(8,128)}, f32[192,768]{1,0:T(8,128)}) custom-call(bf16[128,1280]{1,0:T(8,128)(2,1)} %copy-done.5, bf16[128,1280]{1,0:T(8,128)(2,1)} %later_gather.1.own, bf16[128,1280]{1,0:T(8,128)(2,1)} %copy-done.6, bf16[768,1280]{1,0:T(8,128)(2,1)} %dosage.3), custom_call_target="tpu_custom_call" | custom-call | tf_op jit(solution)/shard_map/products/pallas_call | solution.py:275
  53.7 0.0 collective-permute-start.8
  53.7 0.5 collective-permute-done.left
  54.2 0.0 collective-permute-done.1.right
  54.2 0.7 copy-done.2
  55.0 0.0 copy-start.3
  55.0 0.7 copy-done.3
  55.7 6.9 %products.2 = (f32[200,768]{1,0:T(8,128)}, f32[200,768]{1,0:T(8,128)}, f32[8,128]{1,0:T(8,128)}) custom-call(bf16[144,1280]{1,0:T(8,128)(2,1)} %copy-done.2, bf16[144,1280]{1,0:T(8,128)(2,1)} %get-tuple-element.19.own, bf16[144,1280]{1,0:T(8,128)(2,1)} %copy-done.3, bf16[768,1280]{1,0:T(8,128)(2,1)} %dosage.3), custom_call_target="tpu_custom_call" | custom-call | tf_op jit(solution)/shard_map/products/pallas_call | solution.py:275
  62.6 0.0 collective-permute-start.2
  62.6 0.0 collective-permute-done.8.got
  62.6 0.0 copy-start.1
  62.6 0.8 copy-done.1
  63.5 2.1 %split.3 = (f32[48,768]{1,0:T(8,128)}, f32[48,768]{1,0:T(8,128)}, f32[48,768]{1,0:T(8,128)}, f32[48,768]{1,0:T(8,128)}) custom-call(f32[192,768]{1,0:T(8,128)} %get-tuple-element.28.keep, f32[192,768]{1,0:T(8,128)} %copy-done.1), custom_call_target="tpu_custom_call" | custom-call | tf_op jit(solution)/shard_map/split/pallas_call | solution.py:287
  65.6 0.9 collective-permute-start.10
  66.5 0.0 collective-permute-done.2.got
  66.5 0.0 copy-start
  66.5 0.9 copy-done
  67.4 2.1 %split.2 = (f32[56,768]{1,0:T(8,128)}, f32[56,768]{1,0:T(8,128)}, f32[56,768]{1,0:T(8,128)}, f32[56,768]{1,0:T(8,128)}) custom-call(f32[200,768]{1,0:T(8,128)} %get-tuple-element.21.keep, f32[200,768]{1,0:T(8,128)} %copy-done), custom_call_target="tpu_custom_call" | custom-call | tf_op jit(solution)/shard_map/split/pallas_call | solution.py:287
  69.5 1.1 collective-permute-start.3
  70.6 2.7 %collective-permute-start.4 = (f32[56,768]{1,0:T(8,128)}, f32[56,768]{1,0:T(8,128)S(1)}, u32[]{:S(2)}, u32[]{:S(2)}) collective-permute-start(f32[56,768]{1,0:T(8,128)} %get-tuple-element.25), channel_id=1, source_target_pairs={{0,4},{2,6},{4,0},{6,2},{1,5},{3,7},{5,1},{7,3},{8,12},{10,14},{12... | collective-permute-start | bytes 516104 | tf_op jit(solution)/shard_map/ppermute | solution.py:296
  73.3 1.5 %collective-permute-start.5 = (f32[56,768]{1,0:T(8,128)}, f32[56,768]{1,0:T(8,128)S(1)}, u32[]{:S(2)}, u32[]{:S(2)}) collective-permute-start(f32[56,768]{1,0:T(8,128)} %get-tuple-element.26), channel_id=1, source_target_pairs={{0,6},{2,0},{4,2},{6,4},{1,7},{3,1},{5,3},{7,5},{8,14},{10,8},{12,... | collective-permute-start | bytes 516104 | tf_op jit(solution)/shard_map/ppermute | solution.py:296
  74.7 0.0 collective-permute-start.11
  74.7 0.0 collective-permute-done.10.refs_6_
  74.7 0.0 copy-start.10
  74.7 2.0 %collective-permute-start.9 = (f32[48,768]{1,0:T(8,128)}, f32[48,768]{1,0:T(8,128)S(1)}, u32[]{:S(2)}, u32[]{:S(2)}) collective-permute-start(f32[48,768]{1,0:T(8,128)} %get-tuple-element.31), channel_id=1, source_target_pairs={{0,2},{2,4},{4,6},{6,0},{1,3},{3,5},{5,7},{7,1},{8,10},{10,12},{12... | collective-permute-start | bytes 442376 | tf_op jit(solution)/shard_map/ppermute | solution.py:296
  76.7 8.1 %collective-permute-done.11.refs_7_ = f32[48,768]{1,0:T(8,128)S(1)} collective-permute-done((f32[48,768]{1,0:T(8,128)}, f32[48,768]{1,0:T(8,128)S(1)}, u32[]{:S(2)}, u32[]{:S(2)}) %collective-permute-start.11) | collective-permute-done | bytes 147488 | tf_op jit(solution)/shard_map/ppermute | solution.py:296
  84.8 0.0 copy-start.11
  84.8 0.0 collective-permute-done.9.refs_5_
  84.8 0.0 copy-start.12
  84.8 0.0 collective-permute-done.3.refs_1_
  84.8 0.0 copy-start.7
  84.9 0.0 collective-permute-done.4.refs_2_
  84.9 0.0 copy-start.8
  84.9 0.0 collective-permute-done.5.refs_3_
  84.9 0.0 copy-start.9
  84.9 0.0 copy-done.10
  84.9 0.6 copy-done.11
  85.5 0.1 copy-done.12
  85.5 0.1 copy-done.7
  85.6 0.1 copy-done.8
  85.7 0.1 copy-done.9
  85.8 2.2 %maxima.1 = f32[16,8,128]{2,1,0:T(8,128)} custom-call(s32[3]{0:T(128)} %pad_add_fusion.place, f32[8,128]{1,0:T(8,128)} %get-tuple-element.20.win, f32[56,768]{1,0:T(8,128)} %get-tuple-element.23.refs_0_, f32[56,768]{1,0:T(8,128)} %copy-done.7, f32[56,768]{1,0:T(8,128)} %copy-done.8, f32[56,768]{1,0:T(8,128)} %copy-done.9, ...), custom_call_target="tpu_custom_call" | custom-call | tf_op jit(solution)/shard_map/maxima/pallas_call | solution.py:297
  88.0 13.5 %all_to_all.15.blocks = f32[16,8,128]{2,1,0:T(8,128)} all-to-all(f32[16,8,128]{2,1,0:T(8,128)} %maxima.1), channel_id=1, replica_groups=mesh['gene'=16,'z'=4,'core'=2] {'gene'}, dimensions={0} | all-to-all | bytes 131072 | tf_op jit(solution)/shard_map/all_to_all | solution.py:304
  101.5 1.8 %rank.1 = (f32[8,8,128]{2,1,0:T(8,128)}, f32[1,2]{1,0:T(1,128)}) custom-call(s32[3]{0:T(128)} %pad_add_fusion.place, s32[32]{0:T(128)} %order.1, f32[16,8,128]{2,1,0:T(8,128)} %all_to_all.15.blocks), custom_call_target="tpu_custom_call" | custom-call | tf_op jit(solution)/shard_map/rank/pallas_call | solution.py:305
  103.2 9.5 %all_to_all.16.parts = f32[8,8,128]{2,1,0:T(8,128)} all-to-all(f32[8,8,128]{2,1,0:T(8,128)} %get-tuple-element.35), channel_id=1, replica_groups=mesh['gene'=16,'z'=4,'core'=2] {'z','core'}, dimensions={0} | all-to-all | bytes 65536 | tf_op jit(solution)/shard_map/all_to_all | solution.py:313
  112.7 1.4 %final.1 = f32[2,128]{1,0:T(2,128)} custom-call(f32[8,8,128]{2,1,0:T(8,128)} %all_to_all.16.parts), custom_call_target="tpu_custom_call" | custom-call | tf_op jit(solution)/shard_map/final/pallas_call | solution.py:314
  (1 shorter events, 0.0 us)
Async XLA Ops:
  2.0 11.1 %all-to-all-start = ((f32[8,2,1280]{2,1,0:T(2,128)}), f32[8,2,1280]{2,1,0:T(2,128)S(1)}, u32[]{:S(2)}, u32[]{:S(2)}) async-start(f32[8,2,1280]{2,1,0:T(2,128)} %broadcast_in_dim.2), calls=%async_computation | async-start | bytes 163840 | tf_op jit(solution)/shard_map/all_to_all | solution.py:244
  13.1 0.6 copy-start.4
  33.3 14.1 %collective-permute-start.6 = (bf16[128,1280]{1,0:T(8,128)(2,1)}, bf16[128,1280]{1,0:T(8,128)(2,1)S(1)}, u32[]{:S(2)}, u32[]{:S(2)}) collective-permute-start(bf16[128,1280]{1,0:T(8,128)(2,1)} %later_gather.1.own), channel_id=1, source_target_pairs={{0,8},{8,16},{16,24},{24,32},{32,40},{40,48},{48,56},{56,64},{64,7... | collective-permute-start | bytes 983048 | tf_op jit(solution)/shard_map/ppermute | solution.py:269
  34.8 12.6 %collective-permute-start.7 = (bf16[128,1280]{1,0:T(8,128)(2,1)}, bf16[128,1280]{1,0:T(8,128)(2,1)S(1)}, u32[]{:S(2)}, u32[]{:S(2)}) collective-permute-start(bf16[128,1280]{1,0:T(8,128)(2,1)} %later_gather.1.own), channel_id=1, source_target_pairs={{8,0},{16,8},{24,16},{32,24},{40,32},{48,40},{56,48},{64,56},{72,6... | collective-permute-start | bytes 983048 | tf_op jit(solution)/shard_map/ppermute | solution.py:270
  38.7 15.6 %collective-permute-start = (bf16[144,1280]{1,0:T(8,128)(2,1)}, bf16[144,1280]{1,0:T(8,128)(2,1)S(1)}, u32[]{:S(2)}, u32[]{:S(2)}) collective-permute-start(bf16[144,1280]{1,0:T(8,128)(2,1)} %get-tuple-element.19.own), channel_id=1, source_target_pairs={{0,8},{8,16},{16,24},{24,32},{32,40},{40,48},{48,56},{56,64},{64,7... | collective-permute-start | bytes 1105928 | tf_op jit(solution)/shard_map/ppermute | solution.py:269
  38.7 15.6 %collective-permute-start.1 = (bf16[144,1280]{1,0:T(8,128)(2,1)}, bf16[144,1280]{1,0:T(8,128)(2,1)S(1)}, u32[]{:S(2)}, u32[]{:S(2)}) collective-permute-start(bf16[144,1280]{1,0:T(8,128)(2,1)} %get-tuple-element.19.own), channel_id=1, source_target_pairs={{8,0},{16,8},{24,16},{32,24},{40,32},{48,40},{56,48},{64,56},{72,6... | collective-permute-start | bytes 1105928 | tf_op jit(solution)/shard_map/ppermute | solution.py:270
  47.4 0.7 copy-start.5
  48.1 0.7 copy-start.6
  53.7 8.9 %collective-permute-start.8 = (f32[192,768]{1,0:T(8,128)}, f32[192,768]{1,0:T(8,128)S(1)}, u32[]{:S(2)}, u32[]{:S(2)}) collective-permute-start(f32[192,768]{1,0:T(8,128)} %get-tuple-element.29), channel_id=1, source_target_pairs={{0,1},{1,0},{2,3},{3,2},{4,5},{5,4},{6,7},{7,6},{8,9},{9,8},{10,11... | collective-permute-start | bytes 1769480 | tf_op jit(solution)/shard_map/ppermute | solution.py:285
  54.2 0.7 copy-start.2
  55.0 0.7 copy-start.3
  62.6 3.9 %collective-permute-start.2 = (f32[200,768]{1,0:T(8,128)}, f32[200,768]{1,0:T(8,128)S(1)}, u32[]{:S(2)}, u32[]{:S(2)}) collective-permute-start(f32[200,768]{1,0:T(8,128)} %get-tuple-element.22), channel_id=1, source_target_pairs={{0,1},{1,0},{2,3},{3,2},{4,5},{5,4},{6,7},{7,6},{8,9},{9,8},{10,11... | collective-permute-start | bytes 1843208 | tf_op jit(solution)/shard_map/ppermute | solution.py:285
  62.6 0.8 copy-start.1
  65.6 9.2 %collective-permute-start.10 = (f32[48,768]{1,0:T(8,128)}, f32[48,768]{1,0:T(8,128)S(1)}, u32[]{:S(2)}, u32[]{:S(2)}) collective-permute-start(f32[48,768]{1,0:T(8,128)} %get-tuple-element.32), channel_id=1, source_target_pairs={{0,4},{2,6},{4,0},{6,2},{1,5},{3,7},{5,1},{7,3},{8,12},{10,14},{12... | collective-permute-start | bytes 442376 | tf_op jit(solution)/shard_map/ppermute | solution.py:296
  66.5 0.9 copy-start
  69.5 15.3 %collective-permute-start.3 = (f32[56,768]{1,0:T(8,128)}, f32[56,768]{1,0:T(8,128)S(1)}, u32[]{:S(2)}, u32[]{:S(2)}) collective-permute-start(f32[56,768]{1,0:T(8,128)} %get-tuple-element.24), channel_id=1, source_target_pairs={{0,2},{2,4},{4,6},{6,0},{1,3},{3,5},{5,7},{7,1},{8,10},{10,12},{12... | collective-permute-start | bytes 516104 | tf_op jit(solution)/shard_map/ppermute | solution.py:296
  70.6 14.3 %collective-permute-start.4 = (f32[56,768]{1,0:T(8,128)}, f32[56,768]{1,0:T(8,128)S(1)}, u32[]{:S(2)}, u32[]{:S(2)}) collective-permute-start(f32[56,768]{1,0:T(8,128)} %get-tuple-element.25), channel_id=1, source_target_pairs={{0,4},{2,6},{4,0},{6,2},{1,5},{3,7},{5,1},{7,3},{8,12},{10,14},{12... | collective-permute-start | bytes 516104 | tf_op jit(solution)/shard_map/ppermute | solution.py:296
  73.3 11.6 %collective-permute-start.5 = (f32[56,768]{1,0:T(8,128)}, f32[56,768]{1,0:T(8,128)S(1)}, u32[]{:S(2)}, u32[]{:S(2)}) collective-permute-start(f32[56,768]{1,0:T(8,128)} %get-tuple-element.26), channel_id=1, source_target_pairs={{0,6},{2,0},{4,2},{6,4},{1,7},{3,1},{5,3},{7,5},{8,14},{10,8},{12,... | collective-permute-start | bytes 516104 | tf_op jit(solution)/shard_map/ppermute | solution.py:296
  74.7 10.1 %collective-permute-start.11 = (f32[48,768]{1,0:T(8,128)}, f32[48,768]{1,0:T(8,128)S(1)}, u32[]{:S(2)}, u32[]{:S(2)}) collective-permute-start(f32[48,768]{1,0:T(8,128)} %get-tuple-element.33), channel_id=1, source_target_pairs={{0,6},{2,0},{4,2},{6,4},{1,7},{3,1},{5,3},{7,5},{8,14},{10,8},{12,... | collective-permute-start | bytes 442376 | tf_op jit(solution)/shard_map/ppermute | solution.py:296
  74.7 10.2 %copy-start.10 = (f32[48,768]{1,0:T(8,128)}, f32[48,768]{1,0:T(8,128)S(1)}, u32[]{:S(2)}) copy-start(f32[48,768]{1,0:T(8,128)S(1)} %collective-permute-done.10.refs_6_) | copy-start | bytes 442372
  74.7 10.1 %collective-permute-start.9 = (f32[48,768]{1,0:T(8,128)}, f32[48,768]{1,0:T(8,128)S(1)}, u32[]{:S(2)}, u32[]{:S(2)}) collective-permute-start(f32[48,768]{1,0:T(8,128)} %get-tuple-element.31), channel_id=1, source_target_pairs={{0,2},{2,4},{4,6},{6,0},{1,3},{3,5},{5,7},{7,1},{8,10},{10,12},{12... | collective-permute-start | bytes 442376 | tf_op jit(solution)/shard_map/ppermute | solution.py:296
  84.8 0.7 copy-start.11
  84.8 0.7 copy-start.12
  84.8 0.8 copy-start.7
  84.9 0.8 copy-start.8
  84.9 0.9 copy-start.9

commit v2 on v1

--- a/solution.py
+++ b/solution.py
@@ -7,6 +7,7 @@
 from jax.experimental.pallas import tpu as pltpu
 from jax.sharding import Mesh
 from jax.sharding import PartitionSpec as P
+
 
 epsilon = 1e-06
 LANES = 128
@@ -110,7 +111,26 @@
     )
 
 
-def product_kernel(with_stats, left, own, right, dosage, keep, send, *win):
+def squares_kernel(dosage, out):
+    variants, width = dosage.shape
+    total = jnp.zeros((variants, LANES), jnp.float32)
+    for i in range(width // LANES):
+        d = dosage[:, i * LANES : (i + 1) * LANES].astype(jnp.float32)
+        total = total + d * d
+    out[...] = lax.dot_general(
+        jnp.ones((8, LANES), jnp.float32),
+        total,
+        (((1,), (1,)), ((), ())),
+        precision=lax.Precision.HIGHEST,
+        preferred_element_type=jnp.float32,
+    )
+
+
+def product_kernel(with_stats, left, own, right, dosage, *refs):
+    if with_stats:
+        squares, keep, send, win_ref = refs
+    else:
+        keep, send = refs
     weights = dosage[...]
     small = []
     for o, ref in enumerate((left, own, right)):
@@ -124,24 +144,11 @@
         if with_stats:
             small.append(times(ref[8 * TILE :, :], weights))
     if with_stats:
-        variants, width = dosage.shape
-        total = jnp.zeros((variants, LANES), jnp.float32)
-        for i in range(width // LANES):
-            d = dosage[:, i * LANES : (i + 1) * LANES].astype(jnp.float32)
-            total = total + d * d
-        squares = lax.dot_general(
-            jnp.ones((8, LANES), jnp.float32),
-            total,
-            (((1,), (1,)), ((), ())),
-            precision=lax.Precision.HIGHEST,
-            preferred_element_type=jnp.float32,
-        )
         stats = jnp.concatenate(
             [small[0][:2], small[1][:2], small[2][:2], small[1][4:5], squares[:1]], axis=0
         )
         keep[192:200, :] = stats
         send[192:200, :] = stats
-        win_ref = win[0]
         win_ref[...] = jnp.zeros_like(win_ref)
         for o, ref in enumerate((left, own, right)):
             e = ref[8 * TILE :, :LANES].astype(jnp.float32)
@@ -171,66 +178,86 @@
     lane = lax.broadcasted_iota(jnp.int32, (HALF, LANES), 1)
     tile = jnp.zeros((HALF, LANES), jnp.float32)
     direct = jnp.abs(stats) * scale
+    row = lax.broadcasted_iota(jnp.int32, (HALF, LANES), 0)
+    seen = []
     for o in range(3):
         for j in range(2):
             n = o * 2 + j
             lo = win[o : o + 1, j * 2 : j * 2 + 1]
             hi = win[o : o + 1, j * 2 + 1 : j * 2 + 2]
-            factor = (index >= lo) & (index < hi)
+            inside = (index >= lo) & (index < hi)
             for h in range(CHUNKS):
                 v = jnp.abs(chunks[h][n * HALF : n * HALF + HALF]) * scale
-                best = jnp.max(jnp.where(factor, v, 0.0), axis=1, keepdims=True)
-                tile = jnp.where(lane == h * 6 + n, best, tile)
-            best = jnp.max(jnp.where(factor, direct[n : n + 1], 0.0), axis=1, keepdims=True)
-            tile = jnp.where(lane == 12 + n, best, tile)
-    for i in range(out.shape[0]):
-        out[i] = tile
-
-
-def rank_kernel(place, order, blocks, out, observed, store):
-    owners = blocks.shape[0]
+                best = jnp.max(jnp.where(inside, v, 0.0), axis=1, keepdims=True)
+                tile = jnp.where(lane // HALF == n * CHUNKS + h, best, tile)
+            seen.append(
+                jnp.max(jnp.where(inside, direct[n : n + 1], 0.0), axis=1, keepdims=True)
+            )
+    line = jnp.sum(jnp.where(lane % HALF == row, tile, 0.0), axis=0, keepdims=True)
+    for n in range(6):
+        line = jnp.where(lane[:1] == 96 + n, seen[n], line)
+    for i in range(out.shape[0] // HALF):
+        out[i * HALF : (i + 1) * HALF, :] = jnp.broadcast_to(line, (HALF, LANES))
+
+
+def final_kernel(place, order, parts, out, observed, store):
+    shards = HALF
+    owners = parts.shape[0] // shards
+    block = lambda o: parts[o * shards : (o + 1) * shards, :]
+    width = 2 * HALF
     for o in range(owners):
-        best = blocks[o]
+        best = block(o)
         if o > 0:
-            best = jnp.maximum(best, pltpu.roll(blocks[o - 1], LANES - 2, 1))
+            best = jnp.maximum(best, pltpu.roll(block(o - 1), LANES - 2 * width, 1))
         if o < owners - 1:
-            best = jnp.maximum(best, pltpu.roll(blocks[o + 1], 2, 1))
+            best = jnp.maximum(best, pltpu.roll(block(o + 1), 2 * width, 1))
         store[2 * o] = best
-        store[2 * o + 1] = pltpu.roll(best, LANES - 1, 1)
+        store[2 * o + 1] = pltpu.roll(best, LANES - width, 1)
     g = place[0]
-    zero = jnp.zeros((HALF, LANES), jnp.float32)
+    zero = jnp.zeros((shards, LANES), jnp.float32)
     tails = [zero, zero]
     for i in range(2 * owners):
         value = store[order[i]]
         for k in range(2):
             tails[k] = jnp.where(i >= 2 * g + k, jnp.maximum(tails[k], value), tails[k])
-    lane = lax.broadcasted_iota(jnp.int32, (HALF, LANES), 1)
-    tile = zero
+    lane = lax.broadcasted_iota(jnp.int32, (shards, LANES), 1)
+    row = lax.broadcasted_iota(jnp.int32, (shards, LANES), 0)
     for k in range(2):
-        for h in range(CHUNKS):
-            tile = jnp.where(lane == 2 * k + h, tails[k][:, h * 6 + 2 : h * 6 + 3], tile)
-    for i in range(out.shape[0]):
-        out[i] = tile
-    own = store[2 * g]
-    observed[...] = jnp.concatenate([own[:1, 14:15], own[:1, 15:16]], axis=1)
-
-
-def final_kernel(parts, out):
-    lane = lax.broadcasted_iota(jnp.int32, (HALF, LANES), 1)
-    row = lax.broadcasted_iota(jnp.int32, (HALF, LANES), 0)
-    for k in range(2):
-        spread = jnp.zeros((HALF, LANES), jnp.float32)
-        for d in range(parts.shape[0]):
-            for h in range(CHUNKS):
-                column = parts[d, :, 2 * k + h : 2 * k + h + 1]
-                spread = jnp.where(lane // HALF == d * 2 + h, column, spread)
+        moved = pltpu.roll(tails[k], LANES - 2 * width, 1)
+        moved = pltpu.roll(moved, 0, 1, stride=width, stride_axis=0)
         out[k : k + 1, :] = jnp.sum(
-            jnp.where(lane % HALF == row, spread, 0.0), axis=0, keepdims=True
+            jnp.where(lane // width == row, moved, 0.0), axis=0, keepdims=True
         )
+    part = lambda o: parts[pl.ds(pl.multiple_of(o * shards, shards), shards), :][:1]
+    seen = part(g)
+    left = pltpu.roll(part(jnp.maximum(g - 1, 0)), LANES - 2, 1)
+    right = pltpu.roll(part(jnp.minimum(g + 1, owners - 1)), 2, 1)
+    seen = jnp.maximum(seen, jnp.where(g > 0, left, 0.0))
+    seen = jnp.maximum(seen, jnp.where(g < owners - 1, right, 0.0))
+    observed[...] = seen[:, 98:100]
+
+
+def call(kernel, outs, args, us, scratch=()):
+    scalar = [a.size <= 64 for a in args]
+    many = isinstance(outs, list)
+    made = pl.pallas_call(
+        kernel,
+        out_shape=tuple(outs) if many else outs,
+        in_specs=[SM if k else VM for k in scalar],
+        out_specs=tuple([VM] * len(outs)) if many else VM,
+        scratch_shapes=scratch,
+        compiler_params=pltpu.CompilerParams(vmem_limit_bytes=24 << 20),
+        cost_estimate=pl.CostEstimate(flops=int(us * 1e9), bytes_accessed=0, transcendentals=0),
+    )
+    args = [
+        a if k else pltpu.with_memory_space_constraint(a, pltpu.VMEM)
+        for a, k in zip(args, scalar)
+    ]
+    return made(*args)
 
 
 def shape(dims, kind=jnp.float32):
-    return jax.ShapeDtypeStruct(dims, kind)
+    return pltpu.VMEM(dims, kind)
 
 
 def on_device(dosage, expression, perms, windows, order):
@@ -243,24 +270,23 @@
     copies = jnp.broadcast_to(expression.T[None], (shards, 2, width))
     every = lax.all_to_all(copies, ("z", "core"), 0, 0, tiled=True)
 
+    squares = call(squares_kernel, shape((8, variants)), [dosage], 1)
     table_shape = shape((2, samples // LANES, TILE, LANES), jnp.bfloat16)
-    first, table = pl.pallas_call(
+    first, table = call(
         first_kernel,
-        out_shape=(shape((9 * TILE, width), jnp.bfloat16), table_shape),
-        in_specs=[SM, SM, VM, VM],
-        out_specs=(VM, VM),
-        name="first_gather",
-    )(place, windows, every, perms)
+        [shape((9 * TILE, width), jnp.bfloat16), table_shape],
+        [place, windows, every, perms],
+        9,
+    )
     shuffled = [first]
     for h in range(1, CHUNKS):
         shuffled.append(
-            pl.pallas_call(
+            call(
                 functools.partial(later_kernel, h),
-                out_shape=shape((8 * TILE, width), jnp.bfloat16),
-                in_specs=[SM, VM, VM],
-                out_specs=VM,
-                name="later_gather",
-            )(place, perms, table)
+                shape((8 * TILE, width), jnp.bfloat16),
+                [place, perms, table],
+                9,
+            )
         )
     ahead = [(i, (i + 1) % owners) for i in range(owners)]
     back = [(b, a) for a, b in ahead]
@@ -270,50 +296,34 @@
         right = lax.ppermute(own, "gene", back)
         rows = 200 if h == 0 else 192
         outs = [shape((rows, variants)), shape((rows, variants))]
+        args = [left, own, right, dosage]
         if h == 0:
             outs.append(shape((8, LANES)))
-        made = pl.pallas_call(
-            functools.partial(product_kernel, h == 0),
-            out_shape=tuple(outs),
-            in_specs=[VM] * 4,
-            out_specs=tuple([VM] * len(outs)),
-            name="products",
-        )(left, own, right, dosage)
+            args.append(squares)
+        made = call(functools.partial(product_kernel, h == 0), outs, args, 4)
         if h == 0:
             win = made[2]
         keep, send = made[:2]
         got = lax.ppermute(send, "core", [(0, 1), (1, 0)])
         depth = 56 if h == 0 else 48
-        parts = pl.pallas_call(
-            split_kernel,
-            out_shape=tuple([shape((depth, variants))] * 4),
-            in_specs=[VM] * 2,
-            out_specs=tuple([VM] * 4),
-            name="split",
-        )(keep, got)
+        parts = call(split_kernel, [shape((depth, variants))] * 4, [keep, got], 1)
         sums.append(parts[0])
         for k in range(1, 4):
             sums.append(lax.ppermute(parts[k], "z", [(i, (i + k) % 4) for i in range(4)]))
-    tiles = pl.pallas_call(
-        functools.partial(maxima_kernel, samples),
-        out_shape=shape((owners, HALF, LANES)),
-        in_specs=[SM] + [VM] * (1 + len(sums)),
-        out_specs=VM,
-        name="maxima",
-    )(place, win, *sums)
-    tiles = lax.all_to_all(tiles, "gene", 0, 0, tiled=True)
-    tails, observed = pl.pallas_call(
-        rank_kernel,
-        out_shape=(shape((shards, HALF, LANES)), shape((1, 2))),
-        in_specs=[SM, SM, VM],
-        out_specs=(VM, VM),
-        scratch_shapes=[pltpu.VMEM((2 * owners, HALF, LANES), jnp.float32)],
-        name="rank",
-    )(place, order, tiles)
-    tails = lax.all_to_all(tails, ("z", "core"), 0, 0, tiled=True)
-    successive = pl.pallas_call(
-        final_kernel, out_shape=shape((2, LANES)), in_specs=[VM], out_specs=VM, name="final"
-    )(tails)
+    everyone = owners * shards
+    lines = call(
+        functools.partial(maxima_kernel, samples), shape((everyone, LANES)), [place, win, *sums], 2
+    )
+    lines = lax.all_to_all(
+        lines.reshape(everyone, 1, LANES), ("gene", "z", "core"), 0, 0, tiled=True
+    ).reshape(everyone, LANES)
+    successive, observed = call(
+        final_kernel,
+        [shape((2, LANES)), shape((1, 2))],
+        [place, order, lines],
+        2,
+        [pltpu.VMEM((2 * owners, HALF, LANES), jnp.float32)],
+    )
     return observed.reshape(2), successive
 
 

time: 116 us -> 95.2 us (0.82); the launches traced: 114 us -> 94.7 us
  Pallas kernels: 41 us -> 25 us
  waiting for transfers between devices: 17.1 us -> 24.8 us
  blocking collectives: 23 us -> 17.3 us
  local copies, waits for them, and re-layouts: 7.46 us -> 4.2 us
  starting transfers between devices: 24.3 us -> 22.6 us
    pallas_call x9, Pallas kernels: 41 us -> 25 us  [call(): return made(*args)]
    all_to_all x2 -> x1, blocking collectives: 23 us -> 17.3 us  [on_device(): lax.all_to_all(lines.reshape(everyone, 1, LANES), ('gene', 'z', 'core'),...]
    ppermute x2, waiting for transfers between devices: 3.9 us -> 7.21 us  [on_device(): left = lax.ppermute(own, 'gene', ahead)]
    unnamed x26 -> x12, local copies, waits for them, and re-layouts: 6.1 us -> 2.86 us
    ppermute x6, waiting for transfers between devices: 8.09 us -> 11 us  [on_device(): lax.ppermute(parts[k], 'z', [(i, (i + k) % 4) for i in range(4)])]
    ppermute x6, starting transfers between devices: 8.19 us -> 6.34 us  [on_device(): lax.ppermute(parts[k], 'z', [(i, (i + k) % 4) for i in range(4)])]
  transfers between devices with their start and end apart: 13 -> 13, of which waited for: 4 -> 7; matrix products, arithmetic and copies ran while one was open for 1% -> 0% of each run, Pallas kernels for 14% -> 7%
where the time goes in v2:
time: 95.2 us; the launch traced here: 94.7 us
  Pallas kernels  25 us (26%)
  waiting for transfers between devices  24.8 us (26%)
  starting transfers between devices  22.6 us (24%)
  blocking collectives  17.3 us (18%)
  local copies, waits for them, and re-layouts  4.2 us (4%)
    pallas_call x9, Pallas kernels, call(): return made(*args)  25 us
    all_to_all x1, blocking collectives, on_device(): lax.all_to_all(lines.reshape(everyone, 1, LANES), ('gene', 'z', 'core'),...  17.3 us
    ppermute x6, waiting for transfers between devices, on_device(): lax.ppermute(parts[k], 'z', [(i, (i + k) % 4) for i in range(4)])  11 us
    ppermute x2, starting transfers between devices, on_device(): right = lax.ppermute(own, 'gene', back)  9.22 us
    ppermute x2, waiting for transfers between devices, on_device(): left = lax.ppermute(own, 'gene', ahead)  7.21 us
    ppermute x6, starting transfers between devices, on_device(): lax.ppermute(parts[k], 'z', [(i, (i + k) % 4) for i in range(4)])  6.34 us
    all_to_all x1, waiting for transfers between devices, on_device(): every = lax.all_to_all(copies, ('z', 'core'), 0, 0, tiled=True)  5.63 us
    all_to_all x1, starting transfers between devices, on_device(): every = lax.all_to_all(copies, ('z', 'core'), 0, 0, tiled=True)  5.43 us
  transfers between devices with their start and end apart: 13, of which 7 were waited for; matrix products, arithmetic and copies ran while one was open for 0% of the time, Pallas kernels for 7%

profile of v2, /device:TPU:0, one launch (start us, length us, event | category | flops | bytes accessed | tf_op | source)
XLA Modules:
  0.0 94.7 jit_solution(13571215428463971624)
XLA Ops:
  0.6 1.3 %broadcast_in_dim.2 = f32[8,2,1280]{2,1,0:T(2,128)} broadcast(f32[2,1280]{1,0:T(2,128)} %bitcast.12), dimensions={1,2} | broadcast | bytes 92160 | tf_op jit(solution)/shard_map/broadcast_in_dim | solution.py:270
  2.0 5.4 %all-to-all-start = ((f32[8,2,1280]{2,1,0:T(2,128)}), f32[8,2,1280]{2,1,0:T(2,128)S(1)}, u32[]{:S(2)}, u32[]{:S(2)}) async-start(f32[8,2,1280]{2,1,0:T(2,128)} %broadcast_in_dim.2), calls=%async_computation | async-start | bytes 163840 | tf_op jit(solution)/shard_map/all_to_all | solution.py:271
  7.4 0.1 pad_add_fusion.place
  7.5 5.6 %all-to-all-done.every = f32[8,2,1280]{2,1,0:T(2,128)S(1)} async-done(((f32[8,2,1280]{2,1,0:T(2,128)}), f32[8,2,1280]{2,1,0:T(2,128)S(1)}, u32[]{:S(2)}, u32[]{:S(2)}) %all-to-all-start) | async-done | bytes 81952 | tf_op jit(solution)/shard_map/all_to_all | solution.py:271
  13.1 0.0 copy-start.1
  13.1 1.1 %copy-done.1 = s32[128,1280]{1,0:T(8,128)S(1)} copy-done((s32[128,1280]{1,0:T(8,128)S(1)}, s32[128,1280]{1,0:T(8,128)}, u32[]{:S(2)}) %copy-start.1) | copy-done | bytes 655384
  14.2 0.0 copy-start.3
  14.2 0.7 copy-done.3
  14.9 0.0 copy-start.2
  14.9 8.7 %shard_map.68 = (bf16[144,1280]{1,0:T(8,128)(2,1)S(1)}, bf16[2,80,16,128]{3,2,1,0:T(8,128)(2,1)S(1)}) custom-call(s32[3]{0:T(128)S(1)} %pad_add_fusion.place, s32[2,2]{1,0:T(2,128)S(1)} %copy-done.3, f32[8,2,1280]{2,1,0:T(2,128)S(1)} %all-to-all-done.every, s32[128,1280]{1,0:T(8,128)S(1)} %copy-done.1), custom_call_target="tpu_custom_call" | custom-call | flops 8999999488 | tf_op jit(solution)/shard_map/pallas_call | solution.py:256
  23.6 0.0 copy-done.2
  23.6 0.0 copy-start
  23.6 8.2 %shard_map.72.own = bf16[128,1280]{1,0:T(8,128)(2,1)S(1)} custom-call(s32[3]{0:T(128)S(1)} %pad_add_fusion.place, s32[128,1280]{1,0:T(8,128)S(1)} %copy-done.2, bf16[2,80,16,128]{3,2,1,0:T(8,128)(2,1)S(1)} %get-tuple-element.27.table), custom_call_target="tpu_custom_call" | custom-call | flops 8999999488 | tf_op jit(solution)/shard_map/pallas_call | solution.py:256
  31.9 1.6 %collective-permute-start.6 = (bf16[128,1280]{1,0:T(8,128)(2,1)S(1)}, bf16[128,1280]{1,0:T(8,128)(2,1)S(1)}, u32[]{:S(2)}, u32[]{:S(2)}) collective-permute-start(bf16[128,1280]{1,0:T(8,128)(2,1)S(1)} %shard_map.72.own), channel_id=1, source_target_pairs={{0,8},{8,16},{16,24},{24,32},{32,40},{40,48},{48,56},{56,64},{64,7... | collective-permute-start | bytes 983048 | tf_op jit(solution)/shard_map/ppermute | solution.py:295
  33.4 3.9 %collective-permute-start.7 = (bf16[128,1280]{1,0:T(8,128)(2,1)S(1)}, bf16[128,1280]{1,0:T(8,128)(2,1)S(1)}, u32[]{:S(2)}, u32[]{:S(2)}) collective-permute-start(bf16[128,1280]{1,0:T(8,128)(2,1)S(1)} %shard_map.72.own), channel_id=1, source_target_pairs={{8,0},{16,8},{24,16},{32,24},{40,32},{48,40},{56,48},{64,56},{72,6... | collective-permute-start | bytes 983048 | tf_op jit(solution)/shard_map/ppermute | solution.py:296
  37.3 0.0 copy-done
  37.3 0.7 shard_map.69.refs_0_
  38.0 0.0 collective-permute-start
  38.0 5.4 %collective-permute-start.1 = (bf16[144,1280]{1,0:T(8,128)(2,1)S(1)}, bf16[144,1280]{1,0:T(8,128)(2,1)S(1)}, u32[]{:S(2)}, u32[]{:S(2)}) collective-permute-start(bf16[144,1280]{1,0:T(8,128)(2,1)S(1)} %get-tuple-element.19.own), channel_id=1, source_target_pairs={{8,0},{16,8},{24,16},{32,24},{40,32},{48,40},{56,48},{64,56},{72,6... | collective-permute-start | bytes 1105928 | tf_op jit(solution)/shard_map/ppermute | solution.py:296
  43.3 2.5 %collective-permute-done.6.left = bf16[128,1280]{1,0:T(8,128)(2,1)S(1)} collective-permute-done((bf16[128,1280]{1,0:T(8,128)(2,1)S(1)}, bf16[128,1280]{1,0:T(8,128)(2,1)S(1)}, u32[]{:S(2)}, u32[]{:S(2)}) %collective-permute-start.6) | collective-permute-done | bytes 327712 | tf_op jit(solution)/shard_map/ppermute | solution.py:295
  45.8 0.0 collective-permute-done.7.right
  45.8 2.0 %shard_map.73 = (f32[192,768]{1,0:T(8,128)S(1)}, f32[192,768]{1,0:T(8,128)S(1)}) custom-call(bf16[128,1280]{1,0:T(8,128)(2,1)S(1)} %collective-permute-done.6.left, bf16[128,1280]{1,0:T(8,128)(2,1)S(1)} %shard_map.72.own, bf16[128,1280]{1,0:T(8,128)(2,1)S(1)} %collective-permute-done.7.right, bf16[768,1280]{1,0:T(8,128)(2,1)S(1)} %copy-done), custom_call_target="tpu_custom_call" | custom-call | flops 4000000000 | tf_op jit(solution)/shard_map/pallas_call | solution.py:256
  47.8 0.1 collective-permute-start.8
  47.9 4.7 %collective-permute-done.left = bf16[144,1280]{1,0:T(8,128)(2,1)S(1)} collective-permute-done((bf16[144,1280]{1,0:T(8,128)(2,1)S(1)}, bf16[144,1280]{1,0:T(8,128)(2,1)S(1)}, u32[]{:S(2)}, u32[]{:S(2)}) %collective-permute-start) | collective-permute-done | bytes 368672 | tf_op jit(solution)/shard_map/ppermute | solution.py:295
  52.6 0.0 collective-permute-done.1.right
  52.6 3.5 %shard_map.70 = (f32[200,768]{1,0:T(8,128)S(1)}, f32[200,768]{1,0:T(8,128)S(1)}, f32[8,128]{1,0:T(8,128)S(1)}) custom-call(bf16[144,1280]{1,0:T(8,128)(2,1)S(1)} %collective-permute-done.left, bf16[144,1280]{1,0:T(8,128)(2,1)S(1)} %get-tuple-element.19.own, bf16[144,1280]{1,0:T(8,128)(2,1)S(1)} %collective-permute-done.1.right, ...), custom_call_target="tpu_custom_call" | custom-call | flops 4000000000 | tf_op jit(solution)/shard_map/pallas_call | solution.py:256
  56.1 0.0 collective-permute-start.2
  56.1 0.0 collective-permute-done.8.got
  56.1 0.1 shard_map.74
  56.2 1.0 %collective-permute-start.10 = (f32[48,768]{1,0:T(8,128)S(1)}, f32[48,768]{1,0:T(8,128)S(1)}, u32[]{:S(2)}, u32[]{:S(2)}) collective-permute-start(f32[48,768]{1,0:T(8,128)S(1)} %get-tuple-element.32), channel_id=1, source_target_pairs={{0,4},{2,6},{4,0},{6,2},{1,5},{3,7},{5,1},{7,3},{8,12},{10,14},{12... | collective-permute-start | bytes 442376 | tf_op jit(solution)/shard_map/ppermute | solution.py:312
  57.3 0.9 collective-permute-done.2.got
  58.2 0.1 shard_map.71
  58.2 0.6 collective-permute-start.3
  58.9 2.3 %collective-permute-start.4 = (f32[56,768]{1,0:T(8,128)S(1)}, f32[56,768]{1,0:T(8,128)S(1)}, u32[]{:S(2)}, u32[]{:S(2)}) collective-permute-start(f32[56,768]{1,0:T(8,128)S(1)} %get-tuple-element.25), channel_id=1, source_target_pairs={{0,4},{2,6},{4,0},{6,2},{1,5},{3,7},{5,1},{7,3},{8,12},{10,14},{12... | collective-permute-start | bytes 516104 | tf_op jit(solution)/shard_map/ppermute | solution.py:312
  61.1 1.5 %collective-permute-start.5 = (f32[56,768]{1,0:T(8,128)S(1)}, f32[56,768]{1,0:T(8,128)S(1)}, u32[]{:S(2)}, u32[]{:S(2)}) collective-permute-start(f32[56,768]{1,0:T(8,128)S(1)} %get-tuple-element.26), channel_id=1, source_target_pairs={{0,6},{2,0},{4,2},{6,4},{1,7},{3,1},{5,3},{7,5},{8,14},{10,8},{12,... | collective-permute-start | bytes 516104 | tf_op jit(solution)/shard_map/ppermute | solution.py:312
  62.6 0.3 collective-permute-start.11
  63.0 1.6 %collective-permute-done.10.refs_6_ = f32[48,768]{1,0:T(8,128)S(1)} collective-permute-done((f32[48,768]{1,0:T(8,128)S(1)}, f32[48,768]{1,0:T(8,128)S(1)}, u32[]{:S(2)}, u32[]{:S(2)}) %collective-permute-start.10) | collective-permute-done | bytes 147488 | tf_op jit(solution)/shard_map/ppermute | solution.py:312
  64.5 0.6 collective-permute-start.9
  65.1 8.3 %collective-permute-done.11.refs_7_ = f32[48,768]{1,0:T(8,128)S(1)} collective-permute-done((f32[48,768]{1,0:T(8,128)S(1)}, f32[48,768]{1,0:T(8,128)S(1)}, u32[]{:S(2)}, u32[]{:S(2)}) %collective-permute-start.11) | collective-permute-done | bytes 147488 | tf_op jit(solution)/shard_map/ppermute | solution.py:312
  73.4 1.2 %collective-permute-done.9.refs_5_ = f32[48,768]{1,0:T(8,128)S(1)} collective-permute-done((f32[48,768]{1,0:T(8,128)S(1)}, f32[48,768]{1,0:T(8,128)S(1)}, u32[]{:S(2)}, u32[]{:S(2)}) %collective-permute-start.9) | collective-permute-done | bytes 147488 | tf_op jit(solution)/shard_map/ppermute | solution.py:312
  74.6 0.0 collective-permute-done.3.refs_1_
  74.6 0.0 collective-permute-done.4.refs_2_
  74.6 0.0 collective-permute-done.5.refs_3_
  74.6 0.0 copy-start.4
  74.6 0.8 shard_map.75
  75.4 17.3 %all_to_all.10 = f32[128,1,128]{2,1,0:T(1,128)S(1)} all-to-all(f32[128,1,128]{2,1,0:T(1,128)S(1)} %bitcast.10), channel_id=1, replica_groups=mesh['gene'=16,'z'=4,'core'=2] {'gene','z','core'}, dimensions={0} | all-to-all | bytes 131072 | tf_op jit(solution)/shard_map/all_to_all | solution.py:317
  92.7 0.0 copy-done.4
  92.7 0.9 shard_map.76
  93.6 0.6 copy.9
  94.2 0.5 copy.8
Async XLA Ops:
  2.0 11.1 %all-to-all-start = ((f32[8,2,1280]{2,1,0:T(2,128)}), f32[8,2,1280]{2,1,0:T(2,128)S(1)}, u32[]{:S(2)}, u32[]{:S(2)}) async-start(f32[8,2,1280]{2,1,0:T(2,128)} %broadcast_in_dim.2), calls=%async_computation | async-start | bytes 163840 | tf_op jit(solution)/shard_map/all_to_all | solution.py:271
  13.1 1.1 %copy-start.1 = (s32[128,1280]{1,0:T(8,128)S(1)}, s32[128,1280]{1,0:T(8,128)}, u32[]{:S(2)}) copy-start(s32[128,1280]{1,0:T(8,128)} %perms.3) | copy-start | bytes 1966084
  14.2 0.7 copy-start.3
  14.9 8.7 %copy-start.2 = (s32[128,1280]{1,0:T(8,128)S(1)}, s32[128,1280]{1,0:T(8,128)}, u32[]{:S(2)}) copy-start(s32[128,1280]{1,0:T(8,128)} %perms.3) | copy-start | bytes 1966084
  23.6 13.7 %copy-start = (bf16[768,1280]{1,0:T(8,128)(2,1)S(1)}, bf16[768,1280]{1,0:T(8,128)(2,1)}, u32[]{:S(2)}) copy-start(bf16[768,1280]{1,0:T(8,128)(2,1)} %dosage.5) | copy-start | bytes 5898244
  31.9 14.0 %collective-permute-start.6 = (bf16[128,1280]{1,0:T(8,128)(2,1)S(1)}, bf16[128,1280]{1,0:T(8,128)(2,1)S(1)}, u32[]{:S(2)}, u32[]{:S(2)}) collective-permute-start(bf16[128,1280]{1,0:T(8,128)(2,1)S(1)} %shard_map.72.own), channel_id=1, source_target_pairs={{0,8},{8,16},{16,24},{24,32},{32,40},{40,48},{48,56},{56,64},{64,7... | collective-permute-start | bytes 983048 | tf_op jit(solution)/shard_map/ppermute | solution.py:295
  33.4 12.4 %collective-permute-start.7 = (bf16[128,1280]{1,0:T(8,128)(2,1)S(1)}, bf16[128,1280]{1,0:T(8,128)(2,1)S(1)}, u32[]{:S(2)}, u32[]{:S(2)}) collective-permute-start(bf16[128,1280]{1,0:T(8,128)(2,1)S(1)} %shard_map.72.own), channel_id=1, source_target_pairs={{8,0},{16,8},{24,16},{32,24},{40,32},{48,40},{56,48},{64,56},{72,6... | collective-permute-start | bytes 983048 | tf_op jit(solution)/shard_map/ppermute | solution.py:296
  38.0 14.7 %collective-permute-start = (bf16[144,1280]{1,0:T(8,128)(2,1)S(1)}, bf16[144,1280]{1,0:T(8,128)(2,1)S(1)}, u32[]{:S(2)}, u32[]{:S(2)}) collective-permute-start(bf16[144,1280]{1,0:T(8,128)(2,1)S(1)} %get-tuple-element.19.own), channel_id=1, source_target_pairs={{0,8},{8,16},{16,24},{24,32},{32,40},{40,48},{48,56},{56,64},{64,7... | collective-permute-start | bytes 1105928 | tf_op jit(solution)/shard_map/ppermute | solution.py:295
  38.0 14.7 %collective-permute-start.1 = (bf16[144,1280]{1,0:T(8,128)(2,1)S(1)}, bf16[144,1280]{1,0:T(8,128)(2,1)S(1)}, u32[]{:S(2)}, u32[]{:S(2)}) collective-permute-start(bf16[144,1280]{1,0:T(8,128)(2,1)S(1)} %get-tuple-element.19.own), channel_id=1, source_target_pairs={{8,0},{16,8},{24,16},{32,24},{40,32},{48,40},{56,48},{64,56},{72,6... | collective-permute-start | bytes 1105928 | tf_op jit(solution)/shard_map/ppermute | solution.py:296
  47.8 8.3 %collective-permute-start.8 = (f32[192,768]{1,0:T(8,128)S(1)}, f32[192,768]{1,0:T(8,128)S(1)}, u32[]{:S(2)}, u32[]{:S(2)}) collective-permute-start(f32[192,768]{1,0:T(8,128)S(1)} %get-tuple-element.29), channel_id=1, source_target_pairs={{0,1},{1,0},{2,3},{3,2},{4,5},{5,4},{6,7},{7,6},{8,9},{9,8},{10,11... | collective-permute-start | bytes 1769480 | tf_op jit(solution)/shard_map/ppermute | solution.py:307
  56.1 2.1 %collective-permute-start.2 = (f32[200,768]{1,0:T(8,128)S(1)}, f32[200,768]{1,0:T(8,128)S(1)}, u32[]{:S(2)}, u32[]{:S(2)}) collective-permute-start(f32[200,768]{1,0:T(8,128)S(1)} %get-tuple-element.22), channel_id=1, source_target_pairs={{0,1},{1,0},{2,3},{3,2},{4,5},{5,4},{6,7},{7,6},{8,9},{9,8},{10,11... | collective-permute-start | bytes 1843208 | tf_op jit(solution)/shard_map/ppermute | solution.py:307
  56.2 8.3 %collective-permute-start.10 = (f32[48,768]{1,0:T(8,128)S(1)}, f32[48,768]{1,0:T(8,128)S(1)}, u32[]{:S(2)}, u32[]{:S(2)}) collective-permute-start(f32[48,768]{1,0:T(8,128)S(1)} %get-tuple-element.32), channel_id=1, source_target_pairs={{0,4},{2,6},{4,0},{6,2},{1,5},{3,7},{5,1},{7,3},{8,12},{10,14},{12... | collective-permute-start | bytes 442376 | tf_op jit(solution)/shard_map/ppermute | solution.py:312
  58.2 16.3 %collective-permute-start.3 = (f32[56,768]{1,0:T(8,128)S(1)}, f32[56,768]{1,0:T(8,128)S(1)}, u32[]{:S(2)}, u32[]{:S(2)}) collective-permute-start(f32[56,768]{1,0:T(8,128)S(1)} %get-tuple-element.24), channel_id=1, source_target_pairs={{0,2},{2,4},{4,6},{6,0},{1,3},{3,5},{5,7},{7,1},{8,10},{10,12},{12... | collective-permute-start | bytes 516104 | tf_op jit(solution)/shard_map/ppermute | solution.py:312
  58.9 15.7 %collective-permute-start.4 = (f32[56,768]{1,0:T(8,128)S(1)}, f32[56,768]{1,0:T(8,128)S(1)}, u32[]{:S(2)}, u32[]{:S(2)}) collective-permute-start(f32[56,768]{1,0:T(8,128)S(1)} %get-tuple-element.25), channel_id=1, source_target_pairs={{0,4},{2,6},{4,0},{6,2},{1,5},{3,7},{5,1},{7,3},{8,12},{10,14},{12... | collective-permute-start | bytes 516104 | tf_op jit(solution)/shard_map/ppermute | solution.py:312
  61.1 13.5 %collective-permute-start.5 = (f32[56,768]{1,0:T(8,128)S(1)}, f32[56,768]{1,0:T(8,128)S(1)}, u32[]{:S(2)}, u32[]{:S(2)}) collective-permute-start(f32[56,768]{1,0:T(8,128)S(1)} %get-tuple-element.26), channel_id=1, source_target_pairs={{0,6},{2,0},{4,2},{6,4},{1,7},{3,1},{5,3},{7,5},{8,14},{10,8},{12,... | collective-permute-start | bytes 516104 | tf_op jit(solution)/shard_map/ppermute | solution.py:312
  62.6 10.8 %collective-permute-start.11 = (f32[48,768]{1,0:T(8,128)S(1)}, f32[48,768]{1,0:T(8,128)S(1)}, u32[]{:S(2)}, u32[]{:S(2)}) collective-permute-start(f32[48,768]{1,0:T(8,128)S(1)} %get-tuple-element.33), channel_id=1, source_target_pairs={{0,6},{2,0},{4,2},{6,4},{1,7},{3,1},{5,3},{7,5},{8,14},{10,8},{12,... | collective-permute-start | bytes 442376 | tf_op jit(solution)/shard_map/ppermute | solution.py:312
  64.5 10.1 %collective-permute-start.9 = (f32[48,768]{1,0:T(8,128)S(1)}, f32[48,768]{1,0:T(8,128)S(1)}, u32[]{:S(2)}, u32[]{:S(2)}) collective-permute-start(f32[48,768]{1,0:T(8,128)S(1)} %get-tuple-element.31), channel_id=1, source_target_pairs={{0,2},{2,4},{4,6},{6,0},{1,3},{3,5},{5,7},{7,1},{8,10},{10,12},{12... | collective-permute-start | bytes 442376 | tf_op jit(solution)/shard_map/ppermute | solution.py:312
  74.6 18.1 %copy-start.4 = (s32[32]{0:T(128)S(1)}, s32[32]{0:T(128)}, u32[]{:S(2)}) copy-start(s32[32]{0:T(128)} %order.1) | copy-start | bytes 388

commit v3 on v2

--- a/solution.py
+++ b/solution.py
@@ -68,18 +68,63 @@
     lax.fori_loop(0, 4 * (tiles // group), step, 0)
 
 
-def first_kernel(place, windows, every, perms, out, table):
+def lane_sums(rows):
+    return lax.dot_general(
+        jnp.ones((8, LANES), jnp.float32),
+        rows,
+        (((1,), (1,)), ((), ())),
+        precision=lax.Precision.HIGHEST,
+        preferred_element_type=jnp.float32,
+    )[:1]
+
+
+def pack_kernel(dosage, expression, out, kept, levels, done):
+    shards, _, _ = out.shape
+    variants, width = dosage.shape
+    pieces = variants // LANES
+    copies = []
+    for i in range(pieces):
+        rows = pl.ds(i * LANES, LANES)
+        copies.append(pltpu.make_async_copy(dosage.at[rows], kept.at[rows], done.at[i]))
+        copies[-1].start()
+    fetch = pltpu.make_async_copy(expression, levels, done.at[pieces])
+    fetch.start()
+    for i in range(pieces):
+        copies[i].wait()
+        total = jnp.zeros((LANES, LANES), jnp.float32)
+        square = jnp.zeros((LANES, LANES), jnp.float32)
+        for k in range(width // LANES):
+            v = kept[i * LANES : (i + 1) * LANES, k * LANES : (k + 1) * LANES].astype(jnp.float32)
+            total = total + v
+            square = square + v * v
+        for j, moment in enumerate((lane_sums(total), lane_sums(square))):
+            for d in range(shards):
+                out[d, j : j + 1, width + i * LANES : width + (i + 1) * LANES] = moment
+    fetch.wait()
+    for d in range(shards):
+        out[d, :, :width] = levels[...]
+
+
+def first_kernel(variants, place, windows, every, perms, out, table, stat):
     z, c = place[1], place[2]
-    shards, genes, width = every.shape
+    shards, genes, wide = every.shape
+    width = wide - variants
     samples = shards * width
-    own = every[z * 2 + c]
-    direct = []
+    moments = jnp.sum(every[:, :, width:], axis=0)
+    row_mean = moments[0:1] / samples
+    spread = moments[1:2] / samples - row_mean * row_mean + epsilon
+    stat[...] = jnp.zeros_like(stat)
+    stat[0:1, :] = row_mean
+    stat[1:2, :] = lax.rsqrt(spread * samples)
+    own = every[z * 2 + c][:, :width]
+    direct, sums = [], []
     for j in range(genes):
-        x = every[:, j, :]
+        x = every[:, j, :width]
         mean = jnp.sum(x, keepdims=True) / samples
         center = x - mean
         scale = lax.rsqrt(jnp.sum(center * center, keepdims=True) / samples + epsilon)
-        scaled = center * scale
+        scaled = (center * scale).astype(jnp.bfloat16).astype(jnp.float32)
+        sums.append(jnp.sum(scaled, keepdims=True))
         for k in range(shards):
             for i in range(width // LANES):
                 piece = scaled[k : k + 1, i * LANES : (i + 1) * LANES]
@@ -96,7 +141,11 @@
             digits = ((w >> 7).astype(jnp.float32), (w & 127).astype(jnp.float32))
             for d in range(2):
                 extra = jnp.where((row == 2 + d) & (lane == j * 2 + b), digits[d], extra)
-    extra = jnp.where(row == 4, 1.0, extra)
+        rest = sums[j]
+        for d in range(3):
+            digit = rest.astype(jnp.bfloat16).astype(jnp.float32)
+            rest = rest - digit
+            extra = jnp.where((row == 4 + d) & (lane == j), digit, extra)
     out[8 * TILE : 9 * TILE, :] = extra.astype(jnp.bfloat16)
     gather_chunk(0, place, perms, table, out)
 
@@ -111,88 +160,112 @@
     )
 
 
-def squares_kernel(dosage, out):
-    variants, width = dosage.shape
-    total = jnp.zeros((variants, LANES), jnp.float32)
-    for i in range(width // LANES):
-        d = dosage[:, i * LANES : (i + 1) * LANES].astype(jnp.float32)
-        total = total + d * d
-    out[...] = lax.dot_general(
-        jnp.ones((8, LANES), jnp.float32),
-        total,
-        (((1,), (1,)), ((), ())),
-        precision=lax.Precision.HIGHEST,
-        preferred_element_type=jnp.float32,
-    )
-
-
-def product_kernel(with_stats, left, own, right, dosage, *refs):
-    if with_stats:
-        squares, keep, send, win_ref = refs
-    else:
-        keep, send = refs
-    weights = dosage[...]
-    small = []
-    for o, ref in enumerate((left, own, right)):
-        got = times(ref[: 8 * TILE, :], weights)
-        for kc, dst in ((0, keep), (1, send)):
-            for kz in range(4):
-                for j in range(2):
-                    src = kc * 64 + (kz // 2) * 32 + j * TILE + (kz % 2) * HALF
-                    to = kz * 48 + (o * 2 + j) * HALF
-                    dst[to : to + HALF, :] = got[src : src + HALF]
-        if with_stats:
-            small.append(times(ref[8 * TILE :, :], weights))
-    if with_stats:
-        stats = jnp.concatenate(
-            [small[0][:2], small[1][:2], small[2][:2], small[1][4:5], squares[:1]], axis=0
+def product_kernel(kc, with_direct, left, own, right, dosage, stat, *outs):
+    blocks = [ref[kc * 4 * TILE : (kc + 1) * 4 * TILE, :] for ref in (left, own, right)]
+    if with_direct:
+        blocks += [ref[8 * TILE :, :] for ref in (left, own, right)]
+    rows = jnp.concatenate(blocks, axis=0)
+    mean, scale = stat[0:1, :], stat[1:2, :]
+    got = (times(rows, dosage[...]) - jnp.sum(rows.astype(jnp.float32), axis=1, keepdims=True) * mean) * scale
+    out = outs[0]
+    for o in range(3):
+        for kz in range(4):
+            for j in range(2):
+                src = o * 4 * TILE + (kz // 2) * 2 * TILE + j * TILE + (kz % 2) * HALF
+                to = kz * 48 + (o * 2 + j) * HALF
+                out[to : to + HALF, :] = got[src : src + HALF]
+    if with_direct:
+        first = 12 * TILE
+        zero = jnp.zeros((2, got.shape[1]), jnp.float32)
+        out[192:200, :] = jnp.concatenate(
+            [got[first + o * TILE : first + o * TILE + 2] for o in range(3)] + [zero], axis=0
         )
-        keep[192:200, :] = stats
-        send[192:200, :] = stats
-        win_ref[...] = jnp.zeros_like(win_ref)
+        info = outs[1]
+        info[...] = jnp.zeros_like(info)
+        lane = lax.broadcasted_iota(jnp.int32, (1, LANES), 1)
         for o, ref in enumerate((left, own, right)):
             e = ref[8 * TILE :, :LANES].astype(jnp.float32)
-            win_ref[o : o + 1, :] = e[2:3] * 128.0 + e[3:4]
-
-
-def split_kernel(keep, got, *outs):
-    for kz, out in enumerate(outs):
-        out[:48, :] = keep[kz * 48 : kz * 48 + 48, :] + got[kz * 48 : kz * 48 + 48, :]
-        if out.shape[0] > 48:
-            out[48:, :] = keep[192:200, :] + got[192:200, :]
-
-
-def maxima_kernel(samples, place, win, *refs):
-    refs, out = refs[:-1], refs[-1]
-    chunks = []
-    for h in range(CHUNKS):
-        part = refs[4 * h : 4 * h + 4]
-        chunks.append((part[0][...] + part[1][...]) + (part[2][...] + part[3][...]))
-    stats = chunks[0][48:56]
-    mean = stats[6:7] / samples
-    spread = stats[7:8] / samples - mean * mean + epsilon
-    scale = lax.rsqrt(spread * samples)
-    variants = scale.shape[1]
+            line = jnp.where(lane < 4, e[2:3] * 128.0 + e[3:4], 0.0)
+            total = (e[4:5] + e[5:6]) + e[6:7]
+            for j in range(2):
+                line = jnp.where(lane == 4 + j, total[:, j : j + 1], line)
+            info[o : o + 1, :] = line
+
+
+LEVELS = 32767.0
+PARTS = 256.0
+
+
+def bound_code(largest):
+    return jnp.clip(jnp.ceil(largest * PARTS), 1.0, LEVELS)
+
+
+def coded(values, code):
+    scaled = values * (LEVELS * PARTS / code)
+    return jnp.clip(jnp.round(scaled), -LEVELS, LEVELS)
+
+
+def to_int16(values):
+    return values.astype(jnp.int32).astype(jnp.int16)
+
+
+def split_kernel(keep0, send0, got0, keep1, got1, own, *refs):
+    messages, hold = refs[:3], refs[3]
+    largest = jnp.zeros((HALF, own.shape[1]), jnp.float32)
+    for kz in range(4):
+        for h, (keep, got) in enumerate(((keep0, got0), (keep1, got1))):
+            for t in range(6):
+                at = kz * 48 + t * HALF
+                v = keep[at : at + HALF, :] + got[at : at + HALF, :]
+                to = h * 48 + t * HALF
+                if kz == 0:
+                    own[to : to + HALF, :] = v
+                else:
+                    hold[kz - 1, to : to + HALF, :] = v
+                    largest = jnp.maximum(largest, jnp.abs(v))
+    direct = send0[192:200, :] + got0[192:200, :]
+    own[96:104, :] = direct
+    codes = [bound_code(jnp.max(v, keepdims=True)) for v in (largest, jnp.abs(direct))]
+    row = lax.broadcasted_iota(jnp.int32, direct.shape, 0)
+    tail = jnp.where(row == 0, codes[0], jnp.where(row == 1, codes[1], 0.0))
+    tail = to_int16(jnp.concatenate([coded(direct, codes[1]), tail], axis=0))
+    for k, message in enumerate(messages):
+        for t in range(6):
+            rows = slice(t * TILE, (t + 1) * TILE)
+            message[rows, :] = to_int16(coded(hold[k, rows, :], codes[0]))
+        message[96:112, :] = tail
+
+
+def maxima_kernel(place, info, stat, own, *refs):
+    messages, out = refs[:3], refs[3]
+    values, direct = own[:96, :], own[96:104, :]
+    for message in messages:
+        tail = message[96:112, :].astype(jnp.int32).astype(jnp.float32)
+        unit = 1.0 / (LEVELS * PARTS)
+        values = values + message[:96, :].astype(jnp.int32).astype(jnp.float32) * (tail[8:9] * unit)
+        direct = direct + tail[:8] * (tail[9:10] * unit)
+    offset = stat[0:1, :] * stat[1:2, :]
+    variants = offset.shape[1]
     index = lax.broadcasted_iota(jnp.int32, (1, variants), 1) + place[0] * variants
     index = index.astype(jnp.float32)
     lane = lax.broadcasted_iota(jnp.int32, (HALF, LANES), 1)
+    row = lax.broadcasted_iota(jnp.int32, (HALF, LANES), 0)
     tile = jnp.zeros((HALF, LANES), jnp.float32)
-    direct = jnp.abs(stats) * scale
-    row = lax.broadcasted_iota(jnp.int32, (HALF, LANES), 0)
     seen = []
     for o in range(3):
         for j in range(2):
             n = o * 2 + j
-            lo = win[o : o + 1, j * 2 : j * 2 + 1]
-            hi = win[o : o + 1, j * 2 + 1 : j * 2 + 2]
+            lo = info[o : o + 1, j * 2 : j * 2 + 1]
+            hi = info[o : o + 1, j * 2 + 1 : j * 2 + 2]
+            back = offset * info[o : o + 1, 4 + j : 5 + j]
             inside = (index >= lo) & (index < hi)
             for h in range(CHUNKS):
-                v = jnp.abs(chunks[h][n * HALF : n * HALF + HALF]) * scale
+                at = h * 48 + n * HALF
+                v = jnp.abs(values[at : at + HALF] + back)
                 best = jnp.max(jnp.where(inside, v, 0.0), axis=1, keepdims=True)
                 tile = jnp.where(lane // HALF == n * CHUNKS + h, best, tile)
-            seen.append(
-                jnp.max(jnp.where(inside, direct[n : n + 1], 0.0), axis=1, keepdims=True)
-            )
+            v = jnp.abs(direct[n : n + 1] + back)
+            seen.append(jnp.max(jnp.where(inside, v, 0.0), axis=1, keepdims=True))
     line = jnp.sum(jnp.where(lane % HALF == row, tile, 0.0), axis=0, keepdims=True)
     for n in range(6):
         line = jnp.where(lane[:1] == 96 + n, seen[n], line)
@@ -237,21 +310,26 @@
     observed[...] = seen[:, 98:100]
 
 
-def call(kernel, outs, args, us, scratch=()):
+def call(kernel, outs, args, us, scratch=(), remote=()):
     scalar = [a.size <= 64 for a in args]
     many = isinstance(outs, list)
     made = pl.pallas_call(
         kernel,
         out_shape=tuple(outs) if many else outs,
-        in_specs=[SM if k else VM for k in scalar],
+        in_specs=[
+            pl.BlockSpec(memory_space=pltpu.HBM) if i in remote else SM if k else VM
+            for i, k in enumerate(scalar)
+        ],
         out_specs=tuple([VM] * len(outs)) if many else VM,
         scratch_shapes=scratch,
         compiler_params=pltpu.CompilerParams(vmem_limit_bytes=24 << 20),
         cost_estimate=pl.CostEstimate(flops=int(us * 1e9), bytes_accessed=0, transcendentals=0),
     )
     args = [
-        a if k else pltpu.with_memory_space_constraint(a, pltpu.VMEM)
-        for a, k in zip(args, scalar)
+        a
+        if k
+        else pltpu.with_memory_space_constraint(a, pltpu.HBM if i in remote else pltpu.VMEM)
+        for i, (a, k) in enumerate(zip(args, scalar))
     ]
     return made(*args)
 
@@ -267,14 +345,20 @@
     samples = width * shards
     g, z, c = lax.axis_index("gene"), lax.axis_index("z"), lax.axis_index("core")
     place = jnp.stack([g, z, c]).astype(jnp.int32)
-    copies = jnp.broadcast_to(expression.T[None], (shards, 2, width))
-    every = lax.all_to_all(copies, ("z", "core"), 0, 0, tiled=True)
-
-    squares = call(squares_kernel, shape((8, variants)), [dosage], 1)
+    packed, kept = call(
+        pack_kernel,
+        [shape((shards, 2, width + variants)), shape((variants, width), jnp.bfloat16)],
+        [dosage, expression.T],
+        2,
+        [pltpu.VMEM((2, width), jnp.float32), pltpu.SemaphoreType.DMA((variants // LANES + 1,))],
+        remote=(0, 1),
+    )
+    every = lax.all_to_all(packed, ("z", "core"), 0, 0, tiled=True)
+
     table_shape = shape((2, samples // LANES, TILE, LANES), jnp.bfloat16)
-    first, table = call(
-        first_kernel,
-        [shape((9 * TILE, width), jnp.bfloat16), table_shape],
+    first, table, stat = call(
+        functools.partial(first_kernel, variants),
+        [shape((9 * TILE, width), jnp.bfloat16), table_shape, shape((8, variants))],
         [place, windows, every, perms],
         9,
     )
@@ -290,36 +374,39 @@
         )
     ahead = [(i, (i + 1) % owners) for i in range(owners)]
     back = [(b, a) for a, b in ahead]
-    sums = []
+    halves = []
     for h, own in enumerate(shuffled):
         left = lax.ppermute(own, "gene", ahead)
         right = lax.ppermute(own, "gene", back)
-        rows = 200 if h == 0 else 192
-        outs = [shape((rows, variants)), shape((rows, variants))]
-        args = [left, own, right, dosage]
+        args = [left, own, right, kept, stat]
         if h == 0:
-            outs.append(shape((8, LANES)))
-            args.append(squares)
-        made = call(functools.partial(product_kernel, h == 0), outs, args, 4)
-        if h == 0:
-            win = made[2]
-        keep, send = made[:2]
+            outs = [shape((200, variants)), shape((8, LANES))]
+            send, info = call(functools.partial(product_kernel, 1, True), outs, args, 1)
+        else:
+            send = call(
+                functools.partial(product_kernel, 1, False), shape((192, variants)), args, 1
+            )
         got = lax.ppermute(send, "core", [(0, 1), (1, 0)])
-        depth = 56 if h == 0 else 48
-        parts = call(split_kernel, [shape((depth, variants))] * 4, [keep, got], 1)
-        sums.append(parts[0])
-        for k in range(1, 4):
-            sums.append(lax.ppermute(parts[k], "z", [(i, (i + k) % 4) for i in range(4)]))
+        keep = call(functools.partial(product_kernel, 0, False), shape((192, variants)), args, 1)
+        halves += [keep, send, got] if h == 0 else [keep, got]
+    own, *parts = call(
+        split_kernel,
+        [shape((104, variants))] + [shape((112, variants), jnp.int16)] * 3,
+        halves,
+        1,
+        [pltpu.VMEM((3, 96, variants), jnp.float32)],
+    )
+    sums = []
+    for k in range(1, 4):
+        sums.append(lax.ppermute(parts[k - 1], "z", [(i, (i + k) % 4) for i in range(4)]))
     everyone = owners * shards
-    lines = call(
-        functools.partial(maxima_kernel, samples), shape((everyone, LANES)), [place, win, *sums], 2
-    )
+    lines = call(maxima_kernel, shape((everyone, LANES)), [place, info, stat, own, *sums], 2)
     lines = lax.all_to_all(
         lines.reshape(everyone, 1, LANES), ("gene", "z", "core"), 0, 0, tiled=True
     ).reshape(everyone, LANES)
     successive, observed = call(
         final_kernel,
-        [shape((2, LANES)), shape((1, 2))],
+        [jax.ShapeDtypeStruct((2, LANES), jnp.float32), jax.ShapeDtypeStruct((1, 2), jnp.float32)],
         [place, order, lines],
         2,
         [pltpu.VMEM((2 * owners, HALF, LANES), jnp.float32)],

time: 95.2 us -> 87.7 us (0.921)
  local copies, waits for them, and re-layouts: 4.2 us -> 0.01 us
  blocking collectives: 17.3 us -> 13.8 us
  starting transfers between devices: 22.6 us -> 20.1 us
  Pallas kernels: 25 us -> 27 us
    ppermute x2, waiting for transfers between devices: 0.01 us -> 5.38 us  [on_device(): right = lax.ppermute(own, 'gene', back)]
    all_to_all x1, blocking collectives: 17.3 us -> 13.8 us  [on_device(): lax.all_to_all(lines.reshape(everyone, 1, LANES), ('gene', 'z', 'core'),...]
    unnamed x12 -> x6, local copies, waits for them, and re-layouts: 2.86 us -> 0.01 us
    ppermute x6 -> x3, waiting for transfers between devices: 11 us -> 8.25 us  [on_device(): lax.ppermute(parts[k - 1], 'z', [(i, (i + k) % 4) for i in range(4)])]
    ppermute x6 -> x3, starting transfers between devices: 6.34 us -> 3.78 us  [on_device(): lax.ppermute(parts[k - 1], 'z', [(i, (i + k) % 4) for i in range(4)])]
    pallas_call x9 -> x10, Pallas kernels: 25 us -> 27 us  [call(): return made(*args)]
    ppermute x2, waiting for transfers between devices: 7.21 us -> 5.52 us  [on_device(): left = lax.ppermute(own, 'gene', ahead)]
    ppermute x2, starting transfers between devices: 1.56 us -> 0.01 us  [on_device(): left = lax.ppermute(own, 'gene', ahead)]
  transfers between devices with their start and end apart: 13 -> 10, of which waited for: 7 -> 6; matrix products, arithmetic and copies ran while one was open for 0% -> 0% of each run, Pallas kernels for 7% -> 13%
where the time goes in v3:
time: 87.7 us; the launch traced here: 87.2 us
  Pallas kernels  27 us (31%)
  waiting for transfers between devices  25.5 us (29%)
  starting transfers between devices  20.1 us (23%)
  blocking collectives  13.8 us (16%)
    pallas_call x10, Pallas kernels, call(): return made(*args)  27 us
    all_to_all x1, blocking collectives, on_device(): lax.all_to_all(lines.reshape(everyone, 1, LANES), ('gene', 'z', 'core'),...  13.8 us
    ppermute x2, starting transfers between devices, on_device(): right = lax.ppermute(own, 'gene', back)  10.7 us
    ppermute x3, waiting for transfers between devices, on_device(): lax.ppermute(parts[k - 1], 'z', [(i, (i + k) % 4) for i in range(4)])  8.25 us
    all_to_all x1, waiting for transfers between devices, on_device(): every = lax.all_to_all(packed, ('z', 'core'), 0, 0, tiled=True)  6.03 us
    ppermute x2, waiting for transfers between devices, on_device(): left = lax.ppermute(own, 'gene', ahead)  5.52 us
    all_to_all x1, starting transfers between devices, on_device(): every = lax.all_to_all(packed, ('z', 'core'), 0, 0, tiled=True)  5.44 us
    ppermute x2, waiting for transfers between devices, on_device(): right = lax.ppermute(own, 'gene', back)  5.38 us
  transfers between devices with their start and end apart: 10, of which 6 were waited for; matrix products, arithmetic and copies ran while one was open for 0% of the time, Pallas kernels for 13%

profile of v3, /device:TPU:0, one launch (start us, length us, event | category | flops | bytes accessed | tf_op | source)
XLA Modules:
  0.0 87.2 jit_solution(17288891362267196135)
XLA Ops:
  0.6 0.0 copy-start
  0.6 0.0 copy-start.1
  0.7 4.1 %shard_map.68 = (f32[8,2,2048]{2,1,0:T(2,128)}, bf16[768,1280]{1,0:T(8,128)(2,1)S(1)}) custom-call(bf16[768,1280]{1,0:T(8,128)(2,1)} %dosage.1, f32[2,1280]{1,0:T(2,128)} %bitcast.11), custom_call_target="tpu_custom_call" | custom-call | flops 2000000000 | tf_op jit(solution)/shard_map/pallas_call | solution.py:334
  4.7 5.4 %all-to-all-start = ((f32[8,2,2048]{2,1,0:T(2,128)}), f32[8,2,2048]{2,1,0:T(2,128)S(1)}, u32[]{:S(2)}, u32[]{:S(2)}) async-start(f32[8,2,2048]{2,1,0:T(2,128)} %get-tuple-element.15), calls=%async_computation | async-start | bytes 262144 | tf_op jit(solution)/shard_map/all_to_all | solution.py:356
  10.2 0.1 pad_add_fusion.place
  10.3 6.0 %all-to-all-done.every = f32[8,2,2048]{2,1,0:T(2,128)S(1)} async-done(((f32[8,2,2048]{2,1,0:T(2,128)}), f32[8,2,2048]{2,1,0:T(2,128)S(1)}, u32[]{:S(2)}, u32[]{:S(2)}) %all-to-all-start) | async-done | bytes 131104 | tf_op jit(solution)/shard_map/all_to_all | solution.py:356
  16.3 0.0 copy-done
  16.3 0.0 copy-done.1
  16.3 8.9 %shard_map.69 = (bf16[144,1280]{1,0:T(8,128)(2,1)S(1)}, bf16[2,80,16,128]{3,2,1,0:T(8,128)(2,1)S(1)}, f32[8,768]{1,0:T(8,128)S(1)}) custom-call(s32[3]{0:T(128)S(1)} %pad_add_fusion.place, s32[2,2]{1,0:T(2,128)S(1)} %copy-done.1, f32[8,2,2048]{2,1,0:T(2,128)S(1)} %all-to-all-done.every, s32[128,1280]{1,0:T(8,128)S(1)} %copy-done), custom_call_target="tpu_custom_call" | custom-call | flops 8999999488 | tf_op jit(solution)/shard_map/pallas_call | solution.py:334
  25.2 5.3 %collective-permute-start.1 = (bf16[144,1280]{1,0:T(8,128)(2,1)S(1)}, bf16[144,1280]{1,0:T(8,128)(2,1)S(1)}, u32[]{:S(2)}, u32[]{:S(2)}) collective-permute-start(bf16[144,1280]{1,0:T(8,128)(2,1)S(1)} %get-tuple-element.16.own), channel_id=1, source_target_pairs={{8,0},{16,8},{24,16},{32,24},{40,32},{48,40},{56,48},{64,56},{72,6... | collective-permute-start | bytes 1105928 | tf_op jit(solution)/shard_map/ppermute | solution.py:380
  30.5 0.0 collective-permute-start
  30.5 8.1 %shard_map.72.own = bf16[128,1280]{1,0:T(8,128)(2,1)S(1)} custom-call(s32[3]{0:T(128)S(1)} %pad_add_fusion.place, s32[128,1280]{1,0:T(8,128)S(1)} %copy-done, bf16[2,80,16,128]{3,2,1,0:T(8,128)(2,1)S(1)} %get-tuple-element.21.table), custom_call_target="tpu_custom_call" | custom-call | flops 8999999488 | tf_op jit(solution)/shard_map/pallas_call | solution.py:334
  38.6 5.4 %collective-permute-start.4 = (bf16[128,1280]{1,0:T(8,128)(2,1)S(1)}, bf16[128,1280]{1,0:T(8,128)(2,1)S(1)}, u32[]{:S(2)}, u32[]{:S(2)}) collective-permute-start(bf16[128,1280]{1,0:T(8,128)(2,1)S(1)} %shard_map.72.own), channel_id=1, source_target_pairs={{8,0},{16,8},{24,16},{32,24},{40,32},{48,40},{56,48},{64,56},{72,6... | collective-permute-start | bytes 983048 | tf_op jit(solution)/shard_map/ppermute | solution.py:380
  44.0 0.0 collective-permute-start.3
  44.0 0.0 collective-permute-done.1.right
  44.0 0.0 collective-permute-done.left
  44.0 0.7 shard_map.70
  44.8 0.1 collective-permute-start.2
  44.8 5.4 %collective-permute-done.4.right = bf16[128,1280]{1,0:T(8,128)(2,1)S(1)} collective-permute-done((bf16[128,1280]{1,0:T(8,128)(2,1)S(1)}, bf16[128,1280]{1,0:T(8,128)(2,1)S(1)}, u32[]{:S(2)}, u32[]{:S(2)}) %collective-permute-start.4) | collective-permute-done | bytes 327712 | tf_op jit(solution)/shard_map/ppermute | solution.py:380
  50.2 5.5 %collective-permute-done.3.left = bf16[128,1280]{1,0:T(8,128)(2,1)S(1)} collective-permute-done((bf16[128,1280]{1,0:T(8,128)(2,1)S(1)}, bf16[128,1280]{1,0:T(8,128)(2,1)S(1)}, u32[]{:S(2)}, u32[]{:S(2)}) %collective-permute-start.3) | collective-permute-done | bytes 327712 | tf_op jit(solution)/shard_map/ppermute | solution.py:379
  55.7 0.8 shard_map.74
  56.6 0.1 collective-permute-start.5
  56.6 0.8 shard_map.73.keep1
  57.5 0.8 shard_map.71.keep0
  58.3 0.4 collective-permute-done.5.got1
  58.6 0.0 collective-permute-done.2.got0
  58.6 0.4 shard_map.75
  59.0 0.6 collective-permute-start.6
  59.6 2.1 %collective-permute-start.7 = (s16[112,768]{1,0:T(8,128)(2,1)S(1)}, s16[112,768]{1,0:T(8,128)(2,1)S(1)}, u32[]{:S(2)}, u32[]{:S(2)}) collective-permute-start(s16[112,768]{1,0:T(8,128)(2,1)S(1)} %get-tuple-element.24), channel_id=1, source_target_pairs={{0,4},{2,6},{4,0},{6,2},{1,5},{3,7},{5,1},{7,3},{8,12},{10,14},{12... | collective-permute-start | bytes 516104 | tf_op jit(solution)/shard_map/ppermute | solution.py:401
  61.7 1.1 %collective-permute-start.8 = (s16[112,768]{1,0:T(8,128)(2,1)S(1)}, s16[112,768]{1,0:T(8,128)(2,1)S(1)}, u32[]{:S(2)}, u32[]{:S(2)}) collective-permute-start(s16[112,768]{1,0:T(8,128)(2,1)S(1)} %get-tuple-element.25), channel_id=1, source_target_pairs={{0,6},{2,0},{4,2},{6,4},{1,7},{3,1},{5,3},{7,5},{8,14},{10,8},{12,... | collective-permute-start | bytes 516104 | tf_op jit(solution)/shard_map/ppermute | solution.py:401
  62.8 7.6 %collective-permute-done.6.refs_0_ = s16[112,768]{1,0:T(8,128)(2,1)S(1)} collective-permute-done((s16[112,768]{1,0:T(8,128)(2,1)S(1)}, s16[112,768]{1,0:T(8,128)(2,1)S(1)}, u32[]{:S(2)}, u32[]{:S(2)}) %collective-permute-start.6) | collective-permute-done | bytes 172064 | tf_op jit(solution)/shard_map/ppermute | solution.py:401
  70.4 0.0 collective-permute-done.7.refs_1_
  70.4 0.6 collective-permute-done.8.refs_2_
  71.0 0.0 copy-start.2
  71.1 0.9 %shard_map.76 = f32[128,128]{1,0:T(8,128)S(1)} custom-call(s32[3]{0:T(128)S(1)} %pad_add_fusion.place, f32[8,128]{1,0:T(8,128)S(1)} %get-tuple-element.19.info, f32[8,768]{1,0:T(8,128)S(1)} %get-tuple-element.18.stat, f32[104,768]{1,0:T(8,128)S(1)} %get-tuple-element.22.own, s16[112,768]{1,0:T(8,128)(2,1)S(1)} %collective-permute-done.6.refs_0_, ...), custom_call_target="tpu_custom_call" | custom-call | flops 2000000000 | tf_op jit(solution)/shard_map/pallas_call | solution.py:334
  71.9 13.8 %all_to_all.10 = f32[128,1,128]{2,1,0:T(1,128)S(1)} all-to-all(f32[128,1,128]{2,1,0:T(1,128)S(1)} %bitcast.9), channel_id=1, replica_groups=mesh['gene'=16,'z'=4,'core'=2] {'gene','z','core'}, dimensions={0} | all-to-all | bytes 131072 | tf_op jit(solution)/shard_map/all_to_all | solution.py:404
  85.8 0.0 copy-done.2
  85.8 1.5 %shard_map.77 = (f32[2,128]{1,0:T(2,128)}, f32[1,2]{1,0:T(1,128)}) custom-call(s32[3]{0:T(128)S(1)} %pad_add_fusion.place, s32[32]{0:T(128)S(1)} %copy-done.2, f32[128,128]{1,0:T(8,128)S(1)} %bitcast.10), custom_call_target="tpu_custom_call" | custom-call | flops 2000000000 | tf_op jit(solution)/shard_map/pallas_call | solution.py:334
Async XLA Ops:
  0.6 15.7 %copy-start = (s32[128,1280]{1,0:T(8,128)S(1)}, s32[128,1280]{1,0:T(8,128)}, u32[]{:S(2)}) copy-start(s32[128,1280]{1,0:T(8,128)} %perms.3) | copy-start | bytes 1966084
  0.6 15.6 %copy-start.1 = (s32[2,2]{1,0:T(2,128)S(1)}, s32[2,2]{1,0:T(2,128)}, u32[]{:S(2)}) copy-start(s32[2,2]{1,0:T(2,128)} %windows.1) | copy-start | bytes 52
  4.7 11.5 %all-to-all-start = ((f32[8,2,2048]{2,1,0:T(2,128)}), f32[8,2,2048]{2,1,0:T(2,128)S(1)}, u32[]{:S(2)}, u32[]{:S(2)}) async-start(f32[8,2,2048]{2,1,0:T(2,128)} %get-tuple-element.15), calls=%async_computation | async-start | bytes 262144 | tf_op jit(solution)/shard_map/all_to_all | solution.py:356
  25.2 18.8 %collective-permute-start.1 = (bf16[144,1280]{1,0:T(8,128)(2,1)S(1)}, bf16[144,1280]{1,0:T(8,128)(2,1)S(1)}, u32[]{:S(2)}, u32[]{:S(2)}) collective-permute-start(bf16[144,1280]{1,0:T(8,128)(2,1)S(1)} %get-tuple-element.16.own), channel_id=1, source_target_pairs={{8,0},{16,8},{24,16},{32,24},{40,32},{48,40},{56,48},{64,56},{72,6... | collective-permute-start | bytes 1105928 | tf_op jit(solution)/shard_map/ppermute | solution.py:380
  30.5 13.5 %collective-permute-start = (bf16[144,1280]{1,0:T(8,128)(2,1)S(1)}, bf16[144,1280]{1,0:T(8,128)(2,1)S(1)}, u32[]{:S(2)}, u32[]{:S(2)}) collective-permute-start(bf16[144,1280]{1,0:T(8,128)(2,1)S(1)} %get-tuple-element.16.own), channel_id=1, source_target_pairs={{0,8},{8,16},{16,24},{24,32},{32,40},{40,48},{48,56},{56,64},{64,7... | collective-permute-start | bytes 1105928 | tf_op jit(solution)/shard_map/ppermute | solution.py:379
  38.6 11.6 %collective-permute-start.4 = (bf16[128,1280]{1,0:T(8,128)(2,1)S(1)}, bf16[128,1280]{1,0:T(8,128)(2,1)S(1)}, u32[]{:S(2)}, u32[]{:S(2)}) collective-permute-start(bf16[128,1280]{1,0:T(8,128)(2,1)S(1)} %shard_map.72.own), channel_id=1, source_target_pairs={{8,0},{16,8},{24,16},{32,24},{40,32},{48,40},{56,48},{64,56},{72,6... | collective-permute-start | bytes 983048 | tf_op jit(solution)/shard_map/ppermute | solution.py:380
  44.0 11.7 %collective-permute-start.3 = (bf16[128,1280]{1,0:T(8,128)(2,1)S(1)}, bf16[128,1280]{1,0:T(8,128)(2,1)S(1)}, u32[]{:S(2)}, u32[]{:S(2)}) collective-permute-start(bf16[128,1280]{1,0:T(8,128)(2,1)S(1)} %shard_map.72.own), channel_id=1, source_target_pairs={{0,8},{8,16},{16,24},{24,32},{32,40},{40,48},{48,56},{56,64},{64,7... | collective-permute-start | bytes 983048 | tf_op jit(solution)/shard_map/ppermute | solution.py:379
  44.8 13.9 %collective-permute-start.2 = (f32[200,768]{1,0:T(8,128)S(1)}, f32[200,768]{1,0:T(8,128)S(1)}, u32[]{:S(2)}, u32[]{:S(2)}) collective-permute-start(f32[200,768]{1,0:T(8,128)S(1)} %get-tuple-element.20.send0), channel_id=1, source_target_pairs={{0,1},{1,0},{2,3},{3,2},{4,5},{5,4},{6,7},{7,6},{8,9},{9,8},{10,11... | collective-permute-start | bytes 1843208 | tf_op jit(solution)/shard_map/ppermute | solution.py:389
  56.6 2.1 %collective-permute-start.5 = (f32[192,768]{1,0:T(8,128)S(1)}, f32[192,768]{1,0:T(8,128)S(1)}, u32[]{:S(2)}, u32[]{:S(2)}) collective-permute-start(f32[192,768]{1,0:T(8,128)S(1)} %shard_map.74), channel_id=1, source_target_pairs={{0,1},{1,0},{2,3},{3,2},{4,5},{5,4},{6,7},{7,6},{8,9},{9,8},{10,11... | collective-permute-start | bytes 1769480 | tf_op jit(solution)/shard_map/ppermute | solution.py:389
  59.0 11.4 %collective-permute-start.6 = (s16[112,768]{1,0:T(8,128)(2,1)S(1)}, s16[112,768]{1,0:T(8,128)(2,1)S(1)}, u32[]{:S(2)}, u32[]{:S(2)}) collective-permute-start(s16[112,768]{1,0:T(8,128)(2,1)S(1)} %get-tuple-element.23), channel_id=1, source_target_pairs={{0,2},{2,4},{4,6},{6,0},{1,3},{3,5},{5,7},{7,1},{8,10},{10,12},{12... | collective-permute-start | bytes 516104 | tf_op jit(solution)/shard_map/ppermute | solution.py:401
  59.6 10.8 %collective-permute-start.7 = (s16[112,768]{1,0:T(8,128)(2,1)S(1)}, s16[112,768]{1,0:T(8,128)(2,1)S(1)}, u32[]{:S(2)}, u32[]{:S(2)}) collective-permute-start(s16[112,768]{1,0:T(8,128)(2,1)S(1)} %get-tuple-element.24), channel_id=1, source_target_pairs={{0,4},{2,6},{4,0},{6,2},{1,5},{3,7},{5,1},{7,3},{8,12},{10,14},{12... | collective-permute-start | bytes 516104 | tf_op jit(solution)/shard_map/ppermute | solution.py:401
  61.7 9.3 %collective-permute-start.8 = (s16[112,768]{1,0:T(8,128)(2,1)S(1)}, s16[112,768]{1,0:T(8,128)(2,1)S(1)}, u32[]{:S(2)}, u32[]{:S(2)}) collective-permute-start(s16[112,768]{1,0:T(8,128)(2,1)S(1)} %get-tuple-element.25), channel_id=1, source_target_pairs={{0,6},{2,0},{4,2},{6,4},{1,7},{3,1},{5,3},{7,5},{8,14},{10,8},{12,... | collective-permute-start | bytes 516104 | tf_op jit(solution)/shard_map/ppermute | solution.py:401
  71.0 14.7 %copy-start.2 = (s32[32]{0:T(128)S(1)}, s32[32]{0:T(128)}, u32[]{:S(2)}) copy-start(s32[32]{0:T(128)} %order.1) | copy-start | bytes 388

commit v4 on v3

--- a/solution.py
+++ b/solution.py
@@ -40,7 +40,7 @@
     z, c = place[1], place[2]
     table_rows = table.shape[1]
     tiles = perms.shape[1] // LANES
-    group = 5
+    group = 10
 
     def step(t, carry):
         block, part = t // (tiles // group), t % (tiles // group)
@@ -78,8 +78,8 @@
     )[:1]
 
 
-def pack_kernel(dosage, expression, out, kept, levels, done):
-    shards, _, _ = out.shape
+def pack_kernel(dosage, expression, out, kept, levels, squares, done):
+    shards, genes, _ = out.shape
     variants, width = dosage.shape
     pieces = variants // LANES
     copies = []
@@ -91,18 +91,17 @@
     fetch.start()
     for i in range(pieces):
         copies[i].wait()
-        total = jnp.zeros((LANES, LANES), jnp.float32)
         square = jnp.zeros((LANES, LANES), jnp.float32)
         for k in range(width // LANES):
             v = kept[i * LANES : (i + 1) * LANES, k * LANES : (k + 1) * LANES].astype(jnp.float32)
-            total = total + v
             square = square + v * v
-        for j, moment in enumerate((lane_sums(total), lane_sums(square))):
-            for d in range(shards):
-                out[d, j : j + 1, width + i * LANES : width + (i + 1) * LANES] = moment
+        squares[i * LANES : (i + 1) * LANES, :] = square
+    moments = (times(jnp.ones((TILE, width), jnp.bfloat16), kept[...])[:1], lane_sums(squares[...]))
     fetch.wait()
     for d in range(shards):
         out[d, :, :width] = levels[...]
+        for j in range(genes):
+            out[d, j : j + 1, width:] = moments[j]
 
 
 def first_kernel(variants, place, windows, every, perms, out, table, stat):
@@ -209,43 +208,58 @@
     return values.astype(jnp.int32).astype(jnp.int16)
 
 
-def split_kernel(keep0, send0, got0, keep1, got1, own, *refs):
-    messages, hold = refs[:3], refs[3]
-    largest = jnp.zeros((HALF, own.shape[1]), jnp.float32)
+def split_kernel(*refs):
+    *ins, own, m1, m2, m3, hold = refs
+    keep, got = ins[0], ins[-1]
+    variants = own.shape[1]
+    largest = jnp.zeros((HALF, variants), jnp.float32)
     for kz in range(4):
-        for h, (keep, got) in enumerate(((keep0, got0), (keep1, got1))):
-            for t in range(6):
-                at = kz * 48 + t * HALF
-                v = keep[at : at + HALF, :] + got[at : at + HALF, :]
-                to = h * 48 + t * HALF
-                if kz == 0:
-                    own[to : to + HALF, :] = v
-                else:
-                    hold[kz - 1, to : to + HALF, :] = v
-                    largest = jnp.maximum(largest, jnp.abs(v))
-    direct = send0[192:200, :] + got0[192:200, :]
-    own[96:104, :] = direct
-    codes = [bound_code(jnp.max(v, keepdims=True)) for v in (largest, jnp.abs(direct))]
-    row = lax.broadcasted_iota(jnp.int32, direct.shape, 0)
-    tail = jnp.where(row == 0, codes[0], jnp.where(row == 1, codes[1], 0.0))
-    tail = to_int16(jnp.concatenate([coded(direct, codes[1]), tail], axis=0))
-    for k, message in enumerate(messages):
         for t in range(6):
-            rows = slice(t * TILE, (t + 1) * TILE)
-            message[rows, :] = to_int16(coded(hold[k, rows, :], codes[0]))
-        message[96:112, :] = tail
-
-
-def maxima_kernel(place, info, stat, own, *refs):
-    messages, out = refs[:3], refs[3]
-    values, direct = own[:96, :], own[96:104, :]
-    for message in messages:
-        tail = message[96:112, :].astype(jnp.int32).astype(jnp.float32)
-        unit = 1.0 / (LEVELS * PARTS)
-        values = values + message[:96, :].astype(jnp.int32).astype(jnp.float32) * (tail[8:9] * unit)
-        direct = direct + tail[:8] * (tail[9:10] * unit)
+            at = kz * 48 + t * HALF
+            v = keep[at : at + HALF, :] + got[at : at + HALF, :]
+            if kz == 0:
+                own[t * HALF : (t + 1) * HALF, :] = v
+            else:
+                hold[at - 48 : at - 40, :] = v
+                largest = jnp.maximum(largest, jnp.abs(v))
+    code = bound_code(jnp.max(largest, keepdims=True))
+    if len(ins) == 3:
+        direct = ins[1][192:200, :] + got[192:200, :]
+        own[48:56, :] = direct
+        direct_code = bound_code(jnp.max(jnp.abs(direct), keepdims=True))
+        direct = to_int16(
+            jnp.concatenate([coded(direct, direct_code), jnp.zeros_like(direct)], axis=0)
+        )
+        direct_code = to_int16(jnp.broadcast_to(direct_code, (TILE, LANES)))
+    code_rows = to_int16(jnp.broadcast_to(code, (48, LANES)))
+    for k, message in enumerate((m1, m2, m3)):
+        for t in range(3):
+            rows = hold[k * 48 + t * TILE : k * 48 + (t + 1) * TILE, :]
+            message[t * TILE : (t + 1) * TILE, :variants] = to_int16(coded(rows, code))
+        message[:48, variants:] = code_rows
+        if len(ins) == 3:
+            message[48:64, :variants] = direct
+            message[48:64, variants:] = direct_code
+
+
+def decoded(message, variants):
+    q = message[...].astype(jnp.int32).astype(jnp.float32)
+    return q[:, :variants] * (q[:, variants : variants + 1] * (1.0 / (LEVELS * PARTS)))
+
+
+def maxima_kernel(place, info, stat, *refs):
+    out = refs[-1]
+    variants = stat.shape[1]
+    chunks = []
+    for h in range(CHUNKS):
+        own, *messages = refs[4 * h : 4 * h + 4]
+        rows = own.shape[0]
+        total = own[...]
+        for message in messages:
+            total = total + decoded(message, variants)[:rows]
+        chunks.append(total)
+    direct = chunks[0][48:56]
     offset = stat[0:1, :] * stat[1:2, :]
-    variants = offset.shape[1]
     index = lax.broadcasted_iota(jnp.int32, (1, variants), 1) + place[0] * variants
     index = index.astype(jnp.float32)
     lane = lax.broadcasted_iota(jnp.int32, (HALF, LANES), 1)
@@ -260,8 +274,7 @@
             back = offset * info[o : o + 1, 4 + j : 5 + j]
             inside = (index >= lo) & (index < hi)
             for h in range(CHUNKS):
-                at = h * 48 + n * HALF
-                v = jnp.abs(values[at : at + HALF] + back)
+                v = jnp.abs(chunks[h][n * HALF : (n + 1) * HALF] + back)
                 best = jnp.max(jnp.where(inside, v, 0.0), axis=1, keepdims=True)
                 tile = jnp.where(lane // HALF == n * CHUNKS + h, best, tile)
             v = jnp.abs(direct[n : n + 1] + back)
@@ -350,7 +363,11 @@
         [shape((shards, 2, width + variants)), shape((variants, width), jnp.bfloat16)],
         [dosage, expression.T],
         2,
-        [pltpu.VMEM((2, width), jnp.float32), pltpu.SemaphoreType.DMA((variants // LANES + 1,))],
+        [
+            pltpu.VMEM((2, width), jnp.float32),
+            pltpu.VMEM((variants, LANES), jnp.float32),
+            pltpu.SemaphoreType.DMA((variants // LANES + 1,)),
+        ],
         remote=(0, 1),
     )
     every = lax.all_to_all(packed, ("z", "core"), 0, 0, tiled=True)
@@ -374,7 +391,7 @@
         )
     ahead = [(i, (i + 1) % owners) for i in range(owners)]
     back = [(b, a) for a, b in ahead]
-    halves = []
+    sums = []
     for h, own in enumerate(shuffled):
         left = lax.ppermute(own, "gene", ahead)
         right = lax.ppermute(own, "gene", back)
@@ -388,19 +405,20 @@
             )
         got = lax.ppermute(send, "core", [(0, 1), (1, 0)])
         keep = call(functools.partial(product_kernel, 0, False), shape((192, variants)), args, 1)
-        halves += [keep, send, got] if h == 0 else [keep, got]
-    own, *parts = call(
-        split_kernel,
-        [shape((104, variants))] + [shape((112, variants), jnp.int16)] * 3,
-        halves,
-        1,
-        [pltpu.VMEM((3, 96, variants), jnp.float32)],
-    )
-    sums = []
-    for k in range(1, 4):
-        sums.append(lax.ppermute(parts[k - 1], "z", [(i, (i + k) % 4) for i in range(4)]))
+        depth = 56 if h == 0 else 48
+        own, *parts = call(
+            split_kernel,
+            [shape((depth, variants))]
+            + [shape((64 if h == 0 else 48, variants + LANES), jnp.int16)] * 3,
+            [keep, send, got] if h == 0 else [keep, got],
+            1,
+            [pltpu.VMEM((144, variants), jnp.float32)],
+        )
+        sums.append(own)
+        for k in range(1, 4):
+            sums.append(lax.ppermute(parts[k - 1], "z", [(i, (i + k) % 4) for i in range(4)]))
     everyone = owners * shards
-    lines = call(maxima_kernel, shape((everyone, LANES)), [place, info, stat, own, *sums], 2)
+    lines = call(maxima_kernel, shape((everyone, LANES)), [place, info, stat, *sums], 2)
     lines = lax.all_to_all(
         lines.reshape(everyone, 1, LANES), ("gene", "z", "core"), 0, 0, tiled=True
     ).reshape(everyone, LANES)

time: 87.7 us -> 91 us (1.038)
  waiting for transfers between devices: 25.5 us -> 19.4 us
  starting transfers between devices: 20.1 us -> 25.9 us
  blocking collectives: 13.8 us -> 18.6 us
  Pallas kernels: 27 us -> 25.9 us
    ppermute x3 -> x6, starting transfers between devices: 3.78 us -> 9.54 us  [on_device(): lax.ppermute(parts[k - 1], 'z', [(i, (i + k) % 4) for i in range(4)])]
    ppermute x2, waiting for transfers between devices: 5.38 us -> 0.01 us  [on_device(): right = lax.ppermute(own, 'gene', back)]
    all_to_all x1, blocking collectives: 13.8 us -> 18.6 us  [on_device(): lax.all_to_all(lines.reshape(everyone, 1, LANES), ('gene', 'z', 'core'),...]
    ppermute x3 -> x6, waiting for transfers between devices: 8.25 us -> 4.37 us  [on_device(): lax.ppermute(parts[k - 1], 'z', [(i, (i + k) % 4) for i in range(4)])]
    ppermute x2, waiting for transfers between devices: 5.52 us -> 9.02 us  [on_device(): left = lax.ppermute(own, 'gene', ahead)]
    ppermute x2, starting transfers between devices: 0.01 us -> 1.56 us  [on_device(): left = lax.ppermute(own, 'gene', ahead)]
    ppermute x2, starting transfers between devices: 10.7 us -> 9.2 us  [on_device(): right = lax.ppermute(own, 'gene', back)]
    pallas_call x10 -> x11, Pallas kernels: 27 us -> 25.9 us  [call(): return made(*args)]
  transfers between devices with their start and end apart: 10 -> 13, of which waited for: 6 -> 5; matrix products, arithmetic and copies ran while one was open for 0% -> 0% of each run, Pallas kernels for 13% -> 4%
where the time goes in v4:
time: 91 us; the launch traced here: 90.6 us
  Pallas kernels  25.9 us (28%)
  starting transfers between devices  25.9 us (28%)
  waiting for transfers between devices  19.4 us (21%)
  blocking collectives  18.6 us (20%)
    pallas_call x11, Pallas kernels, call(): return made(*args)  25.9 us
    all_to_all x1, blocking collectives, on_device(): lax.all_to_all(lines.reshape(everyone, 1, LANES), ('gene', 'z', 'core'),...  18.6 us
    ppermute x6, starting transfers between devices, on_device(): lax.ppermute(parts[k - 1], 'z', [(i, (i + k) % 4) for i in range(4)])  9.54 us
    ppermute x2, starting transfers between devices, on_device(): right = lax.ppermute(own, 'gene', back)  9.2 us
    ppermute x2, waiting for transfers between devices, on_device(): left = lax.ppermute(own, 'gene', ahead)  9.02 us
    all_to_all x1, waiting for transfers between devices, on_device(): every = lax.all_to_all(packed, ('z', 'core'), 0, 0, tiled=True)  6.03 us
    all_to_all x1, starting transfers between devices, on_device(): every = lax.all_to_all(packed, ('z', 'core'), 0, 0, tiled=True)  5.44 us
    ppermute x6, waiting for transfers between devices, on_device(): lax.ppermute(parts[k - 1], 'z', [(i, (i + k) % 4) for i in range(4)])  4.37 us
  transfers between devices with their start and end apart: 13, of which 5 were waited for; matrix products, arithmetic and copies ran while one was open for 0% of the time, Pallas kernels for 4%

profile of v4, /device:TPU:0, one launch (start us, length us, event | category | flops | bytes accessed | tf_op | source)
XLA Modules:
  0.0 90.6 jit_solution(15347947612423166736)
XLA Ops:
  0.6 0.0 copy-start
  0.6 0.0 copy-start.1
  0.7 3.2 %shard_map.68 = (f32[8,2,2048]{2,1,0:T(2,128)}, bf16[768,1280]{1,0:T(8,128)(2,1)S(1)}) custom-call(bf16[768,1280]{1,0:T(8,128)(2,1)} %dosage.1, f32[2,1280]{1,0:T(2,128)} %bitcast.11), custom_call_target="tpu_custom_call" | custom-call | flops 2000000000 | tf_op jit(solution)/shard_map/pallas_call | solution.py:347
  3.8 5.4 %all-to-all-start = ((f32[8,2,2048]{2,1,0:T(2,128)}), f32[8,2,2048]{2,1,0:T(2,128)S(1)}, u32[]{:S(2)}, u32[]{:S(2)}) async-start(f32[8,2,2048]{2,1,0:T(2,128)} %get-tuple-element.19), calls=%async_computation | async-start | bytes 262144 | tf_op jit(solution)/shard_map/all_to_all | solution.py:373
  9.3 0.1 pad_add_fusion.place
  9.4 6.0 %all-to-all-done.every = f32[8,2,2048]{2,1,0:T(2,128)S(1)} async-done(((f32[8,2,2048]{2,1,0:T(2,128)}), f32[8,2,2048]{2,1,0:T(2,128)S(1)}, u32[]{:S(2)}, u32[]{:S(2)}) %all-to-all-start) | async-done | bytes 131104 | tf_op jit(solution)/shard_map/all_to_all | solution.py:373
  15.4 0.0 copy-done
  15.4 0.0 copy-done.1
  15.4 8.7 %shard_map.69 = (bf16[144,1280]{1,0:T(8,128)(2,1)S(1)}, bf16[2,80,16,128]{3,2,1,0:T(8,128)(2,1)S(1)}, f32[8,768]{1,0:T(8,128)S(1)}) custom-call(s32[3]{0:T(128)S(1)} %pad_add_fusion.place, s32[2,2]{1,0:T(2,128)S(1)} %copy-done.1, f32[8,2,2048]{2,1,0:T(2,128)S(1)} %all-to-all-done.every, s32[128,1280]{1,0:T(8,128)S(1)} %copy-done), custom_call_target="tpu_custom_call" | custom-call | flops 8999999488 | tf_op jit(solution)/shard_map/pallas_call | solution.py:347
  24.1 7.8 %shard_map.73.own = bf16[128,1280]{1,0:T(8,128)(2,1)S(1)} custom-call(s32[3]{0:T(128)S(1)} %pad_add_fusion.place, s32[128,1280]{1,0:T(8,128)S(1)} %copy-done, bf16[2,80,16,128]{3,2,1,0:T(8,128)(2,1)S(1)} %get-tuple-element.29.table), custom_call_target="tpu_custom_call" | custom-call | flops 8999999488 | tf_op jit(solution)/shard_map/pallas_call | solution.py:347
  31.9 1.6 %collective-permute-start.6 = (bf16[128,1280]{1,0:T(8,128)(2,1)S(1)}, bf16[128,1280]{1,0:T(8,128)(2,1)S(1)}, u32[]{:S(2)}, u32[]{:S(2)}) collective-permute-start(bf16[128,1280]{1,0:T(8,128)(2,1)S(1)} %shard_map.73.own), channel_id=1, source_target_pairs={{0,8},{8,16},{16,24},{24,32},{32,40},{40,48},{48,56},{56,64},{64,7... | collective-permute-start | bytes 983048 | tf_op jit(solution)/shard_map/ppermute | solution.py:396
  33.5 3.9 %collective-permute-start.7 = (bf16[128,1280]{1,0:T(8,128)(2,1)S(1)}, bf16[128,1280]{1,0:T(8,128)(2,1)S(1)}, u32[]{:S(2)}, u32[]{:S(2)}) collective-permute-start(bf16[128,1280]{1,0:T(8,128)(2,1)S(1)} %shard_map.73.own), channel_id=1, source_target_pairs={{8,0},{16,8},{24,16},{32,24},{40,32},{48,40},{56,48},{64,56},{72,6... | collective-permute-start | bytes 983048 | tf_op jit(solution)/shard_map/ppermute | solution.py:397
  37.3 0.0 collective-permute-start
  37.3 5.3 %collective-permute-start.1 = (bf16[144,1280]{1,0:T(8,128)(2,1)S(1)}, bf16[144,1280]{1,0:T(8,128)(2,1)S(1)}, u32[]{:S(2)}, u32[]{:S(2)}) collective-permute-start(bf16[144,1280]{1,0:T(8,128)(2,1)S(1)} %get-tuple-element.20.own), channel_id=1, source_target_pairs={{8,0},{16,8},{24,16},{32,24},{40,32},{48,40},{56,48},{64,56},{72,6... | collective-permute-start | bytes 1105928 | tf_op jit(solution)/shard_map/ppermute | solution.py:397
  42.7 3.2 %collective-permute-done.6.left = bf16[128,1280]{1,0:T(8,128)(2,1)S(1)} collective-permute-done((bf16[128,1280]{1,0:T(8,128)(2,1)S(1)}, bf16[128,1280]{1,0:T(8,128)(2,1)S(1)}, u32[]{:S(2)}, u32[]{:S(2)}) %collective-permute-start.6) | collective-permute-done | bytes 327712 | tf_op jit(solution)/shard_map/ppermute | solution.py:396
  45.9 0.0 collective-permute-done.7.right
  45.9 0.8 shard_map.75
  46.7 0.1 collective-permute-start.8
  46.8 5.8 %collective-permute-done.left = bf16[144,1280]{1,0:T(8,128)(2,1)S(1)} collective-permute-done((bf16[144,1280]{1,0:T(8,128)(2,1)S(1)}, bf16[144,1280]{1,0:T(8,128)(2,1)S(1)}, u32[]{:S(2)}, u32[]{:S(2)}) %collective-permute-start) | collective-permute-done | bytes 368672 | tf_op jit(solution)/shard_map/ppermute | solution.py:396
  52.6 0.0 collective-permute-done.1.right
  52.6 0.7 shard_map.70
  53.3 0.1 collective-permute-start.2
  53.4 0.8 shard_map.74.refs_0_
  54.2 0.8 shard_map.71.refs_0_
  55.1 0.0 collective-permute-done.8.refs_1_
  55.1 0.3 shard_map.76
  55.3 0.6 collective-permute-start.9
  56.0 0.0 collective-permute-done.2.refs_2_
  56.0 0.3 shard_map.72
  56.2 0.5 collective-permute-start.3
  56.8 3.7 %collective-permute-start.4 = (s16[64,896]{1,0:T(8,128)(2,1)S(1)}, s16[64,896]{1,0:T(8,128)(2,1)S(1)}, u32[]{:S(2)}, u32[]{:S(2)}) collective-permute-start(s16[64,896]{1,0:T(8,128)(2,1)S(1)} %get-tuple-element.27), channel_id=1, source_target_pairs={{0,4},{2,6},{4,0},{6,2},{1,5},{3,7},{5,1},{7,3},{8,12},{10,14},{12... | collective-permute-start | bytes 344072 | tf_op jit(solution)/shard_map/ppermute | solution.py:419
  60.4 0.6 collective-permute-start.5
  61.0 1.5 %collective-permute-start.10 = (s16[48,896]{1,0:T(8,128)(2,1)S(1)}, s16[48,896]{1,0:T(8,128)(2,1)S(1)}, u32[]{:S(2)}, u32[]{:S(2)}) collective-permute-start(s16[48,896]{1,0:T(8,128)(2,1)S(1)} %get-tuple-element.32), channel_id=1, source_target_pairs={{0,4},{2,6},{4,0},{6,2},{1,5},{3,7},{5,1},{7,3},{8,12},{10,14},{12... | collective-permute-start | bytes 258056 | tf_op jit(solution)/shard_map/ppermute | solution.py:419
  62.5 0.0 collective-permute-done.9.refs_5_
  62.5 2.7 %collective-permute-start.11 = (s16[48,896]{1,0:T(8,128)(2,1)S(1)}, s16[48,896]{1,0:T(8,128)(2,1)S(1)}, u32[]{:S(2)}, u32[]{:S(2)}) collective-permute-start(s16[48,896]{1,0:T(8,128)(2,1)S(1)} %get-tuple-element.33), channel_id=1, source_target_pairs={{0,6},{2,0},{4,2},{6,4},{1,7},{3,1},{5,3},{7,5},{8,14},{10,8},{12,... | collective-permute-start | bytes 258056 | tf_op jit(solution)/shard_map/ppermute | solution.py:419
  65.1 2.9 %collective-permute-done.10.refs_6_ = s16[48,896]{1,0:T(8,128)(2,1)S(1)} collective-permute-done((s16[48,896]{1,0:T(8,128)(2,1)S(1)}, s16[48,896]{1,0:T(8,128)(2,1)S(1)}, u32[]{:S(2)}, u32[]{:S(2)}) %collective-permute-start.10) | collective-permute-done | bytes 86048 | tf_op jit(solution)/shard_map/ppermute | solution.py:419
  68.1 1.4 %collective-permute-done.11.refs_7_ = s16[48,896]{1,0:T(8,128)(2,1)S(1)} collective-permute-done((s16[48,896]{1,0:T(8,128)(2,1)S(1)}, s16[48,896]{1,0:T(8,128)(2,1)S(1)}, u32[]{:S(2)}, u32[]{:S(2)}) %collective-permute-start.11) | collective-permute-done | bytes 86048 | tf_op jit(solution)/shard_map/ppermute | solution.py:419
  69.5 0.0 collective-permute-done.3.refs_1_
  69.5 0.0 collective-permute-done.4.refs_2_
  69.5 0.0 collective-permute-done.5.refs_3_
  69.5 0.0 copy-start.2
  69.5 1.0 %shard_map.77 = f32[128,128]{1,0:T(8,128)S(1)} custom-call(s32[3]{0:T(128)S(1)} %pad_add_fusion.place, f32[8,128]{1,0:T(8,128)S(1)} %get-tuple-element.23.info, f32[8,768]{1,0:T(8,128)S(1)} %get-tuple-element.22.stat, f32[56,768]{1,0:T(8,128)S(1)} %get-tuple-element.25.refs_0_, s16[64,896]{1,0:T(8,128)(2,1)S(1)} %collective-permute-done.3.refs_1_, ...), custom_call_target="tpu_custom_call" | custom-call | flops 2000000000 | tf_op jit(solution)/shard_map/pallas_call | solution.py:347
  70.6 18.6 %all_to_all.10 = f32[128,1,128]{2,1,0:T(1,128)S(1)} all-to-all(f32[128,1,128]{2,1,0:T(1,128)S(1)} %bitcast.9), channel_id=1, replica_groups=mesh['gene'=16,'z'=4,'core'=2] {'gene','z','core'}, dimensions={0} | all-to-all | bytes 131072 | tf_op jit(solution)/shard_map/all_to_all | solution.py:422
  89.1 0.0 copy-done.2
  89.1 1.5 %shard_map.78 = (f32[2,128]{1,0:T(2,128)}, f32[1,2]{1,0:T(1,128)}) custom-call(s32[3]{0:T(128)S(1)} %pad_add_fusion.place, s32[32]{0:T(128)S(1)} %copy-done.2, f32[128,128]{1,0:T(8,128)S(1)} %bitcast.10), custom_call_target="tpu_custom_call" | custom-call | flops 2000000000 | tf_op jit(solution)/shard_map/pallas_call | solution.py:347
Async XLA Ops:
  0.6 14.8 %copy-start = (s32[128,1280]{1,0:T(8,128)S(1)}, s32[128,1280]{1,0:T(8,128)}, u32[]{:S(2)}) copy-start(s32[128,1280]{1,0:T(8,128)} %perms.3) | copy-start | bytes 1966084
  0.6 14.7 %copy-start.1 = (s32[2,2]{1,0:T(2,128)S(1)}, s32[2,2]{1,0:T(2,128)}, u32[]{:S(2)}) copy-start(s32[2,2]{1,0:T(2,128)} %windows.1) | copy-start | bytes 52
  3.8 11.5 %all-to-all-start = ((f32[8,2,2048]{2,1,0:T(2,128)}), f32[8,2,2048]{2,1,0:T(2,128)S(1)}, u32[]{:S(2)}, u32[]{:S(2)}) async-start(f32[8,2,2048]{2,1,0:T(2,128)} %get-tuple-element.19), calls=%async_computation | async-start | bytes 262144 | tf_op jit(solution)/shard_map/all_to_all | solution.py:373
  31.9 14.0 %collective-permute-start.6 = (bf16[128,1280]{1,0:T(8,128)(2,1)S(1)}, bf16[128,1280]{1,0:T(8,128)(2,1)S(1)}, u32[]{:S(2)}, u32[]{:S(2)}) collective-permute-start(bf16[128,1280]{1,0:T(8,128)(2,1)S(1)} %shard_map.73.own), channel_id=1, source_target_pairs={{0,8},{8,16},{16,24},{24,32},{32,40},{40,48},{48,56},{56,64},{64,7... | collective-permute-start | bytes 983048 | tf_op jit(solution)/shard_map/ppermute | solution.py:396
  33.5 12.4 %collective-permute-start.7 = (bf16[128,1280]{1,0:T(8,128)(2,1)S(1)}, bf16[128,1280]{1,0:T(8,128)(2,1)S(1)}, u32[]{:S(2)}, u32[]{:S(2)}) collective-permute-start(bf16[128,1280]{1,0:T(8,128)(2,1)S(1)} %shard_map.73.own), channel_id=1, source_target_pairs={{8,0},{16,8},{24,16},{32,24},{40,32},{48,40},{56,48},{64,56},{72,6... | collective-permute-start | bytes 983048 | tf_op jit(solution)/shard_map/ppermute | solution.py:397
  37.3 15.3 %collective-permute-start = (bf16[144,1280]{1,0:T(8,128)(2,1)S(1)}, bf16[144,1280]{1,0:T(8,128)(2,1)S(1)}, u32[]{:S(2)}, u32[]{:S(2)}) collective-permute-start(bf16[144,1280]{1,0:T(8,128)(2,1)S(1)} %get-tuple-element.20.own), channel_id=1, source_target_pairs={{0,8},{8,16},{16,24},{24,32},{32,40},{40,48},{48,56},{56,64},{64,7... | collective-permute-start | bytes 1105928 | tf_op jit(solution)/shard_map/ppermute | solution.py:396
  37.3 15.3 %collective-permute-start.1 = (bf16[144,1280]{1,0:T(8,128)(2,1)S(1)}, bf16[144,1280]{1,0:T(8,128)(2,1)S(1)}, u32[]{:S(2)}, u32[]{:S(2)}) collective-permute-start(bf16[144,1280]{1,0:T(8,128)(2,1)S(1)} %get-tuple-element.20.own), channel_id=1, source_target_pairs={{8,0},{16,8},{24,16},{32,24},{40,32},{48,40},{56,48},{64,56},{72,6... | collective-permute-start | bytes 1105928 | tf_op jit(solution)/shard_map/ppermute | solution.py:397
  46.7 8.4 %collective-permute-start.8 = (f32[192,768]{1,0:T(8,128)S(1)}, f32[192,768]{1,0:T(8,128)S(1)}, u32[]{:S(2)}, u32[]{:S(2)}) collective-permute-start(f32[192,768]{1,0:T(8,128)S(1)} %shard_map.75), channel_id=1, source_target_pairs={{0,1},{1,0},{2,3},{3,2},{4,5},{5,4},{6,7},{7,6},{8,9},{9,8},{10,11... | collective-permute-start | bytes 1769480 | tf_op jit(solution)/shard_map/ppermute | solution.py:406
  53.3 2.6 %collective-permute-start.2 = (f32[200,768]{1,0:T(8,128)S(1)}, f32[200,768]{1,0:T(8,128)S(1)}, u32[]{:S(2)}, u32[]{:S(2)}) collective-permute-start(f32[200,768]{1,0:T(8,128)S(1)} %get-tuple-element.24.refs_1_), channel_id=1, source_target_pairs={{0,1},{1,0},{2,3},{3,2},{4,5},{5,4},{6,7},{7,6},{8,9},{9,8},{10,11... | collective-permute-start | bytes 1843208 | tf_op jit(solution)/shard_map/ppermute | solution.py:406
  55.3 7.1 %collective-permute-start.9 = (s16[48,896]{1,0:T(8,128)(2,1)S(1)}, s16[48,896]{1,0:T(8,128)(2,1)S(1)}, u32[]{:S(2)}, u32[]{:S(2)}) collective-permute-start(s16[48,896]{1,0:T(8,128)(2,1)S(1)} %get-tuple-element.31), channel_id=1, source_target_pairs={{0,2},{2,4},{4,6},{6,0},{1,3},{3,5},{5,7},{7,1},{8,10},{10,12},{12... | collective-permute-start | bytes 258056 | tf_op jit(solution)/shard_map/ppermute | solution.py:419
  56.2 13.3 %collective-permute-start.3 = (s16[64,896]{1,0:T(8,128)(2,1)S(1)}, s16[64,896]{1,0:T(8,128)(2,1)S(1)}, u32[]{:S(2)}, u32[]{:S(2)}) collective-permute-start(s16[64,896]{1,0:T(8,128)(2,1)S(1)} %get-tuple-element.26), channel_id=1, source_target_pairs={{0,2},{2,4},{4,6},{6,0},{1,3},{3,5},{5,7},{7,1},{8,10},{10,12},{12... | collective-permute-start | bytes 344072 | tf_op jit(solution)/shard_map/ppermute | solution.py:419
  56.8 12.7 %collective-permute-start.4 = (s16[64,896]{1,0:T(8,128)(2,1)S(1)}, s16[64,896]{1,0:T(8,128)(2,1)S(1)}, u32[]{:S(2)}, u32[]{:S(2)}) collective-permute-start(s16[64,896]{1,0:T(8,128)(2,1)S(1)} %get-tuple-element.27), channel_id=1, source_target_pairs={{0,4},{2,6},{4,0},{6,2},{1,5},{3,7},{5,1},{7,3},{8,12},{10,14},{12... | collective-permute-start | bytes 344072 | tf_op jit(solution)/shard_map/ppermute | solution.py:419
  60.4 9.1 %collective-permute-start.5 = (s16[64,896]{1,0:T(8,128)(2,1)S(1)}, s16[64,896]{1,0:T(8,128)(2,1)S(1)}, u32[]{:S(2)}, u32[]{:S(2)}) collective-permute-start(s16[64,896]{1,0:T(8,128)(2,1)S(1)} %get-tuple-element.28), channel_id=1, source_target_pairs={{0,6},{2,0},{4,2},{6,4},{1,7},{3,1},{5,3},{7,5},{8,14},{10,8},{12,... | collective-permute-start | bytes 344072 | tf_op jit(solution)/shard_map/ppermute | solution.py:419
  61.0 7.1 %collective-permute-start.10 = (s16[48,896]{1,0:T(8,128)(2,1)S(1)}, s16[48,896]{1,0:T(8,128)(2,1)S(1)}, u32[]{:S(2)}, u32[]{:S(2)}) collective-permute-start(s16[48,896]{1,0:T(8,128)(2,1)S(1)} %get-tuple-element.32), channel_id=1, source_target_pairs={{0,4},{2,6},{4,0},{6,2},{1,5},{3,7},{5,1},{7,3},{8,12},{10,14},{12... | collective-permute-start | bytes 258056 | tf_op jit(solution)/shard_map/ppermute | solution.py:419
  62.5 7.0 %collective-permute-start.11 = (s16[48,896]{1,0:T(8,128)(2,1)S(1)}, s16[48,896]{1,0:T(8,128)(2,1)S(1)}, u32[]{:S(2)}, u32[]{:S(2)}) collective-permute-start(s16[48,896]{1,0:T(8,128)(2,1)S(1)} %get-tuple-element.33), channel_id=1, source_target_pairs={{0,6},{2,0},{4,2},{6,4},{1,7},{3,1},{5,3},{7,5},{8,14},{10,8},{12,... | collective-permute-start | bytes 258056 | tf_op jit(solution)/shard_map/ppermute | solution.py:419
  69.5 19.6 %copy-start.2 = (s32[32]{0:T(128)S(1)}, s32[32]{0:T(128)}, u32[]{:S(2)}) copy-start(s32[32]{0:T(128)} %order.1) | copy-start | bytes 388

commit v5 on v4

--- a/solution.py
+++ b/solution.py
@@ -36,36 +36,34 @@
     )
 
 
-def gather_chunk(chunk, place, perms, table, out):
+def look_up(chunk, genes, place, perms, theirs, table, out):
     z, c = place[1], place[2]
     table_rows = table.shape[1]
-    tiles = perms.shape[1] // LANES
-    group = 10
-
-    def step(t, carry):
-        block, part = t // (tiles // group), t % (tiles // group)
-        kc, pair = block // 2, block % 2
+    width = perms.shape[1]
+
+    def step(pair, carry):
         first = []
         for k in range(2):
-            zz = lax.rem(z + pair * 2 + k, 4)
-            cc = lax.rem(c + kc, 2)
-            first.append(pl.multiple_of((zz * 2 + cc) * 2 * HALF + chunk * HALF, HALF))
-        for u in range(group):
-            lane = pl.ds(pl.multiple_of((part * group + u) * LANES, LANES), LANES)
-            index = jnp.concatenate([perms[pl.ds(f, HALF), lane] for f in first], axis=0)
+            d = lax.rem(z + pair * 2 + k, 4) * 2 + c
+            first.append(pl.multiple_of(d * 2 * HALF + chunk * HALF, HALF))
+        for u in range(2 * width // LANES):
+            source = perms if u < width // LANES else theirs
+            lane = u % (width // LANES) * LANES
+            rows = [source[pl.ds(f, HALF), lane : lane + LANES] for f in first]
+            index = jnp.concatenate(rows, axis=0)
             low = (index & (LANES - 1)).astype(jnp.int16)
             high = (index >> 7).astype(jnp.int16)
-            found = [jnp.zeros((TILE, LANES), jnp.bfloat16) for _ in range(2)]
+            found = [jnp.zeros((TILE, LANES), jnp.bfloat16) for _ in genes]
             for r in range(table_rows):
                 here = high == jnp.int16(r)
-                for j in range(2):
-                    found[j] = jnp.where(here, lane_gather(table[j, r], low), found[j])
-            for j in range(2):
-                row = pl.multiple_of(block * 2 * TILE + j * TILE, TILE)
-                out[pl.ds(row, TILE), lane] = found[j]
+                for n, j in enumerate(genes):
+                    found[n] = jnp.where(here, lane_gather(table[j, r], low), found[n])
+            for n in range(len(genes)):
+                row = pl.multiple_of(n * 2 * TILE + pair * TILE, TILE)
+                out[pl.ds(row, TILE), u * LANES : (u + 1) * LANES] = found[n]
         return carry
 
-    lax.fori_loop(0, 4 * (tiles // group), step, 0)
+    lax.fori_loop(0, 2, step, 0)
 
 
 def lane_sums(rows):
@@ -78,7 +76,7 @@
     )[:1]
 
 
-def pack_kernel(dosage, expression, out, kept, levels, squares, done):
+def pack_kernel(dosage, expression, out, kept, levels, sums, done):
     shards, genes, _ = out.shape
     variants, width = dosage.shape
     pieces = variants // LANES
@@ -91,12 +89,16 @@
     fetch.start()
     for i in range(pieces):
         copies[i].wait()
+        rows = slice(i * LANES, (i + 1) * LANES)
+        total = jnp.zeros((LANES, LANES), jnp.float32)
         square = jnp.zeros((LANES, LANES), jnp.float32)
         for k in range(width // LANES):
-            v = kept[i * LANES : (i + 1) * LANES, k * LANES : (k + 1) * LANES].astype(jnp.float32)
+            v = kept[rows, k * LANES : (k + 1) * LANES].astype(jnp.float32)
+            total = total + v
             square = square + v * v
-        squares[i * LANES : (i + 1) * LANES, :] = square
-    moments = (times(jnp.ones((TILE, width), jnp.bfloat16), kept[...])[:1], lane_sums(squares[...]))
+        sums[0, rows, :] = total
+        sums[1, rows, :] = square
+    moments = [lane_sums(sums[j]) for j in range(2)]
     fetch.wait()
     for d in range(shards):
         out[d, :, :width] = levels[...]
@@ -104,7 +106,7 @@
             out[d, j : j + 1, width:] = moments[j]
 
 
-def first_kernel(variants, place, windows, every, perms, out, table, stat):
+def first_kernel(variants, place, windows, every, perms, theirs, out, table, stat):
     z, c = place[1], place[2]
     shards, genes, wide = every.shape
     width = wide - variants
@@ -115,7 +117,7 @@
     stat[...] = jnp.zeros_like(stat)
     stat[0:1, :] = row_mean
     stat[1:2, :] = lax.rsqrt(spread * samples)
-    own = every[z * 2 + c][:, :width]
+    own = jnp.concatenate([every[z * 2 + c][:, :width], every[z * 2 + 1 - c][:, :width]], axis=1)
     direct, sums = [], []
     for j in range(genes):
         x = every[:, j, :width]
@@ -131,8 +133,8 @@
                     jnp.bfloat16
                 )
         direct.append((own[j : j + 1] - mean) * scale)
-    row = lax.broadcasted_iota(jnp.int32, (TILE, width), 0)
-    lane = lax.broadcasted_iota(jnp.int32, (TILE, width), 1)
+    row = lax.broadcasted_iota(jnp.int32, (TILE, 2 * width), 0)
+    lane = lax.broadcasted_iota(jnp.int32, (TILE, 2 * width), 1)
     extra = jnp.where(row == 0, direct[0], jnp.where(row == 1, direct[1], 0.0))
     for j in range(genes):
         for b in range(2):
@@ -145,12 +147,12 @@
             digit = rest.astype(jnp.bfloat16).astype(jnp.float32)
             rest = rest - digit
             extra = jnp.where((row == 4 + d) & (lane == j), digit, extra)
-    out[8 * TILE : 9 * TILE, :] = extra.astype(jnp.bfloat16)
-    gather_chunk(0, place, perms, table, out)
-
-
-def later_kernel(chunk, place, perms, table, out):
-    gather_chunk(chunk, place, perms, table, out)
+    out[4 * TILE : 5 * TILE, :] = extra.astype(jnp.bfloat16)
+    look_up(0, (0, 1), place, perms, theirs, table, out)
+
+
+def later_kernel(gene, place, perms, theirs, table, out):
+    look_up(1, (gene,), place, perms, theirs, table, out)
 
 
 def times(rows, dosage):
@@ -159,87 +161,78 @@
     )
 
 
-def product_kernel(kc, with_direct, left, own, right, dosage, stat, *outs):
-    blocks = [ref[kc * 4 * TILE : (kc + 1) * 4 * TILE, :] for ref in (left, own, right)]
-    if with_direct:
-        blocks += [ref[8 * TILE :, :] for ref in (left, own, right)]
-    rows = jnp.concatenate(blocks, axis=0)
-    mean, scale = stat[0:1, :], stat[1:2, :]
-    got = (times(rows, dosage[...]) - jnp.sum(rows.astype(jnp.float32), axis=1, keepdims=True) * mean) * scale
-    out = outs[0]
+LEVELS = 32767.0
+PARTS = 256.0
+
+
+def bound_code(largest):
+    return jnp.clip(jnp.ceil(largest * PARTS), 1.0, LEVELS)
+
+
+def coded(values, code):
+    scaled = values * (LEVELS * PARTS / code)
+    return jnp.clip(jnp.round(scaled), -LEVELS, LEVELS)
+
+
+def to_int16(values):
+    return values.astype(jnp.int32).astype(jnp.int16)
+
+
+def sums_kernel(chunk, *refs):
+    count = 3 if chunk == 0 else 6
+    blocks = refs[:count]
+    kept, theirs, stat, own, m1, m2, m3 = refs[count : count + 7]
+    variants, width = kept.shape
+    pieces = []
     for o in range(3):
-        for kz in range(4):
-            for j in range(2):
-                src = o * 4 * TILE + (kz // 2) * 2 * TILE + j * TILE + (kz % 2) * HALF
-                to = kz * 48 + (o * 2 + j) * HALF
-                out[to : to + HALF, :] = got[src : src + HALF]
-    if with_direct:
+        for j in range(2):
+            if chunk == 0:
+                pieces.append(blocks[o][j * 2 * TILE : (j + 1) * 2 * TILE, :])
+            else:
+                pieces.append(blocks[j * 3 + o][...])
+    if chunk == 0:
+        pieces += [block[4 * TILE :, :] for block in blocks]
+    rows = jnp.concatenate(pieces, axis=0)
+    both = times(rows[:, :width], kept[...]) + times(rows[:, width:], theirs[...])
+    column = jnp.sum(rows.astype(jnp.float32), axis=1, keepdims=True)
+    got = (both - column * stat[0:1, :]) * stat[1:2, :]
+    part = lambda n, kz: got[n * 2 * TILE + kz * HALF : n * 2 * TILE + (kz + 1) * HALF]
+    for n in range(6):
+        own[n * HALF : (n + 1) * HALF, :] = part(n, 0)
+    largest = jnp.abs(part(0, 1))
+    for n in range(6):
+        for kz in range(1, 4):
+            largest = jnp.maximum(largest, jnp.abs(part(n, kz)))
+    code = bound_code(jnp.max(largest, keepdims=True))
+    code_rows = to_int16(jnp.broadcast_to(code, (48, LANES)))
+    for k, message in enumerate((m1, m2, m3)):
+        for t in range(3):
+            values = jnp.concatenate([part(2 * t, k + 1), part(2 * t + 1, k + 1)], axis=0)
+            message[t * TILE : (t + 1) * TILE, :variants] = to_int16(coded(values, code))
+        message[:48, variants:] = code_rows
+    if chunk == 0:
         first = 12 * TILE
-        zero = jnp.zeros((2, got.shape[1]), jnp.float32)
-        out[192:200, :] = jnp.concatenate(
+        zero = jnp.zeros((2, variants), jnp.float32)
+        direct = jnp.concatenate(
             [got[first + o * TILE : first + o * TILE + 2] for o in range(3)] + [zero], axis=0
         )
-        info = outs[1]
+        own[48:56, :] = direct
+        code = bound_code(jnp.max(jnp.abs(direct), keepdims=True))
+        tail = to_int16(jnp.concatenate([coded(direct, code), jnp.zeros_like(direct)], axis=0))
+        code = to_int16(jnp.broadcast_to(code, (TILE, LANES)))
+        for message in (m1, m2, m3):
+            message[48:64, :variants] = tail
+            message[48:64, variants:] = code
+        info = refs[-1]
         info[...] = jnp.zeros_like(info)
         lane = lax.broadcasted_iota(jnp.int32, (1, LANES), 1)
-        for o, ref in enumerate((left, own, right)):
-            e = ref[8 * TILE :, :LANES].astype(jnp.float32)
+        for o, block in enumerate(blocks):
+            e = block[4 * TILE :, :LANES].astype(jnp.float32)
             line = jnp.where(lane < 4, e[2:3] * 128.0 + e[3:4], 0.0)
             total = (e[4:5] + e[5:6]) + e[6:7]
             for j in range(2):
                 line = jnp.where(lane == 4 + j, total[:, j : j + 1], line)
             info[o : o + 1, :] = line
-
-
-LEVELS = 32767.0
-PARTS = 256.0
-
-
-def bound_code(largest):
-    return jnp.clip(jnp.ceil(largest * PARTS), 1.0, LEVELS)
-
-
-def coded(values, code):
-    scaled = values * (LEVELS * PARTS / code)
-    return jnp.clip(jnp.round(scaled), -LEVELS, LEVELS)
-
-
-def to_int16(values):
-    return values.astype(jnp.int32).astype(jnp.int16)
-
-
-def split_kernel(*refs):
-    *ins, own, m1, m2, m3, hold = refs
-    keep, got = ins[0], ins[-1]
-    variants = own.shape[1]
-    largest = jnp.zeros((HALF, variants), jnp.float32)
-    for kz in range(4):
-        for t in range(6):
-            at = kz * 48 + t * HALF
-            v = keep[at : at + HALF, :] + got[at : at + HALF, :]
-            if kz == 0:
-                own[t * HALF : (t + 1) * HALF, :] = v
-            else:
-                hold[at - 48 : at - 40, :] = v
-                largest = jnp.maximum(largest, jnp.abs(v))
-    code = bound_code(jnp.max(largest, keepdims=True))
-    if len(ins) == 3:
-        direct = ins[1][192:200, :] + got[192:200, :]
-        own[48:56, :] = direct
-        direct_code = bound_code(jnp.max(jnp.abs(direct), keepdims=True))
-        direct = to_int16(
-            jnp.concatenate([coded(direct, direct_code), jnp.zeros_like(direct)], axis=0)
-        )
-        direct_code = to_int16(jnp.broadcast_to(direct_code, (TILE, LANES)))
-    code_rows = to_int16(jnp.broadcast_to(code, (48, LANES)))
-    for k, message in enumerate((m1, m2, m3)):
-        for t in range(3):
-            rows = hold[k * 48 + t * TILE : k * 48 + (t + 1) * TILE, :]
-            message[t * TILE : (t + 1) * TILE, :variants] = to_int16(coded(rows, code))
-        message[:48, variants:] = code_rows
-        if len(ins) == 3:
-            message[48:64, :variants] = direct
-            message[48:64, variants:] = direct_code
 
 
 def decoded(message, variants):
@@ -358,14 +351,18 @@
     samples = width * shards
     g, z, c = lax.axis_index("gene"), lax.axis_index("z"), lax.axis_index("core")
     place = jnp.stack([g, z, c]).astype(jnp.int32)
-    packed, kept = call(
+    mates = [(0, 1), (1, 0)]
+    their_perms = lax.ppermute(perms, "core", mates)
+    theirs = lax.ppermute(dosage, "core", mates)
+    packed = call(
         pack_kernel,
-        [shape((shards, 2, width + variants)), shape((variants, width), jnp.bfloat16)],
+        shape((shards, 2, width + variants)),
         [dosage, expression.T],
         2,
         [
+            pltpu.VMEM((variants, width), jnp.bfloat16),
             pltpu.VMEM((2, width), jnp.float32),
-            pltpu.VMEM((variants, LANES), jnp.float32),
+            pltpu.VMEM((2, variants, LANES), jnp.float32),
             pltpu.SemaphoreType.DMA((variants // LANES + 1,)),
         ],
         remote=(0, 1),
@@ -375,45 +372,39 @@
     table_shape = shape((2, samples // LANES, TILE, LANES), jnp.bfloat16)
     first, table, stat = call(
         functools.partial(first_kernel, variants),
-        [shape((9 * TILE, width), jnp.bfloat16), table_shape, shape((8, variants))],
-        [place, windows, every, perms],
+        [shape((5 * TILE, 2 * width), jnp.bfloat16), table_shape, shape((8, variants))],
+        [place, windows, every, perms, their_perms],
         9,
     )
     shuffled = [first]
-    for h in range(1, CHUNKS):
+    for j in range(2):
         shuffled.append(
             call(
-                functools.partial(later_kernel, h),
-                shape((8 * TILE, width), jnp.bfloat16),
-                [place, perms, table],
-                9,
+                functools.partial(later_kernel, j),
+                shape((2 * TILE, 2 * width), jnp.bfloat16),
+                [place, perms, their_perms, table],
+                4,
             )
         )
     ahead = [(i, (i + 1) % owners) for i in range(owners)]
     back = [(b, a) for a, b in ahead]
-    sums = []
-    for h, own in enumerate(shuffled):
+    around = []
+    for own in shuffled:
         left = lax.ppermute(own, "gene", ahead)
         right = lax.ppermute(own, "gene", back)
-        args = [left, own, right, kept, stat]
+        around.append([left, own, right])
+    sums = []
+    for h in range(CHUNKS):
+        depth, deep = (56, 64) if h == 0 else (48, 48)
+        outs = [shape((depth, variants))] + [shape((deep, variants + LANES), jnp.int16)] * 3
+        own, *parts = call(
+            functools.partial(sums_kernel, h),
+            outs + ([shape((8, LANES))] if h == 0 else []),
+            (around[0] if h == 0 else around[1] + around[2]) + [dosage, theirs, stat],
+            2,
+        )
         if h == 0:
-            outs = [shape((200, variants)), shape((8, LANES))]
-            send, info = call(functools.partial(product_kernel, 1, True), outs, args, 1)
-        else:
-            send = call(
-                functools.partial(product_kernel, 1, False), shape((192, variants)), args, 1
-            )
-        got = lax.ppermute(send, "core", [(0, 1), (1, 0)])
-        keep = call(functools.partial(product_kernel, 0, False), shape((192, variants)), args, 1)
-        depth = 56 if h == 0 else 48
-        own, *parts = call(
-            split_kernel,
-            [shape((depth, variants))]
-            + [shape((64 if h == 0 else 48, variants + LANES), jnp.int16)] * 3,
-            [keep, send, got] if h == 0 else [keep, got],
-            1,
-            [pltpu.VMEM((144, variants), jnp.float32)],
-        )
+            info = parts.pop()
         sums.append(own)
         for k in range(1, 4):
             sums.append(lax.ppermute(parts[k - 1], "z", [(i, (i + k) % 4) for i in range(4)]))

time: 91 us -> 95.7 us (1.052)
  blocking collectives: 18.6 us -> 15.1 us
  waiting for transfers between devices: 19.4 us -> 22.2 us
  Pallas kernels: 25.9 us -> 28.5 us
  starting transfers between devices: 25.9 us -> 28.5 us
    ppermute x2 -> x3, waiting for transfers between devices: 0.01 us -> 6.53 us  [on_device(): right = lax.ppermute(own, 'gene', back)]
    all_to_all x1, blocking collectives: 18.6 us -> 15.1 us  [on_device(): lax.all_to_all(lines.reshape(everyone, 1, LANES), ('gene', 'z', 'core'),...]
    ppermute x2 -> x3, starting transfers between devices: 9.2 us -> 12.6 us  [on_device(): right = lax.ppermute(own, 'gene', back)]
    pallas_call x11 -> x8, Pallas kernels: 25.9 us -> 28.5 us  [call(): return made(*args)]
    ppermute x2 -> x3, waiting for transfers between devices: 9.02 us -> 7.18 us  [on_device(): left = lax.ppermute(own, 'gene', ahead)]
    ppermute x6, waiting for transfers between devices: 4.37 us -> 2.94 us  [on_device(): lax.ppermute(parts[k - 1], 'z', [(i, (i + k) % 4) for i in range(4)])]
    ppermute x2 -> x3, starting transfers between devices: 1.56 us -> 0.15 us  [on_device(): left = lax.ppermute(own, 'gene', ahead)]
  transfers between devices with their start and end apart: 13 -> 15, of which waited for: 5 -> 6; matrix products, arithmetic and copies ran while one was open for 0% -> 0% of each run, Pallas kernels for 4% -> 27%
where the time goes in v5:
time: 95.7 us; the launch traced here: 95.2 us
  starting transfers between devices  28.5 us (30%)
  Pallas kernels  28.5 us (30%)
  waiting for transfers between devices  22.2 us (23%)
  blocking collectives  15.1 us (16%)
    pallas_call x8, Pallas kernels, call(): return made(*args)  28.5 us
    all_to_all x1, blocking collectives, on_device(): lax.all_to_all(lines.reshape(everyone, 1, LANES), ('gene', 'z', 'core'),...  15.1 us
    ppermute x3, starting transfers between devices, on_device(): right = lax.ppermute(own, 'gene', back)  12.6 us
    ppermute x6, starting transfers between devices, on_device(): lax.ppermute(parts[k - 1], 'z', [(i, (i + k) % 4) for i in range(4)])  9.72 us
    ppermute x3, waiting for transfers between devices, on_device(): left = lax.ppermute(own, 'gene', ahead)  7.18 us
    ppermute x3, waiting for transfers between devices, on_device(): right = lax.ppermute(own, 'gene', back)  6.53 us
    all_to_all x1, waiting for transfers between devices, on_device(): every = lax.all_to_all(packed, ('z', 'core'), 0, 0, tiled=True)  5.52 us
    all_to_all x1, starting transfers between devices, on_device(): every = lax.all_to_all(packed, ('z', 'core'), 0, 0, tiled=True)  5.51 us
  transfers between devices with their start and end apart: 15, of which 6 were waited for; matrix products, arithmetic and copies ran while one was open for 0% of the time, Pallas kernels for 27%

profile of v5, /device:TPU:0, one launch (start us, length us, event | category | flops | bytes accessed | tf_op | source)
XLA Modules:
  0.0 95.2 jit_solution(18090675913702637855)
XLA Ops:
  0.6 0.1 collective-permute-start
  0.7 0.0 copy-start
  0.7 0.0 copy-start.1
  0.7 0.0 copy-start.2
  0.8 3.1 %shard_map.68 = f32[8,2,2048]{2,1,0:T(2,128)} custom-call(bf16[768,1280]{1,0:T(8,128)(2,1)} %refs_6_.1, f32[2,1280]{1,0:T(2,128)} %bitcast.11), custom_call_target="tpu_custom_call" | custom-call | flops 2000000000 | tf_op jit(solution)/shard_map/pallas_call | solution.py:340
  3.8 5.5 %all-to-all-start = ((f32[8,2,2048]{2,1,0:T(2,128)}), f32[8,2,2048]{2,1,0:T(2,128)S(1)}, u32[]{:S(2)}, u32[]{:S(2)}) async-start(f32[8,2,2048]{2,1,0:T(2,128)} %shard_map.68), calls=%async_computation | async-start | bytes 262144 | tf_op jit(solution)/shard_map/all_to_all | solution.py:370
  9.3 0.0 copy-done
  9.3 0.5 collective-permute-start.3
  9.8 0.1 pad_add_fusion.place
  9.9 5.5 %all-to-all-done.every = f32[8,2,2048]{2,1,0:T(2,128)S(1)} async-done(((f32[8,2,2048]{2,1,0:T(2,128)}), f32[8,2,2048]{2,1,0:T(2,128)S(1)}, u32[]{:S(2)}, u32[]{:S(2)}) %all-to-all-start) | async-done | bytes 131104 | tf_op jit(solution)/shard_map/all_to_all | solution.py:370
  15.4 0.0 collective-permute-done.theirs
  15.4 0.0 copy-done.1
  15.4 0.0 copy-done.2
  15.4 8.5 %shard_map.69 = (bf16[80,2560]{1,0:T(8,128)(2,1)S(1)}, bf16[2,80,16,128]{3,2,1,0:T(8,128)(2,1)S(1)}, f32[8,768]{1,0:T(8,128)S(1)}) custom-call(s32[3]{0:T(128)S(1)} %pad_add_fusion.place, s32[2,2]{1,0:T(2,128)S(1)} %copy-done.2, f32[8,2,2048]{2,1,0:T(2,128)S(1)} %all-to-all-done.every, s32[128,1280]{1,0:T(8,128)S(1)} %copy-done.1, ...), custom_call_target="tpu_custom_call" | custom-call | flops 8999999488 | tf_op jit(solution)/shard_map/pallas_call | solution.py:340
  23.9 4.2 %shard_map.72.refs_4_ = bf16[32,2560]{1,0:T(8,128)(2,1)S(1)} custom-call(s32[3]{0:T(128)S(1)} %pad_add_fusion.place, s32[128,1280]{1,0:T(8,128)S(1)} %copy-done.1, s32[128,1280]{1,0:T(8,128)S(1)} %collective-permute-done.theirs, bf16[2,80,16,128]{3,2,1,0:T(8,128)(2,1)S(1)} %get-tuple-element.23.table), custom_call_target="tpu_custom_call" | custom-call | flops 4000000000 | tf_op jit(solution)/shard_map/pallas_call | solution.py:340
  28.1 5.3 %collective-permute-start.10 = (bf16[32,2560]{1,0:T(8,128)(2,1)S(1)}, bf16[32,2560]{1,0:T(8,128)(2,1)S(1)}, u32[]{:S(2)}, u32[]{:S(2)}) collective-permute-start(bf16[32,2560]{1,0:T(8,128)(2,1)S(1)} %shard_map.72.refs_4_), channel_id=1, source_target_pairs={{8,0},{16,8},{24,16},{32,24},{40,32},{48,40},{56,48},{64,56},{72,6... | collective-permute-start | bytes 491528 | tf_op jit(solution)/shard_map/ppermute | solution.py:394
  33.4 4.2 %shard_map.71.refs_1_ = bf16[32,2560]{1,0:T(8,128)(2,1)S(1)} custom-call(s32[3]{0:T(128)S(1)} %pad_add_fusion.place, s32[128,1280]{1,0:T(8,128)S(1)} %copy-done.1, s32[128,1280]{1,0:T(8,128)S(1)} %collective-permute-done.theirs, bf16[2,80,16,128]{3,2,1,0:T(8,128)(2,1)S(1)} %get-tuple-element.23.table), custom_call_target="tpu_custom_call" | custom-call | flops 4000000000 | tf_op jit(solution)/shard_map/pallas_call | solution.py:340
  37.6 0.1 collective-permute-start.7
  37.7 0.1 collective-permute-start.1
  37.7 5.3 %collective-permute-start.2 = (bf16[80,2560]{1,0:T(8,128)(2,1)S(1)}, bf16[80,2560]{1,0:T(8,128)(2,1)S(1)}, u32[]{:S(2)}, u32[]{:S(2)}) collective-permute-start(bf16[80,2560]{1,0:T(8,128)(2,1)S(1)} %get-tuple-element.16.refs_1_), channel_id=1, source_target_pairs={{8,0},{16,8},{24,16},{32,24},{40,32},{48,40},{56,48},{64,56},{72,6... | collective-permute-start | bytes 1228808 | tf_op jit(solution)/shard_map/ppermute | solution.py:394
  43.1 0.0 collective-permute-done.10.refs_5_
  43.1 1.9 %collective-permute-start.8 = (bf16[32,2560]{1,0:T(8,128)(2,1)S(1)}, bf16[32,2560]{1,0:T(8,128)(2,1)S(1)}, u32[]{:S(2)}, u32[]{:S(2)}) collective-permute-start(bf16[32,2560]{1,0:T(8,128)(2,1)S(1)} %shard_map.71.refs_1_), channel_id=1, source_target_pairs={{8,0},{16,8},{24,16},{32,24},{40,32},{48,40},{56,48},{64,56},{72,6... | collective-permute-start | bytes 491528 | tf_op jit(solution)/shard_map/ppermute | solution.py:394
  45.0 3.0 %collective-permute-done.7.refs_0_ = bf16[32,2560]{1,0:T(8,128)(2,1)S(1)} collective-permute-done((bf16[32,2560]{1,0:T(8,128)(2,1)S(1)}, bf16[32,2560]{1,0:T(8,128)(2,1)S(1)}, u32[]{:S(2)}, u32[]{:S(2)}) %collective-permute-start.7) | collective-permute-done | bytes 163872 | tf_op jit(solution)/shard_map/ppermute | solution.py:393
  48.0 0.0 collective-permute-start.9
  48.0 6.5 %collective-permute-done.8.refs_2_ = bf16[32,2560]{1,0:T(8,128)(2,1)S(1)} collective-permute-done((bf16[32,2560]{1,0:T(8,128)(2,1)S(1)}, bf16[32,2560]{1,0:T(8,128)(2,1)S(1)}, u32[]{:S(2)}, u32[]{:S(2)}) %collective-permute-start.8) | collective-permute-done | bytes 163872 | tf_op jit(solution)/shard_map/ppermute | solution.py:394
  54.6 4.2 %collective-permute-done.9.refs_3_ = bf16[32,2560]{1,0:T(8,128)(2,1)S(1)} collective-permute-done((bf16[32,2560]{1,0:T(8,128)(2,1)S(1)}, bf16[32,2560]{1,0:T(8,128)(2,1)S(1)}, u32[]{:S(2)}, u32[]{:S(2)}) %collective-permute-start.9) | collective-permute-done | bytes 163872 | tf_op jit(solution)/shard_map/ppermute | solution.py:393
  58.7 0.0 collective-permute-done.3.refs_4_.refs_7_
  58.7 3.2 %shard_map.73 = (f32[48,768]{1,0:T(8,128)S(1)}, s16[48,896]{1,0:T(8,128)(2,1)S(1)}, s16[48,896]{1,0:T(8,128)(2,1)S(1)}, s16[48,896]{1,0:T(8,128)(2,1)S(1)}) custom-call(bf16[32,2560]{1,0:T(8,128)(2,1)S(1)} %collective-permute-done.7.refs_0_, bf16[32,2560]{1,0:T(8,128)(2,1)S(1)} %shard_map.71.refs_1_, bf16[32,2560]{1,0:T(8,128)(2,1)S(1)} %collective-permute-done.8.refs_2_, ...), custom_call_target="tpu_custom_call" | custom-call | flops 2000000000 | tf_op jit(solution)/shard_map/pallas_call | solution.py:340
  61.9 0.8 collective-permute-start.11
  62.7 0.0 collective-permute-done.1.refs_0_
  62.7 0.0 collective-permute-done.2.refs_2_
  62.7 3.0 %shard_map.70 = (f32[56,768]{1,0:T(8,128)S(1)}, s16[64,896]{1,0:T(8,128)(2,1)S(1)}, s16[64,896]{1,0:T(8,128)(2,1)S(1)}, s16[64,896]{1,0:T(8,128)(2,1)S(1)}, f32[8,128]{1,0:T(8,128)S(1)}) custom-call(bf16[80,2560]{1,0:T(8,128)(2,1)S(1)} %collective-permute-done.1.refs_0_, bf16[80,2560]{1,0:T(8,128)(2,1)S(1)} %get-tuple-element.16.refs_1_, ...), custom_call_target="tpu_custom_call" | custom-call | flops 2000000000 | tf_op jit(solution)/shard_map/pallas_call | solution.py:340
  65.7 0.6 collective-permute-start.4
  66.2 3.7 %collective-permute-start.5 = (s16[64,896]{1,0:T(8,128)(2,1)S(1)}, s16[64,896]{1,0:T(8,128)(2,1)S(1)}, u32[]{:S(2)}, u32[]{:S(2)}) collective-permute-start(s16[64,896]{1,0:T(8,128)(2,1)S(1)} %get-tuple-element.21), channel_id=1, source_target_pairs={{0,4},{2,6},{4,0},{6,2},{1,5},{3,7},{5,1},{7,3},{8,12},{10,14},{12... | collective-permute-start | bytes 344072 | tf_op jit(solution)/shard_map/ppermute | solution.py:410
  69.9 0.6 collective-permute-start.6
  70.5 1.5 %collective-permute-start.12 = (s16[48,896]{1,0:T(8,128)(2,1)S(1)}, s16[48,896]{1,0:T(8,128)(2,1)S(1)}, u32[]{:S(2)}, u32[]{:S(2)}) collective-permute-start(s16[48,896]{1,0:T(8,128)(2,1)S(1)} %get-tuple-element.26), channel_id=1, source_target_pairs={{0,4},{2,6},{4,0},{6,2},{1,5},{3,7},{5,1},{7,3},{8,12},{10,14},{12... | collective-permute-start | bytes 258056 | tf_op jit(solution)/shard_map/ppermute | solution.py:410
  71.9 0.0 collective-permute-done.11.refs_5_
  71.9 2.7 %collective-permute-start.13 = (s16[48,896]{1,0:T(8,128)(2,1)S(1)}, s16[48,896]{1,0:T(8,128)(2,1)S(1)}, u32[]{:S(2)}, u32[]{:S(2)}) collective-permute-start(s16[48,896]{1,0:T(8,128)(2,1)S(1)} %get-tuple-element.27), channel_id=1, source_target_pairs={{0,6},{2,0},{4,2},{6,4},{1,7},{3,1},{5,3},{7,5},{8,14},{10,8},{12,... | collective-permute-start | bytes 258056 | tf_op jit(solution)/shard_map/ppermute | solution.py:410
  74.6 1.8 %collective-permute-done.12.refs_6_ = s16[48,896]{1,0:T(8,128)(2,1)S(1)} collective-permute-done((s16[48,896]{1,0:T(8,128)(2,1)S(1)}, s16[48,896]{1,0:T(8,128)(2,1)S(1)}, u32[]{:S(2)}, u32[]{:S(2)}) %collective-permute-start.12) | collective-permute-done | bytes 86048 | tf_op jit(solution)/shard_map/ppermute | solution.py:410
  76.4 1.1 %collective-permute-done.13.refs_7_ = s16[48,896]{1,0:T(8,128)(2,1)S(1)} collective-permute-done((s16[48,896]{1,0:T(8,128)(2,1)S(1)}, s16[48,896]{1,0:T(8,128)(2,1)S(1)}, u32[]{:S(2)}, u32[]{:S(2)}) %collective-permute-start.13) | collective-permute-done | bytes 86048 | tf_op jit(solution)/shard_map/ppermute | solution.py:410
  77.5 0.0 collective-permute-done.4.refs_1_
  77.5 0.0 collective-permute-done.5.refs_2_
  77.5 0.0 collective-permute-done.6.refs_3_
  77.5 0.0 copy-start.3
  77.6 1.0 %shard_map.74 = f32[128,128]{1,0:T(8,128)S(1)} custom-call(s32[3]{0:T(128)S(1)} %pad_add_fusion.place, f32[8,128]{1,0:T(8,128)S(1)} %get-tuple-element.18.info, f32[8,768]{1,0:T(8,128)S(1)} %get-tuple-element.17.refs_5_.refs_8_.stat, f32[56,768]{1,0:T(8,128)S(1)} %get-tuple-element.19.refs_0_, s16[64,896]{1,0:T(8,128)(2,1)S(1)} %collective-permute-done.4.refs_1_, ...), custom_call_target="tpu_custom_call" | custom-call | flops 2000000000 | tf_op jit(solution)/shard_map/pallas_call | solution.py:340
  78.6 15.1 %all_to_all.10 = f32[128,1,128]{2,1,0:T(1,128)S(1)} all-to-all(f32[128,1,128]{2,1,0:T(1,128)S(1)} %bitcast.9), channel_id=1, replica_groups=mesh['gene'=16,'z'=4,'core'=2] {'gene','z','core'}, dimensions={0} | all-to-all | bytes 131072 | tf_op jit(solution)/shard_map/all_to_all | solution.py:413
  93.7 0.0 copy-done.3
  93.7 1.5 %shard_map.75 = (f32[2,128]{1,0:T(2,128)}, f32[1,2]{1,0:T(1,128)}) custom-call(s32[3]{0:T(128)S(1)} %pad_add_fusion.place, s32[32]{0:T(128)S(1)} %copy-done.3, f32[128,128]{1,0:T(8,128)S(1)} %bitcast.10), custom_call_target="tpu_custom_call" | custom-call | flops 2000000000 | tf_op jit(solution)/shard_map/pallas_call | solution.py:340
Async XLA Ops:
  0.6 14.8 %collective-permute-start = (s32[128,1280]{1,0:T(8,128)}, s32[128,1280]{1,0:T(8,128)S(1)}, u32[]{:S(2)}, u32[]{:S(2)}) collective-permute-start(s32[128,1280]{1,0:T(8,128)} %perms.5), channel_id=1, source_target_pairs={{0,1},{1,0},{2,3},{3,2},{4,5},{5,4},{6,7},{7,6},{8,9},{9,8},{10,11... | collective-permute-start | bytes 1966088 | tf_op jit(solution)/shard_map/ppermute | solution.py:355
  0.7 8.6 %copy-start = (bf16[768,1280]{1,0:T(8,128)(2,1)S(1)}, bf16[768,1280]{1,0:T(8,128)(2,1)}, u32[]{:S(2)}) copy-start(bf16[768,1280]{1,0:T(8,128)(2,1)} %refs_6_.1) | copy-start | bytes 5898244
  0.7 14.7 %copy-start.1 = (s32[128,1280]{1,0:T(8,128)S(1)}, s32[128,1280]{1,0:T(8,128)}, u32[]{:S(2)}) copy-start(s32[128,1280]{1,0:T(8,128)} %perms.5) | copy-start | bytes 1966084
  0.7 14.7 %copy-start.2 = (s32[2,2]{1,0:T(2,128)S(1)}, s32[2,2]{1,0:T(2,128)}, u32[]{:S(2)}) copy-start(s32[2,2]{1,0:T(2,128)} %windows.1) | copy-start | bytes 52
  3.8 11.6 %all-to-all-start = ((f32[8,2,2048]{2,1,0:T(2,128)}), f32[8,2,2048]{2,1,0:T(2,128)S(1)}, u32[]{:S(2)}, u32[]{:S(2)}) async-start(f32[8,2,2048]{2,1,0:T(2,128)} %shard_map.68), calls=%async_computation | async-start | bytes 262144 | tf_op jit(solution)/shard_map/all_to_all | solution.py:370
  9.3 49.4 %collective-permute-start.3 = (bf16[768,1280]{1,0:T(8,128)(2,1)S(1)}, bf16[768,1280]{1,0:T(8,128)(2,1)}, u32[]{:S(2)}, u32[]{:S(2)}) collective-permute-start(bf16[768,1280]{1,0:T(8,128)(2,1)S(1)} %copy-done), channel_id=1, source_target_pairs={{0,1},{1,0},{2,3},{3,2},{4,5},{5,4},{6,7},{7,6},{8,9},{9,8},{10,11... | collective-permute-start | bytes 5898248 | tf_op jit(solution)/shard_map/ppermute | solution.py:356
  28.1 15.0 %collective-permute-start.10 = (bf16[32,2560]{1,0:T(8,128)(2,1)S(1)}, bf16[32,2560]{1,0:T(8,128)(2,1)S(1)}, u32[]{:S(2)}, u32[]{:S(2)}) collective-permute-start(bf16[32,2560]{1,0:T(8,128)(2,1)S(1)} %shard_map.72.refs_4_), channel_id=1, source_target_pairs={{8,0},{16,8},{24,16},{32,24},{40,32},{48,40},{56,48},{64,56},{72,6... | collective-permute-start | bytes 491528 | tf_op jit(solution)/shard_map/ppermute | solution.py:394
  37.6 10.5 %collective-permute-start.7 = (bf16[32,2560]{1,0:T(8,128)(2,1)S(1)}, bf16[32,2560]{1,0:T(8,128)(2,1)S(1)}, u32[]{:S(2)}, u32[]{:S(2)}) collective-permute-start(bf16[32,2560]{1,0:T(8,128)(2,1)S(1)} %shard_map.71.refs_1_), channel_id=1, source_target_pairs={{0,8},{8,16},{16,24},{24,32},{32,40},{40,48},{48,56},{56,64},{64,7... | collective-permute-start | bytes 491528 | tf_op jit(solution)/shard_map/ppermute | solution.py:393
  37.7 25.1 %collective-permute-start.1 = (bf16[80,2560]{1,0:T(8,128)(2,1)S(1)}, bf16[80,2560]{1,0:T(8,128)(2,1)S(1)}, u32[]{:S(2)}, u32[]{:S(2)}) collective-permute-start(bf16[80,2560]{1,0:T(8,128)(2,1)S(1)} %get-tuple-element.16.refs_1_), channel_id=1, source_target_pairs={{0,8},{8,16},{16,24},{24,32},{32,40},{40,48},{48,56},{56,64},{64,7... | collective-permute-start | bytes 1228808 | tf_op jit(solution)/shard_map/ppermute | solution.py:393
  37.7 25.0 %collective-permute-start.2 = (bf16[80,2560]{1,0:T(8,128)(2,1)S(1)}, bf16[80,2560]{1,0:T(8,128)(2,1)S(1)}, u32[]{:S(2)}, u32[]{:S(2)}) collective-permute-start(bf16[80,2560]{1,0:T(8,128)(2,1)S(1)} %get-tuple-element.16.refs_1_), channel_id=1, source_target_pairs={{8,0},{16,8},{24,16},{32,24},{40,32},{48,40},{56,48},{64,56},{72,6... | collective-permute-start | bytes 1228808 | tf_op jit(solution)/shard_map/ppermute | solution.py:394
  43.1 11.5 %collective-permute-start.8 = (bf16[32,2560]{1,0:T(8,128)(2,1)S(1)}, bf16[32,2560]{1,0:T(8,128)(2,1)S(1)}, u32[]{:S(2)}, u32[]{:S(2)}) collective-permute-start(bf16[32,2560]{1,0:T(8,128)(2,1)S(1)} %shard_map.71.refs_1_), channel_id=1, source_target_pairs={{8,0},{16,8},{24,16},{32,24},{40,32},{48,40},{56,48},{64,56},{72,6... | collective-permute-start | bytes 491528 | tf_op jit(solution)/shard_map/ppermute | solution.py:394
  48.0 10.7 %collective-permute-start.9 = (bf16[32,2560]{1,0:T(8,128)(2,1)S(1)}, bf16[32,2560]{1,0:T(8,128)(2,1)S(1)}, u32[]{:S(2)}, u32[]{:S(2)}) collective-permute-start(bf16[32,2560]{1,0:T(8,128)(2,1)S(1)} %shard_map.72.refs_4_), channel_id=1, source_target_pairs={{0,8},{8,16},{16,24},{24,32},{32,40},{40,48},{48,56},{56,64},{64,7... | collective-permute-start | bytes 491528 | tf_op jit(solution)/shard_map/ppermute | solution.py:393
  61.9 10.0 %collective-permute-start.11 = (s16[48,896]{1,0:T(8,128)(2,1)S(1)}, s16[48,896]{1,0:T(8,128)(2,1)S(1)}, u32[]{:S(2)}, u32[]{:S(2)}) collective-permute-start(s16[48,896]{1,0:T(8,128)(2,1)S(1)} %get-tuple-element.25), channel_id=1, source_target_pairs={{0,2},{2,4},{4,6},{6,0},{1,3},{3,5},{5,7},{7,1},{8,10},{10,12},{12... | collective-permute-start | bytes 258056 | tf_op jit(solution)/shard_map/ppermute | solution.py:410
  65.7 11.8 %collective-permute-start.4 = (s16[64,896]{1,0:T(8,128)(2,1)S(1)}, s16[64,896]{1,0:T(8,128)(2,1)S(1)}, u32[]{:S(2)}, u32[]{:S(2)}) collective-permute-start(s16[64,896]{1,0:T(8,128)(2,1)S(1)} %get-tuple-element.20), channel_id=1, source_target_pairs={{0,2},{2,4},{4,6},{6,0},{1,3},{3,5},{5,7},{7,1},{8,10},{10,12},{12... | collective-permute-start | bytes 344072 | tf_op jit(solution)/shard_map/ppermute | solution.py:410
  66.2 11.3 %collective-permute-start.5 = (s16[64,896]{1,0:T(8,128)(2,1)S(1)}, s16[64,896]{1,0:T(8,128)(2,1)S(1)}, u32[]{:S(2)}, u32[]{:S(2)}) collective-permute-start(s16[64,896]{1,0:T(8,128)(2,1)S(1)} %get-tuple-element.21), channel_id=1, source_target_pairs={{0,4},{2,6},{4,0},{6,2},{1,5},{3,7},{5,1},{7,3},{8,12},{10,14},{12... | collective-permute-start | bytes 344072 | tf_op jit(solution)/shard_map/ppermute | solution.py:410
  69.9 7.6 %collective-permute-start.6 = (s16[64,896]{1,0:T(8,128)(2,1)S(1)}, s16[64,896]{1,0:T(8,128)(2,1)S(1)}, u32[]{:S(2)}, u32[]{:S(2)}) collective-permute-start(s16[64,896]{1,0:T(8,128)(2,1)S(1)} %get-tuple-element.22), channel_id=1, source_target_pairs={{0,6},{2,0},{4,2},{6,4},{1,7},{3,1},{5,3},{7,5},{8,14},{10,8},{12,... | collective-permute-start | bytes 344072 | tf_op jit(solution)/shard_map/ppermute | solution.py:410
  70.5 6.0 %collective-permute-start.12 = (s16[48,896]{1,0:T(8,128)(2,1)S(1)}, s16[48,896]{1,0:T(8,128)(2,1)S(1)}, u32[]{:S(2)}, u32[]{:S(2)}) collective-permute-start(s16[48,896]{1,0:T(8,128)(2,1)S(1)} %get-tuple-element.26), channel_id=1, source_target_pairs={{0,4},{2,6},{4,0},{6,2},{1,5},{3,7},{5,1},{7,3},{8,12},{10,14},{12... | collective-permute-start | bytes 258056 | tf_op jit(solution)/shard_map/ppermute | solution.py:410
  71.9 5.6 %collective-permute-start.13 = (s16[48,896]{1,0:T(8,128)(2,1)S(1)}, s16[48,896]{1,0:T(8,128)(2,1)S(1)}, u32[]{:S(2)}, u32[]{:S(2)}) collective-permute-start(s16[48,896]{1,0:T(8,128)(2,1)S(1)} %get-tuple-element.27), channel_id=1, source_target_pairs={{0,6},{2,0},{4,2},{6,4},{1,7},{3,1},{5,3},{7,5},{8,14},{10,8},{12,... | collective-permute-start | bytes 258056 | tf_op jit(solution)/shard_map/ppermute | solution.py:410
  77.5 16.2 %copy-start.3 = (s32[32]{0:T(128)S(1)}, s32[32]{0:T(128)}, u32[]{:S(2)}) copy-start(s32[32]{0:T(128)} %order.1) | copy-start | bytes 388

commit v6 on v5

v6 whole, which is shorter than its diff:
```python
import functools

import jax
import jax.numpy as jnp
from jax import lax
from jax.experimental import pallas as pl
from jax.experimental.pallas import tpu as pltpu
from jax.sharding import Mesh
from jax.sharding import PartitionSpec as P


epsilon = 1e-06
LANES = 128
TILE = 16
HALF = 8
CHUNKS = 2

VM = pl.BlockSpec(memory_space=pltpu.VMEM)
SM = pl.BlockSpec(memory_space=pltpu.SMEM)


def lane_gather(table, index):
    dims = lax.GatherDimensionNumbers(
        offset_dims=(),
        collapsed_slice_dims=(1,),
        start_index_map=(1,),
        operand_batching_dims=(0,),
        start_indices_batching_dims=(0,),
    )
    return lax.gather(
        table,
        index[..., None],
        dims,
        slice_sizes=(1, 1),
        mode=lax.GatherScatterMode.PROMISE_IN_BOUNDS,
    )


def look_up(chunk, genes, place, perms, theirs, table, out):
    z, c = place[1], place[2]
    table_rows = table.shape[1]
    width = perms.shape[1]

    def step(pair, carry):
        first = []
        for k in range(2):
            d = lax.rem(z + pair * 2 + k, 4) * 2 + c
            first.append(pl.multiple_of(d * 2 * HALF + chunk * HALF, HALF))
        for u in range(2 * width // LANES):
            source = perms if u < width // LANES else theirs
            lane = u % (width // LANES) * LANES
            rows = [source[pl.ds(f, HALF), lane : lane + LANES] for f in first]
            index = jnp.concatenate(rows, axis=0)
            low = (index & (LANES - 1)).astype(jnp.int16)
            high = (index >> 7).astype(jnp.int16)
            found = [jnp.zeros((TILE, LANES), jnp.bfloat16) for _ in genes]
            for r in range(table_rows):
                here = high == jnp.int16(r)
                for n, j in enumerate(genes):
                    found[n] = jnp.where(here, lane_gather(table[j, r], low), found[n])
            for n in range(len(genes)):
                row = pl.multiple_of(n * 2 * TILE + pair * TILE, TILE)
                out[pl.ds(row, TILE), u * LANES : (u + 1) * LANES] = found[n]
        return carry

    lax.fori_loop(0, 2, step, 0)


def lane_sums(rows):
    return lax.dot_general(
        jnp.ones((8, LANES), jnp.float32),
        rows,
        (((1,), (1,)), ((), ())),
        precision=lax.Precision.HIGHEST,
        preferred_element_type=jnp.float32,
    )[:1]


def copies_kernel(expression, out, done):
    copies = [
        pltpu.make_async_copy(expression, out.at[d], done.at[d]) for d in range(out.shape[0])
    ]
    for copy in copies:
        copy.start()
    for copy in copies:
        copy.wait()


def moments_kernel(dosage, theirs, out, sums):
    variants, width = dosage.shape

    def step(i, carry):
        rows = pl.ds(pl.multiple_of(i * LANES, LANES), LANES)
        total = jnp.zeros((LANES, LANES), jnp.float32)
        square = jnp.zeros((LANES, LANES), jnp.float32)
        for source in (dosage, theirs):
            for k in range(width // LANES):
                v = source[rows, k * LANES : (k + 1) * LANES].astype(jnp.float32)
                total = total + v
                square = square + v * v
        sums[0, rows, :] = total
        sums[1, rows, :] = square
        return carry

    lax.fori_loop(0, variants // LANES, step, 0)
    out[...] = jnp.zeros_like(out)
    for j in range(2):
        out[j : j + 1, :] = lane_sums(sums[j])


def first_kernel(place, windows, every, perms, theirs, out, table):
    z, c = place[1], place[2]
    shards, genes, width = every.shape
    samples = shards * width
    own = jnp.concatenate([every[z * 2 + c], every[z * 2 + 1 - c]], axis=1)
    direct = []
    for j in range(genes):
        x = every[:, j, :]
        mean = jnp.sum(x, keepdims=True) / samples
        center = x - mean
        scale = lax.rsqrt(jnp.sum(center * center, keepdims=True) / samples + epsilon)
        scaled = center * scale
        for k in range(shards):
            for i in range(width // LANES):
                piece = scaled[k : k + 1, i * LANES : (i + 1) * LANES]
                table[j, k * (width // LANES) + i] = jnp.broadcast_to(piece, (TILE, LANES)).astype(
                    jnp.bfloat16
                )
        direct.append((own[j : j + 1] - mean) * scale)
    row = lax.broadcasted_iota(jnp.int32, (TILE, 2 * width), 0)
    lane = lax.broadcasted_iota(jnp.int32, (TILE, 2 * width), 1)
    extra = jnp.where(row == 0, direct[0], jnp.where(row == 1, direct[1], 0.0))
    for j in range(genes):
        for b in range(2):
            w = windows[j, b]
            digits = ((w >> 7).astype(jnp.float32), (w & 127).astype(jnp.float32))
            for d in range(2):
                extra = jnp.where((row == 2 + d) & (lane == j * 2 + b), digits[d], extra)
    out[4 * TILE : 5 * TILE, :] = extra.astype(jnp.bfloat16)
    look_up(0, (0, 1), place, perms, theirs, table, out)


def later_kernel(chunk, place, perms, theirs, table, out):
    look_up(chunk, (0, 1), place, perms, theirs, table, out)


def times(rows, dosage):
    return lax.dot_general(
        rows, dosage, (((1,), (1,)), ((), ())), preferred_element_type=jnp.float32
    )


LEVELS = 32767.0
PARTS = 256.0


def bound_code(largest):
    return jnp.clip(jnp.ceil(largest * PARTS), 1.0, LEVELS)


def coded(values, code):
    scaled = values * (LEVELS * PARTS / code)
    return jnp.clip(jnp.round(scaled), -LEVELS, LEVELS)


def to_int16(values):
    return values.astype(jnp.int32).astype(jnp.int16)


def digits(x):
    whole = jnp.floor(x)
    rest = (x - whole) * 32768.0
    high = jnp.floor(rest)
    return whole, high, jnp.floor((rest - high) * 32768.0)


def undigits(whole, high, low):
    return whole + (high + low * (1.0 / 32768.0)) * (1.0 / 32768.0)


def mean_and_size(total, square, count):
    mean = total / count
    return mean, jnp.sqrt(jnp.maximum(square - total * mean, 0.0) + count * epsilon)


def sums_kernel(chunk, *refs):
    blocks = refs[:3]
    dosage, theirs, stat, own, m1, m2, m3 = refs[3:10]
    variants, width = dosage.shape
    rows = jnp.concatenate([block[: 4 * TILE, :] for block in blocks], axis=0)
    if chunk == 0:
        rows = jnp.concatenate([rows] + [block[4 * TILE :, :] for block in blocks], axis=0)
    both = times(rows[:, :width], dosage[...]) + times(rows[:, width:], theirs[...])
    column = jnp.sum(rows.astype(jnp.float32), axis=1, keepdims=True)
    mean, size = mean_and_size(stat[0:1, :], stat[1:2, :], 2.0 * width)
    got = (both - column * mean) * (1.0 / size)
    column = jnp.broadcast_to(column, (column.shape[0], LANES))
    at = lambda n, kz: slice(n * 2 * TILE + kz * HALF, n * 2 * TILE + (kz + 1) * HALF)
    for n in range(6):
        own[n * HALF : (n + 1) * HALF, :] = both[at(n, 0)]
    largest = jnp.abs(got[at(0, 1)])
    for n in range(6):
        for kz in range(1, 4):
            largest = jnp.maximum(largest, jnp.abs(got[at(n, kz)]))

    def beside(code, columns):
        lane = lax.broadcasted_iota(jnp.int32, columns.shape, 1)
        whole, high, low = digits(columns)
        line = jnp.where(lane == 1, whole, jnp.where(lane == 2, high, low))
        return to_int16(jnp.where(lane == 0, code, line))

    code = bound_code(jnp.max(largest, keepdims=True))
    for k, message in enumerate((m1, m2, m3)):
        for t in range(3):
            pair = [at(2 * t, k + 1), at(2 * t + 1, k + 1)]
            values = jnp.concatenate([got[p] for p in pair], axis=0)
            columns = jnp.concatenate([column[p] for p in pair], axis=0)
            message[t * TILE : (t + 1) * TILE, :variants] = to_int16(coded(values, code))
            message[t * TILE : (t + 1) * TILE, variants:] = beside(code, columns)
    if chunk == 0:
        spots = [slice((12 + o) * TILE, (12 + o) * TILE + 2) for o in range(3)]
        gather = lambda x: jnp.concatenate([x[p] for p in spots] + [jnp.zeros_like(x[:2])], axis=0)
        own[48:56, :] = gather(both)
        values, columns = gather(got), gather(column)
        code = bound_code(jnp.max(jnp.abs(values), keepdims=True))
        rest = list(digits(stat[0:1, :]) + digits(stat[1:2, :]))
        rest.append(jnp.zeros((2, variants), jnp.float32))
        tail = to_int16(jnp.concatenate([coded(values, code)] + rest, axis=0))
        side = beside(code, jnp.concatenate([columns, jnp.zeros_like(columns)], axis=0))
        for message in (m1, m2, m3):
            message[48:64, :variants] = tail
            message[48:64, variants:] = side
        info = refs[-1]
        info[...] = jnp.zeros_like(info)
        for o, block in enumerate(blocks):
            e = block[4 * TILE :, :LANES].astype(jnp.float32)
            info[o : o + 1, :] = e[2:3] * 128.0 + e[3:4]


def added(own, messages, means, sizes):
    total = own[...]
    rows, variants = total.shape
    for message, mean, size in zip(messages, means, sizes):
        side = message[:rows, variants:].astype(jnp.int32).astype(jnp.float32)
        column = undigits(side[:, 1:2], side[:, 2:3], side[:, 3:4])
        unit = side[:, 0:1] * (1.0 / (LEVELS * PARTS))
        codes = message[:rows, :variants].astype(jnp.int32).astype(jnp.float32)
        total = total + (codes * unit * size + column * mean)
    return total


def inside_rows(place, info, variants):
    index = lax.broadcasted_iota(jnp.int32, (1, variants), 1) + place[0] * variants
    index = index.astype(jnp.float32)
    for o in range(3):
        for j in range(2):
            lo = info[o : o + 1, j * 2 : j * 2 + 1]
            hi = info[o : o + 1, j * 2 + 1 : j * 2 + 2]
            yield (index >= lo) & (index < hi)


def best_tile(tile, h, total, inside):
    lane = lax.broadcasted_iota(jnp.int32, (HALF, LANES), 1)
    for n, mask in enumerate(inside):
        v = jnp.abs(total[n * HALF : (n + 1) * HALF])
        best = jnp.max(jnp.where(mask, v, 0.0), axis=1, keepdims=True)
        tile = jnp.where(lane // HALF == n * CHUNKS + h, best, tile)
    return tile


def early_kernel(samples, place, info, stat, own, m1, m2, m3, out, aux):
    variants = own.shape[1]
    count = samples / 4.0
    total, square = stat[0:1, :], stat[1:2, :]
    means, sizes = [], []
    for message in (m1, m2, m3):
        d = message[48:64, :variants].astype(jnp.int32).astype(jnp.float32)
        their_total = undigits(d[8:9], d[9:10], d[10:11])
        their_square = undigits(d[11:12], d[12:13], d[13:14])
        mean, size = mean_and_size(their_total, their_square, count)
        means.append(mean)
        sizes.append(size)
        total = total + their_total
        square = square + their_square
    row_mean = total / samples
    spread = square / samples - row_mean * row_mean + epsilon
    scale = lax.rsqrt(spread * samples)
    aux[0:1, :] = scale
    for q in range(3):
        aux[1 + q : 2 + q, :] = means[q]
        aux[4 + q : 5 + q, :] = sizes[q]
    aux[7:8, :] = jnp.zeros_like(scale)
    sums = added(own, (m1, m2, m3), means, sizes) * scale
    inside = list(inside_rows(place, info, variants))
    tile = best_tile(jnp.zeros((HALF, LANES), jnp.float32), 0, sums, inside)
    lane = lax.broadcasted_iota(jnp.int32, (HALF, LANES), 1)
    for n, mask in enumerate(inside):
        v = jnp.abs(sums[48 + n : 49 + n])
        best = jnp.max(jnp.where(mask, v, 0.0), axis=1, keepdims=True)
        tile = jnp.where(lane == 96 + n, best, tile)
    out[...] = tile


def maxima_kernel(place, info, aux, tile, own, m1, m2, m3, out):
    variants = own.shape[1]
    means = [aux[1 + q : 2 + q, :] for q in range(3)]
    sizes = [aux[4 + q : 5 + q, :] for q in range(3)]
    sums = added(own, (m1, m2, m3), means, sizes) * aux[0:1, :]
    tile = best_tile(tile[...], 1, sums, inside_rows(place, info, variants))
    lane = lax.broadcasted_iota(jnp.int32, (HALF, LANES), 1)
    row = lax.broadcasted_iota(jnp.int32, (HALF, LANES), 0)
    keep = ((lane < 96) & (lane % HALF == row)) | ((lane >= 96) & (row == 0))
    line = jnp.sum(jnp.where(keep, tile, 0.0), axis=0, keepdims=True)
    for i in range(out.shape[0] // HALF):
        out[i * HALF : (i + 1) * HALF, :] = jnp.broadcast_to(line, (HALF, LANES))


def final_kernel(place, order, parts, out, observed, store):
    shards = HALF
    owners = parts.shape[0] // shards
    block = lambda o: parts[o * shards : (o + 1) * shards, :]
    width = 2 * HALF
    for o in range(owners):
        best = block(o)
        if o > 0:
            best = jnp.maximum(best, pltpu.roll(block(o - 1), LANES - 2 * width, 1))
        if o < owners - 1:
            best = jnp.maximum(best, pltpu.roll(block(o + 1), 2 * width, 1))
        store[2 * o] = best
        store[2 * o + 1] = pltpu.roll(best, LANES - width, 1)
    g = place[0]
    zero = jnp.zeros((shards, LANES), jnp.float32)
    tails = [zero, zero]
    for i in range(2 * owners):
        value = store[order[i]]
        for k in range(2):
            tails[k] = jnp.where(i >= 2 * g + k, jnp.maximum(tails[k], value), tails[k])
    lane = lax.broadcasted_iota(jnp.int32, (shards, LANES), 1)
    row = lax.broadcasted_iota(jnp.int32, (shards, LANES), 0)
    for k in range(2):
        moved = pltpu.roll(tails[k], LANES - 2 * width, 1)
        moved = pltpu.roll(moved, 0, 1, stride=width, stride_axis=0)
        out[k : k + 1, :] = jnp.sum(
            jnp.where(lane // width == row, moved, 0.0), axis=0, keepdims=True
        )
    part = lambda o: parts[pl.ds(pl.multiple_of(o * shards, shards), shards), :][:1]
    seen = part(g)
    left = pltpu.roll(part(jnp.maximum(g - 1, 0)), LANES - 2, 1)
    right = pltpu.roll(part(jnp.minimum(g + 1, owners - 1)), 2, 1)
    seen = jnp.maximum(seen, jnp.where(g > 0, left, 0.0))
    seen = jnp.maximum(seen, jnp.where(g < owners - 1, right, 0.0))
    observed[...] = seen[:, 98:100]


def call(kernel, outs, args, us, scratch=(), remote=()):
    scalar = [a.size <= 64 for a in args]
    many = isinstance(outs, list)
    made = pl.pallas_call(
        kernel,
        out_shape=tuple(outs) if many else outs,
        in_specs=[
            pl.BlockSpec(memory_space=pltpu.HBM) if i in remote else SM if k else VM
            for i, k in enumerate(scalar)
        ],
        out_specs=tuple([VM] * len(outs))
        if many
        else pl.BlockSpec(memory_space=pltpu.HBM)
        if remote
        else VM,
        scratch_shapes=scratch,
        compiler_params=pltpu.CompilerParams(vmem_limit_bytes=24 << 20),
        cost_estimate=pl.CostEstimate(flops=int(us * 1e9), bytes_accessed=0, transcendentals=0),
    )
    args = [
        a
        if k
        else pltpu.with_memory_space_constraint(a, pltpu.HBM if i in remote else pltpu.VMEM)
        for i, (a, k) in enumerate(zip(args, scalar))
    ]
    return made(*args)


def shape(dims, kind=jnp.float32):
    return pltpu.VMEM(dims, kind)


def on_device(dosage, expression, perms, windows, order):
    variants, width = dosage.shape
    owners = lax.axis_size("gene")
    shards = 8
    samples = width * shards
    g, z, c = lax.axis_index("gene"), lax.axis_index("z"), lax.axis_index("core")
    place = jnp.stack([g, z, c]).astype(jnp.int32)
    mates = [(0, 1), (1, 0)]
    their_perms = lax.ppermute(perms, "core", mates)
    theirs = lax.ppermute(dosage, "core", mates)
    copies = call(
        copies_kernel,
        pltpu.HBM((shards, 2, width), jnp.float32),
        [expression.T],
        1,
        [pltpu.SemaphoreType.DMA((shards,))],
        remote=(0,),
    )
    every = lax.all_to_all(copies, ("z", "core"), 0, 0, tiled=True)
    stat = call(
        moments_kernel,
        shape((8, variants)),
        [dosage, theirs],
        2,
        [pltpu.VMEM((2, variants, LANES), jnp.float32)],
    )

    table_shape = shape((2, samples // LANES, TILE, LANES), jnp.bfloat16)
    first, table = call(
        first_kernel,
        [shape((5 * TILE, 2 * width), jnp.bfloat16), table_shape],
        [place, windows, every, perms, their_perms],
        9,
    )
    second = call(
        functools.partial(later_kernel, 1),
        shape((4 * TILE, 2 * width), jnp.bfloat16),
        [place, perms, their_perms, table],
        8,
    )
    ahead = [(i, (i + 1) % owners) for i in range(owners)]
    back = [(b, a) for a, b in ahead]
    sums = []
    for h, own in enumerate((first, second)):
        left = lax.ppermute(own, "gene", ahead)
        right = lax.ppermute(own, "gene", back)
        depth, deep = (56, 64) if h == 0 else (48, 48)
        outs = [shape((depth, variants))] + [shape((deep, variants + LANES), jnp.int16)] * 3
        own, *parts = call(
            functools.partial(sums_kernel, h),
            outs + ([shape((8, LANES))] if h == 0 else []),
            [left, own, right, dosage, theirs, stat],
            2,
        )
        if h == 0:
            info = parts.pop()
        group = [own]
        for k in range(1, 4):
            group.append(lax.ppermute(parts[k - 1], "z", [(i, (i + k) % 4) for i in range(4)]))
        sums.append(group)
    tile, aux = call(
        functools.partial(early_kernel, samples),
        [shape((HALF, LANES)), shape((8, variants))],
        [place, info, stat, *sums[0]],
        1,
    )
    everyone = owners * shards
    lines = call(maxima_kernel, shape((everyone, LANES)), [place, info, aux, tile, *sums[1]], 2)
    lines = lax.all_to_all(
        lines.reshape(everyone, 1, LANES), ("gene", "z", "core"), 0, 0, tiled=True
    ).reshape(everyone, LANES)
    successive, observed = call(
        final_kernel,
        [jax.ShapeDtypeStruct((2, LANES), jnp.float32), jax.ShapeDtypeStruct((1, 2), jnp.float32)],
        [place, order, lines],
        2,
        [pltpu.VMEM((2 * owners, HALF, LANES), jnp.float32)],
    )
    return observed.reshape(2), successive


def solution(mesh):
    split = Mesh(mesh.devices.reshape(16, 4, 2), ("gene", "z", "core"))
    samp = ("z", "core")
    placed = (P("gene", samp), P(samp, "gene"), P(None, samp), P("gene", None), P())
    return jax.shard_map(
        on_device,
        mesh=split,
        in_specs=placed,
        out_specs=(P("gene"), P("gene", None)),
        check_vma=False,
    )
```

time: 95.7 us -> 79.5 us (0.83)
  waiting for transfers between devices: 22.2 us -> 9.55 us
  starting transfers between devices: 28.5 us -> 25.2 us
    ppermute x3 -> x2, waiting for transfers between devices: 7.18 us -> 0.01 us  [on_device(): left = lax.ppermute(own, 'gene', ahead)]
    ppermute x3 -> x2, waiting for transfers between devices: 6.53 us -> 0.01 us  [on_device(): right = lax.ppermute(own, 'gene', back)]
    ppermute x3 -> x2, starting transfers between devices: 12.6 us -> 9.19 us  [on_device(): right = lax.ppermute(own, 'gene', back)]
    ppermute x3 -> x2, starting transfers between devices: 0.15 us -> 1.63 us  [on_device(): left = lax.ppermute(own, 'gene', ahead)]
    ppermute x6, starting transfers between devices: 9.72 us -> 8.33 us  [on_device(): lax.ppermute(parts[k - 1], 'z', [(i, (i + k) % 4) for i in range(4)])]
    ppermute x6, waiting for transfers between devices: 2.94 us -> 3.9 us  [on_device(): lax.ppermute(parts[k - 1], 'z', [(i, (i + k) % 4) for i in range(4)])]
    pallas_call x8 -> x9, Pallas kernels: 28.5 us -> 27.7 us  [call(): return made(*args)]
  transfers between devices with their start and end apart: 15 -> 13, of which waited for: 6 -> 5; matrix products, arithmetic and copies ran while one was open for 0% -> 0% of each run, Pallas kernels for 27% -> 32%
where the time goes in v6:
time: 79.5 us; the launch traced here: 79.1 us
  Pallas kernels  27.7 us (35%)
  starting transfers between devices  25.2 us (32%)
  blocking collectives  15.8 us (20%)
  waiting for transfers between devices  9.55 us (12%)
    pallas_call x9, Pallas kernels, call(): return made(*args)  27.7 us
    all_to_all x1, blocking collectives, on_device(): lax.all_to_all(lines.reshape(everyone, 1, LANES), ('gene', 'z', 'core'),...  15.8 us
    ppermute x2, starting transfers between devices, on_device(): right = lax.ppermute(own, 'gene', back)  9.19 us
    ppermute x6, starting transfers between devices, on_device(): lax.ppermute(parts[k - 1], 'z', [(i, (i + k) % 4) for i in range(4)])  8.33 us
    all_to_all x1, waiting for transfers between devices, on_device(): every = lax.all_to_all(copies, ('z', 'core'), 0, 0, tiled=True)  5.63 us
    all_to_all x1, starting transfers between devices, on_device(): every = lax.all_to_all(copies, ('z', 'core'), 0, 0, tiled=True)  5.44 us
    ppermute x6, waiting for transfers between devices, on_device(): lax.ppermute(parts[k - 1], 'z', [(i, (i + k) % 4) for i in range(4)])  3.9 us
    ppermute x2, starting transfers between devices, on_device(): left = lax.ppermute(own, 'gene', ahead)  1.63 us
  transfers between devices with their start and end apart: 13, of which 5 were waited for; matrix products, arithmetic and copies ran while one was open for 0% of the time, Pallas kernels for 32%

profile of v6, /device:TPU:0, one launch (start us, length us, event | category | flops | bytes accessed | tf_op | source)
XLA Modules:
  0.0 79.1 jit_solution(6917836945554277093)
XLA Ops:
  0.6 0.0 copy-start.1
  0.6 0.0 copy-start.2
  0.7 0.1 collective-permute-start
  0.7 0.5 collective-permute-start.3
  1.2 3.7 %shard_map.68 = f32[8,2,1280]{2,1,0:T(2,128)} custom-call(f32[2,1280]{1,0:T(2,128)} %bitcast.11), custom_call_target="tpu_custom_call" | custom-call | flops 1000000000 | tf_op jit(solution)/shard_map/pallas_call | solution.py:380
  4.9 5.4 %all-to-all-start = ((f32[8,2,1280]{2,1,0:T(2,128)}), f32[8,2,1280]{2,1,0:T(2,128)S(1)}, u32[]{:S(2)}, u32[]{:S(2)}) async-start(f32[8,2,1280]{2,1,0:T(2,128)} %shard_map.68), calls=%async_computation | async-start | bytes 163840 | tf_op jit(solution)/shard_map/all_to_all | solution.py:405
  10.3 0.1 pad_add_fusion.place
  10.4 5.6 %all-to-all-done.every = f32[8,2,1280]{2,1,0:T(2,128)S(1)} async-done(((f32[8,2,1280]{2,1,0:T(2,128)}), f32[8,2,1280]{2,1,0:T(2,128)S(1)}, u32[]{:S(2)}, u32[]{:S(2)}) %all-to-all-start) | async-done | bytes 81952 | tf_op jit(solution)/shard_map/all_to_all | solution.py:405
  16.1 0.0 collective-permute-done.theirs
  16.1 0.0 copy-done.1
  16.1 0.0 copy-done.2
  16.1 8.2 %shard_map.69 = (bf16[80,2560]{1,0:T(8,128)(2,1)S(1)}, bf16[2,80,16,128]{3,2,1,0:T(8,128)(2,1)S(1)}) custom-call(s32[3]{0:T(128)S(1)} %pad_add_fusion.place, s32[2,2]{1,0:T(2,128)S(1)} %copy-done.2, f32[8,2,1280]{2,1,0:T(2,128)S(1)} %all-to-all-done.every, s32[128,1280]{1,0:T(8,128)S(1)} %copy-done.1, s32[128,1280]{1,0:T(8,128)S(1)} %collective-permute-done.theirs), custom_call_target="tpu_custom_call" | custom-call | flops 8999999488 | tf_op jit(solution)/shard_map/pallas_call | solution.py:380
  24.2 1.6 %collective-permute-start.1 = (bf16[80,2560]{1,0:T(8,128)(2,1)S(1)}, bf16[80,2560]{1,0:T(8,128)(2,1)S(1)}, u32[]{:S(2)}, u32[]{:S(2)}) collective-permute-start(bf16[80,2560]{1,0:T(8,128)(2,1)S(1)} %get-tuple-element.17.refs_1_), channel_id=1, source_target_pairs={{0,8},{8,16},{16,24},{24,32},{32,40},{40,48},{48,56},{56,64},{64,7... | collective-permute-start | bytes 1228808 | tf_op jit(solution)/shard_map/ppermute | solution.py:431
  25.8 3.9 %collective-permute-start.2 = (bf16[80,2560]{1,0:T(8,128)(2,1)S(1)}, bf16[80,2560]{1,0:T(8,128)(2,1)S(1)}, u32[]{:S(2)}, u32[]{:S(2)}) collective-permute-start(bf16[80,2560]{1,0:T(8,128)(2,1)S(1)} %get-tuple-element.17.refs_1_), channel_id=1, source_target_pairs={{8,0},{16,8},{24,16},{32,24},{40,32},{48,40},{56,48},{64,56},{72,6... | collective-permute-start | bytes 1228808 | tf_op jit(solution)/shard_map/ppermute | solution.py:432
  29.7 0.0 copy-start
  29.7 7.7 %shard_map.73.refs_1_ = bf16[64,2560]{1,0:T(8,128)(2,1)S(1)} custom-call(s32[3]{0:T(128)S(1)} %pad_add_fusion.place, s32[128,1280]{1,0:T(8,128)S(1)} %copy-done.1, s32[128,1280]{1,0:T(8,128)S(1)} %collective-permute-done.theirs, bf16[2,80,16,128]{3,2,1,0:T(8,128)(2,1)S(1)} %get-tuple-element.25.table), custom_call_target="tpu_custom_call" | custom-call | flops 8000000000 | tf_op jit(solution)/shard_map/pallas_call | solution.py:380
  37.3 0.1 collective-permute-start.7
  37.4 5.3 %collective-permute-start.8 = (bf16[64,2560]{1,0:T(8,128)(2,1)S(1)}, bf16[64,2560]{1,0:T(8,128)(2,1)S(1)}, u32[]{:S(2)}, u32[]{:S(2)}) collective-permute-start(bf16[64,2560]{1,0:T(8,128)(2,1)S(1)} %shard_map.73.refs_1_), channel_id=1, source_target_pairs={{8,0},{16,8},{24,16},{32,24},{40,32},{48,40},{56,48},{64,56},{72,6... | collective-permute-start | bytes 983048 | tf_op jit(solution)/shard_map/ppermute | solution.py:432
  42.7 0.0 collective-permute-done.3.theirs.refs_4_
  42.7 0.0 copy-done
  42.7 1.8 %shard_map.70.refs_5_.stat = f32[8,768]{1,0:T(8,128)S(1)} custom-call(bf16[768,1280]{1,0:T(8,128)(2,1)S(1)} %copy-done, bf16[768,1280]{1,0:T(8,128)(2,1)S(1)} %collective-permute-done.3.theirs.refs_4_), custom_call_target="tpu_custom_call" | custom-call | flops 2000000000 | tf_op jit(solution)/shard_map/pallas_call | solution.py:380
  44.6 0.0 collective-permute-done.1.refs_0_
  44.6 0.0 collective-permute-done.2.refs_2_
  44.6 1.5 %shard_map.71 = (f32[56,768]{1,0:T(8,128)S(1)}, s16[64,896]{1,0:T(8,128)(2,1)S(1)}, s16[64,896]{1,0:T(8,128)(2,1)S(1)}, s16[64,896]{1,0:T(8,128)(2,1)S(1)}, f32[8,128]{1,0:T(8,128)S(1)}) custom-call(bf16[80,2560]{1,0:T(8,128)(2,1)S(1)} %collective-permute-done.1.refs_0_, bf16[80,2560]{1,0:T(8,128)(2,1)S(1)} %get-tuple-element.17.refs_1_, ...), custom_call_target="tpu_custom_call" | custom-call | flops 2000000000 | tf_op jit(solution)/shard_map/pallas_call | solution.py:380
  46.0 0.6 collective-permute-start.4
  46.7 2.1 %collective-permute-start.5 = (s16[64,896]{1,0:T(8,128)(2,1)S(1)}, s16[64,896]{1,0:T(8,128)(2,1)S(1)}, u32[]{:S(2)}, u32[]{:S(2)}) collective-permute-start(s16[64,896]{1,0:T(8,128)(2,1)S(1)} %get-tuple-element.21), channel_id=1, source_target_pairs={{0,4},{2,6},{4,0},{6,2},{1,5},{3,7},{5,1},{7,3},{8,12},{10,14},{12... | collective-permute-start | bytes 344072 | tf_op jit(solution)/shard_map/ppermute | solution.py:445
  48.7 1.0 %collective-permute-start.6 = (s16[64,896]{1,0:T(8,128)(2,1)S(1)}, s16[64,896]{1,0:T(8,128)(2,1)S(1)}, u32[]{:S(2)}, u32[]{:S(2)}) collective-permute-start(s16[64,896]{1,0:T(8,128)(2,1)S(1)} %get-tuple-element.22), channel_id=1, source_target_pairs={{0,6},{2,0},{4,2},{6,4},{1,7},{3,1},{5,3},{7,5},{8,14},{10,8},{12,... | collective-permute-start | bytes 344072 | tf_op jit(solution)/shard_map/ppermute | solution.py:445
  49.7 0.0 collective-permute-done.7.refs_0_
  49.7 0.0 collective-permute-done.8.refs_2_
  49.7 1.6 %shard_map.74 = (f32[48,768]{1,0:T(8,128)S(1)}, s16[48,896]{1,0:T(8,128)(2,1)S(1)}, s16[48,896]{1,0:T(8,128)(2,1)S(1)}, s16[48,896]{1,0:T(8,128)(2,1)S(1)}) custom-call(bf16[64,2560]{1,0:T(8,128)(2,1)S(1)} %collective-permute-done.7.refs_0_, bf16[64,2560]{1,0:T(8,128)(2,1)S(1)} %shard_map.73.refs_1_, bf16[64,2560]{1,0:T(8,128)(2,1)S(1)} %collective-permute-done.8.refs_2_, ...), custom_call_target="tpu_custom_call" | custom-call | flops 2000000000 | tf_op jit(solution)/shard_map/pallas_call | solution.py:380
  51.3 2.7 %collective-permute-start.10 = (s16[48,896]{1,0:T(8,128)(2,1)S(1)}, s16[48,896]{1,0:T(8,128)(2,1)S(1)}, u32[]{:S(2)}, u32[]{:S(2)}) collective-permute-start(s16[48,896]{1,0:T(8,128)(2,1)S(1)} %get-tuple-element.28), channel_id=1, source_target_pairs={{0,4},{2,6},{4,0},{6,2},{1,5},{3,7},{5,1},{7,3},{8,12},{10,14},{12... | collective-permute-start | bytes 258056 | tf_op jit(solution)/shard_map/ppermute | solution.py:445
  54.0 1.2 %collective-permute-start.11 = (s16[48,896]{1,0:T(8,128)(2,1)S(1)}, s16[48,896]{1,0:T(8,128)(2,1)S(1)}, u32[]{:S(2)}, u32[]{:S(2)}) collective-permute-start(s16[48,896]{1,0:T(8,128)(2,1)S(1)} %get-tuple-element.29), channel_id=1, source_target_pairs={{0,6},{2,0},{4,2},{6,4},{1,7},{3,1},{5,3},{7,5},{8,14},{10,8},{12,... | collective-permute-start | bytes 258056 | tf_op jit(solution)/shard_map/ppermute | solution.py:445
  55.1 0.0 collective-permute-done.4.m1
  55.1 0.9 %collective-permute-start.9 = (s16[48,896]{1,0:T(8,128)(2,1)S(1)}, s16[48,896]{1,0:T(8,128)(2,1)S(1)}, u32[]{:S(2)}, u32[]{:S(2)}) collective-permute-start(s16[48,896]{1,0:T(8,128)(2,1)S(1)} %get-tuple-element.27), channel_id=1, source_target_pairs={{0,2},{2,4},{4,6},{6,0},{1,3},{3,5},{5,7},{7,1},{8,10},{10,12},{12... | collective-permute-start | bytes 258056 | tf_op jit(solution)/shard_map/ppermute | solution.py:445
  56.0 0.0 collective-permute-done.5.m2
  56.0 0.1 collective-permute-done.6.m3
  56.1 0.9 %shard_map.72 = (f32[8,128]{1,0:T(8,128)S(1)}, f32[8,768]{1,0:T(8,128)S(1)}) custom-call(s32[3]{0:T(128)S(1)} %pad_add_fusion.place, f32[8,128]{1,0:T(8,128)S(1)} %get-tuple-element.18.info, f32[8,768]{1,0:T(8,128)S(1)} %shard_map.70.refs_5_.stat, f32[56,768]{1,0:T(8,128)S(1)} %get-tuple-element.19.own, s16[64,896]{1,0:T(8,128)(2,1)S(1)} %collective-permute-done.4.m1, ...), custom_call_target="tpu_custom_call" | custom-call | flops 1000000000 | tf_op jit(solution)/shard_map/pallas_call | solution.py:380
  57.0 0.5 collective-permute-done.10.m2
  57.5 1.0 %collective-permute-done.11.m3 = s16[48,896]{1,0:T(8,128)(2,1)S(1)} collective-permute-done((s16[48,896]{1,0:T(8,128)(2,1)S(1)}, s16[48,896]{1,0:T(8,128)(2,1)S(1)}, u32[]{:S(2)}, u32[]{:S(2)}) %collective-permute-start.11) | collective-permute-done | bytes 86048 | tf_op jit(solution)/shard_map/ppermute | solution.py:445
  58.5 2.4 %collective-permute-done.9.m1 = s16[48,896]{1,0:T(8,128)(2,1)S(1)} collective-permute-done((s16[48,896]{1,0:T(8,128)(2,1)S(1)}, s16[48,896]{1,0:T(8,128)(2,1)S(1)}, u32[]{:S(2)}, u32[]{:S(2)}) %collective-permute-start.9) | collective-permute-done | bytes 86048 | tf_op jit(solution)/shard_map/ppermute | solution.py:445
  60.8 0.0 copy-start.3
  60.8 0.9 %shard_map.75 = f32[128,128]{1,0:T(8,128)S(1)} custom-call(s32[3]{0:T(128)S(1)} %pad_add_fusion.place, f32[8,128]{1,0:T(8,128)S(1)} %get-tuple-element.18.info, f32[8,768]{1,0:T(8,128)S(1)} %get-tuple-element.23.aux, f32[8,128]{1,0:T(8,128)S(1)} %get-tuple-element.24.tile, f32[48,768]{1,0:T(8,128)S(1)} %get-tuple-element.26.own, ...), custom_call_target="tpu_custom_call" | custom-call | flops 2000000000 | tf_op jit(solution)/shard_map/pallas_call | solution.py:380
  61.8 15.8 %all_to_all.10 = f32[128,1,128]{2,1,0:T(1,128)S(1)} all-to-all(f32[128,1,128]{2,1,0:T(1,128)S(1)} %bitcast.9), channel_id=1, replica_groups=mesh['gene'=16,'z'=4,'core'=2] {'gene','z','core'}, dimensions={0} | all-to-all | bytes 131072 | tf_op jit(solution)/shard_map/all_to_all | solution.py:455
  77.6 0.0 copy-done.3
  77.6 1.5 %shard_map.76 = (f32[2,128]{1,0:T(2,128)}, f32[1,2]{1,0:T(1,128)}) custom-call(s32[3]{0:T(128)S(1)} %pad_add_fusion.place, s32[32]{0:T(128)S(1)} %copy-done.3, f32[128,128]{1,0:T(8,128)S(1)} %bitcast.10), custom_call_target="tpu_custom_call" | custom-call | flops 2000000000 | tf_op jit(solution)/shard_map/pallas_call | solution.py:380
Async XLA Ops:
  0.6 15.4 %copy-start.1 = (s32[128,1280]{1,0:T(8,128)S(1)}, s32[128,1280]{1,0:T(8,128)}, u32[]{:S(2)}) copy-start(s32[128,1280]{1,0:T(8,128)} %perms.3) | copy-start | bytes 1966084
  0.6 15.4 %copy-start.2 = (s32[2,2]{1,0:T(2,128)S(1)}, s32[2,2]{1,0:T(2,128)}, u32[]{:S(2)}) copy-start(s32[2,2]{1,0:T(2,128)} %windows.1) | copy-start | bytes 52
  0.7 15.4 %collective-permute-start = (s32[128,1280]{1,0:T(8,128)}, s32[128,1280]{1,0:T(8,128)S(1)}, u32[]{:S(2)}, u32[]{:S(2)}) collective-permute-start(s32[128,1280]{1,0:T(8,128)} %perms.3), channel_id=1, source_target_pairs={{0,1},{1,0},{2,3},{3,2},{4,5},{5,4},{6,7},{7,6},{8,9},{9,8},{10,11... | collective-permute-start | bytes 1966088 | tf_op jit(solution)/shard_map/ppermute | solution.py:395
  0.7 42.0 %collective-permute-start.3 = (bf16[768,1280]{1,0:T(8,128)(2,1)}, bf16[768,1280]{1,0:T(8,128)(2,1)S(1)}, u32[]{:S(2)}, u32[]{:S(2)}) collective-permute-start(bf16[768,1280]{1,0:T(8,128)(2,1)} %refs_3_.3), channel_id=1, source_target_pairs={{0,1},{1,0},{2,3},{3,2},{4,5},{5,4},{6,7},{7,6},{8,9},{9,8},{10,11... | collective-permute-start | bytes 5898248 | tf_op jit(solution)/shard_map/ppermute | solution.py:396
  4.9 11.1 %all-to-all-start = ((f32[8,2,1280]{2,1,0:T(2,128)}), f32[8,2,1280]{2,1,0:T(2,128)S(1)}, u32[]{:S(2)}, u32[]{:S(2)}) async-start(f32[8,2,1280]{2,1,0:T(2,128)} %shard_map.68), calls=%async_computation | async-start | bytes 163840 | tf_op jit(solution)/shard_map/all_to_all | solution.py:405
  24.2 20.3 %collective-permute-start.1 = (bf16[80,2560]{1,0:T(8,128)(2,1)S(1)}, bf16[80,2560]{1,0:T(8,128)(2,1)S(1)}, u32[]{:S(2)}, u32[]{:S(2)}) collective-permute-start(bf16[80,2560]{1,0:T(8,128)(2,1)S(1)} %get-tuple-element.17.refs_1_), channel_id=1, source_target_pairs={{0,8},{8,16},{16,24},{24,32},{32,40},{40,48},{48,56},{56,64},{64,7... | collective-permute-start | bytes 1228808 | tf_op jit(solution)/shard_map/ppermute | solution.py:431
  25.8 18.8 %collective-permute-start.2 = (bf16[80,2560]{1,0:T(8,128)(2,1)S(1)}, bf16[80,2560]{1,0:T(8,128)(2,1)S(1)}, u32[]{:S(2)}, u32[]{:S(2)}) collective-permute-start(bf16[80,2560]{1,0:T(8,128)(2,1)S(1)} %get-tuple-element.17.refs_1_), channel_id=1, source_target_pairs={{8,0},{16,8},{24,16},{32,24},{40,32},{48,40},{56,48},{64,56},{72,6... | collective-permute-start | bytes 1228808 | tf_op jit(solution)/shard_map/ppermute | solution.py:432
  29.7 13.1 %copy-start = (bf16[768,1280]{1,0:T(8,128)(2,1)S(1)}, bf16[768,1280]{1,0:T(8,128)(2,1)}, u32[]{:S(2)}) copy-start(bf16[768,1280]{1,0:T(8,128)(2,1)} %refs_3_.3) | copy-start | bytes 5898244
  37.3 12.4 %collective-permute-start.7 = (bf16[64,2560]{1,0:T(8,128)(2,1)S(1)}, bf16[64,2560]{1,0:T(8,128)(2,1)S(1)}, u32[]{:S(2)}, u32[]{:S(2)}) collective-permute-start(bf16[64,2560]{1,0:T(8,128)(2,1)S(1)} %shard_map.73.refs_1_), channel_id=1, source_target_pairs={{0,8},{8,16},{16,24},{24,32},{32,40},{40,48},{48,56},{56,64},{64,7... | collective-permute-start | bytes 983048 | tf_op jit(solution)/shard_map/ppermute | solution.py:431
  37.4 12.3 %collective-permute-start.8 = (bf16[64,2560]{1,0:T(8,128)(2,1)S(1)}, bf16[64,2560]{1,0:T(8,128)(2,1)S(1)}, u32[]{:S(2)}, u32[]{:S(2)}) collective-permute-start(bf16[64,2560]{1,0:T(8,128)(2,1)S(1)} %shard_map.73.refs_1_), channel_id=1, source_target_pairs={{8,0},{16,8},{24,16},{32,24},{40,32},{48,40},{56,48},{64,56},{72,6... | collective-permute-start | bytes 983048 | tf_op jit(solution)/shard_map/ppermute | solution.py:432
  46.0 9.1 %collective-permute-start.4 = (s16[64,896]{1,0:T(8,128)(2,1)S(1)}, s16[64,896]{1,0:T(8,128)(2,1)S(1)}, u32[]{:S(2)}, u32[]{:S(2)}) collective-permute-start(s16[64,896]{1,0:T(8,128)(2,1)S(1)} %get-tuple-element.20), channel_id=1, source_target_pairs={{0,2},{2,4},{4,6},{6,0},{1,3},{3,5},{5,7},{7,1},{8,10},{10,12},{12... | collective-permute-start | bytes 344072 | tf_op jit(solution)/shard_map/ppermute | solution.py:445
  46.7 9.3 %collective-permute-start.5 = (s16[64,896]{1,0:T(8,128)(2,1)S(1)}, s16[64,896]{1,0:T(8,128)(2,1)S(1)}, u32[]{:S(2)}, u32[]{:S(2)}) collective-permute-start(s16[64,896]{1,0:T(8,128)(2,1)S(1)} %get-tuple-element.21), channel_id=1, source_target_pairs={{0,4},{2,6},{4,0},{6,2},{1,5},{3,7},{5,1},{7,3},{8,12},{10,14},{12... | collective-permute-start | bytes 344072 | tf_op jit(solution)/shard_map/ppermute | solution.py:445
  48.7 7.3 %collective-permute-start.6 = (s16[64,896]{1,0:T(8,128)(2,1)S(1)}, s16[64,896]{1,0:T(8,128)(2,1)S(1)}, u32[]{:S(2)}, u32[]{:S(2)}) collective-permute-start(s16[64,896]{1,0:T(8,128)(2,1)S(1)} %get-tuple-element.22), channel_id=1, source_target_pairs={{0,6},{2,0},{4,2},{6,4},{1,7},{3,1},{5,3},{7,5},{8,14},{10,8},{12,... | collective-permute-start | bytes 344072 | tf_op jit(solution)/shard_map/ppermute | solution.py:445
  51.3 6.2 %collective-permute-start.10 = (s16[48,896]{1,0:T(8,128)(2,1)S(1)}, s16[48,896]{1,0:T(8,128)(2,1)S(1)}, u32[]{:S(2)}, u32[]{:S(2)}) collective-permute-start(s16[48,896]{1,0:T(8,128)(2,1)S(1)} %get-tuple-element.28), channel_id=1, source_target_pairs={{0,4},{2,6},{4,0},{6,2},{1,5},{3,7},{5,1},{7,3},{8,12},{10,14},{12... | collective-permute-start | bytes 258056 | tf_op jit(solution)/shard_map/ppermute | solution.py:445
  54.0 4.5 %collective-permute-start.11 = (s16[48,896]{1,0:T(8,128)(2,1)S(1)}, s16[48,896]{1,0:T(8,128)(2,1)S(1)}, u32[]{:S(2)}, u32[]{:S(2)}) collective-permute-start(s16[48,896]{1,0:T(8,128)(2,1)S(1)} %get-tuple-element.29), channel_id=1, source_target_pairs={{0,6},{2,0},{4,2},{6,4},{1,7},{3,1},{5,3},{7,5},{8,14},{10,8},{12,... | collective-permute-start | bytes 258056 | tf_op jit(solution)/shard_map/ppermute | solution.py:445
  55.1 5.7 %collective-permute-start.9 = (s16[48,896]{1,0:T(8,128)(2,1)S(1)}, s16[48,896]{1,0:T(8,128)(2,1)S(1)}, u32[]{:S(2)}, u32[]{:S(2)}) collective-permute-start(s16[48,896]{1,0:T(8,128)(2,1)S(1)} %get-tuple-element.27), channel_id=1, source_target_pairs={{0,2},{2,4},{4,6},{6,0},{1,3},{3,5},{5,7},{7,1},{8,10},{10,12},{12... | collective-permute-start | bytes 258056 | tf_op jit(solution)/shard_map/ppermute | solution.py:445
  60.8 16.8 %copy-start.3 = (s32[32]{0:T(128)S(1)}, s32[32]{0:T(128)}, u32[]{:S(2)}) copy-start(s32[32]{0:T(128)} %order.1) | copy-start | bytes 388

commit v7 on v6

--- a/solution.py
+++ b/solution.py
@@ -76,28 +76,17 @@
     )[:1]
 
 
-def copies_kernel(expression, out, done):
-    copies = [
-        pltpu.make_async_copy(expression, out.at[d], done.at[d]) for d in range(out.shape[0])
-    ]
-    for copy in copies:
-        copy.start()
-    for copy in copies:
-        copy.wait()
-
-
-def moments_kernel(dosage, theirs, out, sums):
+def moments_kernel(dosage, out, sums):
     variants, width = dosage.shape
 
     def step(i, carry):
         rows = pl.ds(pl.multiple_of(i * LANES, LANES), LANES)
         total = jnp.zeros((LANES, LANES), jnp.float32)
         square = jnp.zeros((LANES, LANES), jnp.float32)
-        for source in (dosage, theirs):
-            for k in range(width // LANES):
-                v = source[rows, k * LANES : (k + 1) * LANES].astype(jnp.float32)
-                total = total + v
-                square = square + v * v
+        for k in range(width // LANES):
+            v = dosage[rows, k * LANES : (k + 1) * LANES].astype(jnp.float32)
+            total = total + v
+            square = square + v * v
         sums[0, rows, :] = total
         sums[1, rows, :] = square
         return carry
@@ -127,16 +116,19 @@
                     jnp.bfloat16
                 )
         direct.append((own[j : j + 1] - mean) * scale)
-    row = lax.broadcasted_iota(jnp.int32, (TILE, 2 * width), 0)
-    lane = lax.broadcasted_iota(jnp.int32, (TILE, 2 * width), 1)
-    extra = jnp.where(row == 0, direct[0], jnp.where(row == 1, direct[1], 0.0))
-    for j in range(genes):
-        for b in range(2):
-            w = windows[j, b]
-            digits = ((w >> 7).astype(jnp.float32), (w & 127).astype(jnp.float32))
-            for d in range(2):
-                extra = jnp.where((row == 2 + d) & (lane == j * 2 + b), digits[d], extra)
-    out[4 * TILE : 5 * TILE, :] = extra.astype(jnp.bfloat16)
+    tiles = 2 * width // LANES
+    lines = [direct[j][:, t * LANES : (t + 1) * LANES] for j in range(genes) for t in range(tiles)]
+    lane = lax.broadcasted_iota(jnp.int32, (1, LANES), 1)
+    for d in range(2):
+        line = jnp.zeros((1, LANES), jnp.float32)
+        for j in range(genes):
+            for b in range(2):
+                w = windows[j, b]
+                digit = (w & 127) if d else (w >> 7)
+                line = jnp.where(lane == j * 2 + b, digit.astype(jnp.float32), line)
+        lines.append(line)
+    lines.append(jnp.zeros((4 * TILE - len(lines), LANES), jnp.float32))
+    out[:, 2 * width :] = jnp.concatenate(lines, axis=0).astype(jnp.bfloat16)
     look_up(0, (0, 1), place, perms, theirs, table, out)
 
 
@@ -185,11 +177,20 @@
 
 def sums_kernel(chunk, *refs):
     blocks = refs[:3]
-    dosage, theirs, stat, own, m1, m2, m3 = refs[3:10]
+    dosage, theirs, stat, their_stat, own, m1, m2, m3 = refs[3:11]
     variants, width = dosage.shape
-    rows = jnp.concatenate([block[: 4 * TILE, :] for block in blocks], axis=0)
+    stat = stat[...] + their_stat[...]
+    rows = jnp.concatenate([block[:, : 2 * width] for block in blocks], axis=0)
     if chunk == 0:
-        rows = jnp.concatenate([rows] + [block[4 * TILE :, :] for block in blocks], axis=0)
+        tiles = 2 * width // LANES
+        extra = [block[:, 2 * width :].astype(jnp.float32) for block in blocks]
+        direct = [
+            jnp.concatenate([e[j * tiles + t : j * tiles + t + 1] for t in range(tiles)], axis=1)
+            for e in extra
+            for j in range(2)
+        ]
+        direct.append(jnp.zeros((TILE - 6, 2 * width), jnp.float32))
+        rows = jnp.concatenate([rows, jnp.concatenate(direct, axis=0).astype(jnp.bfloat16)], axis=0)
     both = times(rows[:, :width], dosage[...]) + times(rows[:, width:], theirs[...])
     column = jnp.sum(rows.astype(jnp.float32), axis=1, keepdims=True)
     mean, size = mean_and_size(stat[0:1, :], stat[1:2, :], 2.0 * width)
@@ -218,10 +219,9 @@
             message[t * TILE : (t + 1) * TILE, :variants] = to_int16(coded(values, code))
             message[t * TILE : (t + 1) * TILE, variants:] = beside(code, columns)
     if chunk == 0:
-        spots = [slice((12 + o) * TILE, (12 + o) * TILE + 2) for o in range(3)]
-        gather = lambda x: jnp.concatenate([x[p] for p in spots] + [jnp.zeros_like(x[:2])], axis=0)
-        own[48:56, :] = gather(both)
-        values, columns = gather(got), gather(column)
+        spots = slice(12 * TILE, 12 * TILE + HALF)
+        own[48:56, :] = both[spots]
+        values, columns = got[spots], column[spots]
         code = bound_code(jnp.max(jnp.abs(values), keepdims=True))
         rest = list(digits(stat[0:1, :]) + digits(stat[1:2, :]))
         rest.append(jnp.zeros((2, variants), jnp.float32))
@@ -232,9 +232,8 @@
             message[48:64, variants:] = side
         info = refs[-1]
         info[...] = jnp.zeros_like(info)
-        for o, block in enumerate(blocks):
-            e = block[4 * TILE :, :LANES].astype(jnp.float32)
-            info[o : o + 1, :] = e[2:3] * 128.0 + e[3:4]
+        for o, e in enumerate(extra):
+            info[o : o + 1, :] = e[2 * tiles : 2 * tiles + 1] * 128.0 + e[2 * tiles + 1 : 2 * tiles + 2]
 
 
 def added(own, messages, means, sizes):
@@ -268,9 +267,10 @@
     return tile
 
 
-def early_kernel(samples, place, info, stat, own, m1, m2, m3, out, aux):
+def early_kernel(samples, place, info, stat, their_stat, own, m1, m2, m3, out, aux):
     variants = own.shape[1]
     count = samples / 4.0
+    stat = stat[...] + their_stat[...]
     total, square = stat[0:1, :], stat[1:2, :]
     means, sizes = [], []
     for message in (m1, m2, m3):
@@ -391,30 +391,24 @@
     samples = width * shards
     g, z, c = lax.axis_index("gene"), lax.axis_index("z"), lax.axis_index("core")
     place = jnp.stack([g, z, c]).astype(jnp.int32)
+    copies = jnp.broadcast_to(expression.T[None], (shards, 2, width))
+    every = lax.all_to_all(copies, ("z", "core"), 0, 0, tiled=True)
     mates = [(0, 1), (1, 0)]
     their_perms = lax.ppermute(perms, "core", mates)
     theirs = lax.ppermute(dosage, "core", mates)
-    copies = call(
-        copies_kernel,
-        pltpu.HBM((shards, 2, width), jnp.float32),
-        [expression.T],
-        1,
-        [pltpu.SemaphoreType.DMA((shards,))],
-        remote=(0,),
-    )
-    every = lax.all_to_all(copies, ("z", "core"), 0, 0, tiled=True)
     stat = call(
         moments_kernel,
         shape((8, variants)),
-        [dosage, theirs],
+        [dosage],
         2,
         [pltpu.VMEM((2, variants, LANES), jnp.float32)],
     )
+    their_stat = lax.ppermute(stat, "core", mates)
 
     table_shape = shape((2, samples // LANES, TILE, LANES), jnp.bfloat16)
     first, table = call(
         first_kernel,
-        [shape((5 * TILE, 2 * width), jnp.bfloat16), table_shape],
+        [shape((4 * TILE, 2 * width + LANES), jnp.bfloat16), table_shape],
         [place, windows, every, perms, their_perms],
         9,
     )
@@ -435,7 +429,7 @@
         own, *parts = call(
             functools.partial(sums_kernel, h),
             outs + ([shape((8, LANES))] if h == 0 else []),
-            [left, own, right, dosage, theirs, stat],
+            [left, own, right, dosage, theirs, stat, their_stat],
             2,
         )
         if h == 0:
@@ -447,7 +441,7 @@
     tile, aux = call(
         functools.partial(early_kernel, samples),
         [shape((HALF, LANES)), shape((8, variants))],
-        [place, info, stat, *sums[0]],
+        [place, info, stat, their_stat, *sums[0]],
         1,
     )
     everyone = owners * shards

time: 79.5 us -> 77.2 us (0.971)
  Pallas kernels: 27.7 us -> 23.4 us
  waiting for transfers between devices: 9.55 us -> 5.94 us
  local copies, waits for them, and re-layouts: 0.02 us -> 2.91 us
  blocking collectives: 15.8 us -> 18.5 us
    pallas_call x9 -> x8, Pallas kernels: 27.7 us -> 23.4 us  [call(): return made(*args)]
    all_to_all x1, waiting for transfers between devices: 5.63 us -> 2.3 us  [on_device(): every = lax.all_to_all(copies, ('z', 'core'), 0, 0, tiled=True)]
    all_to_all x1, blocking collectives: 15.8 us -> 18.5 us  [on_device(): lax.all_to_all(lines.reshape(everyone, 1, LANES), ('gene', 'z', 'core'),...]
    ppermute x6, waiting for transfers between devices: 3.9 us -> 2.25 us  [on_device(): lax.ppermute(parts[k - 1], 'z', [(i, (i + k) % 4) for i in range(4)])]
    unnamed x8 -> x10, local copies, waits for them, and re-layouts: 0.02 us -> 1.56 us
    ppermute x2, waiting for transfers between devices: 0.01 us -> 1.38 us  [on_device(): left = lax.ppermute(own, 'gene', ahead)]
    broadcast_in_dim x0 -> x1, local copies, waits for them, and re-layouts: none -> 1.35 us  [on_device(): copies = jnp.broadcast_to(expression.T[None], (shards, 2, width))]
  transfers between devices with their start and end apart: 13 -> 14, of which waited for: 5 -> 5; matrix products, arithmetic and copies ran while one was open for 0% -> 2% of each run, Pallas kernels for 32% -> 27%
where the time goes in v7:
time: 77.2 us; the launch traced here: 76.7 us
  starting transfers between devices  25.2 us (33%)
  Pallas kernels  23.4 us (30%)
  blocking collectives  18.5 us (24%)
  waiting for transfers between devices  5.94 us (8%)
  local copies, waits for them, and re-layouts  2.91 us (4%)
    pallas_call x8, Pallas kernels, call(): return made(*args)  23.4 us
    all_to_all x1, blocking collectives, on_device(): lax.all_to_all(lines.reshape(everyone, 1, LANES), ('gene', 'z', 'core'),...  18.5 us
    ppermute x2, starting transfers between devices, on_device(): right = lax.ppermute(own, 'gene', back)  9.18 us
    ppermute x6, starting transfers between devices, on_device(): lax.ppermute(parts[k - 1], 'z', [(i, (i + k) % 4) for i in range(4)])  8.28 us
    all_to_all x1, starting transfers between devices, on_device(): every = lax.all_to_all(copies, ('z', 'core'), 0, 0, tiled=True)  5.52 us
    all_to_all x1, waiting for transfers between devices, on_device(): every = lax.all_to_all(copies, ('z', 'core'), 0, 0, tiled=True)  2.3 us
    ppermute x6, waiting for transfers between devices, on_device(): lax.ppermute(parts[k - 1], 'z', [(i, (i + k) % 4) for i in range(4)])  2.25 us
    ppermute x2, starting transfers between devices, on_device(): left = lax.ppermute(own, 'gene', ahead)  1.63 us
  transfers between devices with their start and end apart: 14, of which 5 were waited for; matrix products, arithmetic and copies ran while one was open for 2% of the time, Pallas kernels for 27%

profile of v7, /device:TPU:0, one launch (start us, length us, event | category | flops | bytes accessed | tf_op | source)
XLA Modules:
  0.0 76.7 jit_solution(674143446697341461)
XLA Ops:
  0.6 0.1 collective-permute-start
  0.7 1.3 %broadcast_in_dim.2 = f32[8,2,1280]{2,1,0:T(2,128)} broadcast(f32[2,1280]{1,0:T(2,128)} %bitcast.11), dimensions={1,2} | broadcast | bytes 92160 | tf_op jit(solution)/shard_map/broadcast_in_dim | solution.py:394
  2.1 5.5 %all-to-all-start = ((f32[8,2,1280]{2,1,0:T(2,128)}), f32[8,2,1280]{2,1,0:T(2,128)S(1)}, u32[]{:S(2)}, u32[]{:S(2)}) async-start(f32[8,2,1280]{2,1,0:T(2,128)} %broadcast_in_dim.2), calls=%async_computation | async-start | bytes 163840 | tf_op jit(solution)/shard_map/all_to_all | solution.py:395
  7.6 0.5 collective-permute-start.3
  8.1 0.0 copy-start
  8.1 1.5 %copy-done = bf16[768,1280]{1,0:T(8,128)(2,1)S(1)} copy-done((bf16[768,1280]{1,0:T(8,128)(2,1)S(1)}, bf16[768,1280]{1,0:T(8,128)(2,1)}, u32[]{:S(2)}) %copy-start) | copy-done | bytes 1966104
  9.6 0.0 copy-start.2
  9.6 0.0 copy-start.3
  9.7 1.3 %shard_map.69.refs_5_.stat = f32[8,768]{1,0:T(8,128)S(1)} custom-call(bf16[768,1280]{1,0:T(8,128)(2,1)S(1)} %copy-done), custom_call_target="tpu_custom_call" | custom-call | flops 2000000000 | tf_op jit(solution)/shard_map/pallas_call | solution.py:380
  10.9 0.0 collective-permute-start.4
  10.9 0.1 pad_add_fusion.place
  11.0 2.3 %all-to-all-done.every = f32[8,2,1280]{2,1,0:T(2,128)S(1)} async-done(((f32[8,2,1280]{2,1,0:T(2,128)}), f32[8,2,1280]{2,1,0:T(2,128)S(1)}, u32[]{:S(2)}, u32[]{:S(2)}) %all-to-all-start) | async-done | bytes 81952 | tf_op jit(solution)/shard_map/all_to_all | solution.py:395
  13.3 0.0 collective-permute-done.theirs
  13.3 0.0 copy-done.2
  13.3 0.0 copy-done.3
  13.3 8.0 %shard_map.68 = (bf16[64,2688]{1,0:T(8,128)(2,1)S(1)}, bf16[2,80,16,128]{3,2,1,0:T(8,128)(2,1)S(1)}) custom-call(s32[3]{0:T(128)S(1)} %pad_add_fusion.place, s32[2,2]{1,0:T(2,128)S(1)} %copy-done.3, f32[8,2,1280]{2,1,0:T(2,128)S(1)} %all-to-all-done.every, s32[128,1280]{1,0:T(8,128)S(1)} %copy-done.2, s32[128,1280]{1,0:T(8,128)S(1)} %collective-permute-done.theirs), custom_call_target="tpu_custom_call" | custom-call | flops 8999999488 | tf_op jit(solution)/shard_map/pallas_call | solution.py:380
  21.4 1.6 %collective-permute-start.1 = (bf16[64,2688]{1,0:T(8,128)(2,1)S(1)}, bf16[64,2688]{1,0:T(8,128)(2,1)S(1)}, u32[]{:S(2)}, u32[]{:S(2)}) collective-permute-start(bf16[64,2688]{1,0:T(8,128)(2,1)S(1)} %get-tuple-element.17.refs_1_), channel_id=1, source_target_pairs={{0,8},{8,16},{16,24},{24,32},{32,40},{40,48},{48,56},{56,64},{64,7... | collective-permute-start | bytes 1032200 | tf_op jit(solution)/shard_map/ppermute | solution.py:425
  22.9 3.9 %collective-permute-start.2 = (bf16[64,2688]{1,0:T(8,128)(2,1)S(1)}, bf16[64,2688]{1,0:T(8,128)(2,1)S(1)}, u32[]{:S(2)}, u32[]{:S(2)}) collective-permute-start(bf16[64,2688]{1,0:T(8,128)(2,1)S(1)} %get-tuple-element.17.refs_1_), channel_id=1, source_target_pairs={{8,0},{16,8},{24,16},{32,24},{40,32},{48,40},{56,48},{64,56},{72,6... | collective-permute-start | bytes 1032200 | tf_op jit(solution)/shard_map/ppermute | solution.py:426
  26.8 0.0 copy-start.1
  26.8 7.6 %shard_map.72.refs_1_ = bf16[64,2560]{1,0:T(8,128)(2,1)S(1)} custom-call(s32[3]{0:T(128)S(1)} %pad_add_fusion.place, s32[128,1280]{1,0:T(8,128)S(1)} %copy-done.2, s32[128,1280]{1,0:T(8,128)S(1)} %collective-permute-done.theirs, bf16[2,80,16,128]{3,2,1,0:T(8,128)(2,1)S(1)} %get-tuple-element.25.table), custom_call_target="tpu_custom_call" | custom-call | flops 8000000000 | tf_op jit(solution)/shard_map/pallas_call | solution.py:380
  34.3 0.1 collective-permute-start.8
  34.4 0.0 collective-permute-done.4.refs_6_.their_stat
  34.4 5.3 %collective-permute-start.9 = (bf16[64,2560]{1,0:T(8,128)(2,1)S(1)}, bf16[64,2560]{1,0:T(8,128)(2,1)S(1)}, u32[]{:S(2)}, u32[]{:S(2)}) collective-permute-start(bf16[64,2560]{1,0:T(8,128)(2,1)S(1)} %shard_map.72.refs_1_), channel_id=1, source_target_pairs={{8,0},{16,8},{24,16},{32,24},{40,32},{48,40},{56,48},{64,56},{72,6... | collective-permute-start | bytes 983048 | tf_op jit(solution)/shard_map/ppermute | solution.py:426
  39.7 0.0 collective-permute-done.1.refs_0_
  39.7 0.0 collective-permute-done.2.refs_2_
  39.8 0.0 collective-permute-done.3.refs_4_
  39.8 0.0 copy-done.1
  39.8 1.6 %shard_map.70 = (f32[56,768]{1,0:T(8,128)S(1)}, s16[64,896]{1,0:T(8,128)(2,1)S(1)}, s16[64,896]{1,0:T(8,128)(2,1)S(1)}, s16[64,896]{1,0:T(8,128)(2,1)S(1)}, f32[8,128]{1,0:T(8,128)S(1)}) custom-call(bf16[64,2688]{1,0:T(8,128)(2,1)S(1)} %collective-permute-done.1.refs_0_, bf16[64,2688]{1,0:T(8,128)(2,1)S(1)} %get-tuple-element.17.refs_1_, ...), custom_call_target="tpu_custom_call" | custom-call | flops 2000000000 | tf_op jit(solution)/shard_map/pallas_call | solution.py:380
  41.4 0.7 collective-permute-start.5
  42.0 2.0 %collective-permute-start.6 = (s16[64,896]{1,0:T(8,128)(2,1)S(1)}, s16[64,896]{1,0:T(8,128)(2,1)S(1)}, u32[]{:S(2)}, u32[]{:S(2)}) collective-permute-start(s16[64,896]{1,0:T(8,128)(2,1)S(1)} %get-tuple-element.21), channel_id=1, source_target_pairs={{0,4},{2,6},{4,0},{6,2},{1,5},{3,7},{5,1},{7,3},{8,12},{10,14},{12... | collective-permute-start | bytes 344072 | tf_op jit(solution)/shard_map/ppermute | solution.py:439
  44.1 1.2 %collective-permute-start.7 = (s16[64,896]{1,0:T(8,128)(2,1)S(1)}, s16[64,896]{1,0:T(8,128)(2,1)S(1)}, u32[]{:S(2)}, u32[]{:S(2)}) collective-permute-start(s16[64,896]{1,0:T(8,128)(2,1)S(1)} %get-tuple-element.22), channel_id=1, source_target_pairs={{0,6},{2,0},{4,2},{6,4},{1,7},{3,1},{5,3},{7,5},{8,14},{10,8},{12,... | collective-permute-start | bytes 344072 | tf_op jit(solution)/shard_map/ppermute | solution.py:439
  45.3 1.4 %collective-permute-done.8.refs_0_ = bf16[64,2560]{1,0:T(8,128)(2,1)S(1)} collective-permute-done((bf16[64,2560]{1,0:T(8,128)(2,1)S(1)}, bf16[64,2560]{1,0:T(8,128)(2,1)S(1)}, u32[]{:S(2)}, u32[]{:S(2)}) %collective-permute-start.8) | collective-permute-done | bytes 327712 | tf_op jit(solution)/shard_map/ppermute | solution.py:425
  46.7 0.0 collective-permute-done.9.refs_2_
  46.7 1.6 %shard_map.73 = (f32[48,768]{1,0:T(8,128)S(1)}, s16[48,896]{1,0:T(8,128)(2,1)S(1)}, s16[48,896]{1,0:T(8,128)(2,1)S(1)}, s16[48,896]{1,0:T(8,128)(2,1)S(1)}) custom-call(bf16[64,2560]{1,0:T(8,128)(2,1)S(1)} %collective-permute-done.8.refs_0_, bf16[64,2560]{1,0:T(8,128)(2,1)S(1)} %shard_map.72.refs_1_, bf16[64,2560]{1,0:T(8,128)(2,1)S(1)} %collective-permute-done.9.refs_2_, ...), custom_call_target="tpu_custom_call" | custom-call | flops 2000000000 | tf_op jit(solution)/shard_map/pallas_call | solution.py:380
  48.3 0.6 collective-permute-start.10
  49.0 2.2 %collective-permute-start.11 = (s16[48,896]{1,0:T(8,128)(2,1)S(1)}, s16[48,896]{1,0:T(8,128)(2,1)S(1)}, u32[]{:S(2)}, u32[]{:S(2)}) collective-permute-start(s16[48,896]{1,0:T(8,128)(2,1)S(1)} %get-tuple-element.28), channel_id=1, source_target_pairs={{0,4},{2,6},{4,0},{6,2},{1,5},{3,7},{5,1},{7,3},{8,12},{10,14},{12... | collective-permute-start | bytes 258056 | tf_op jit(solution)/shard_map/ppermute | solution.py:439
  51.2 0.0 collective-permute-done.5.m1
  51.2 1.5 %collective-permute-start.12 = (s16[48,896]{1,0:T(8,128)(2,1)S(1)}, s16[48,896]{1,0:T(8,128)(2,1)S(1)}, u32[]{:S(2)}, u32[]{:S(2)}) collective-permute-start(s16[48,896]{1,0:T(8,128)(2,1)S(1)} %get-tuple-element.29), channel_id=1, source_target_pairs={{0,6},{2,0},{4,2},{6,4},{1,7},{3,1},{5,3},{7,5},{8,14},{10,8},{12,... | collective-permute-start | bytes 258056 | tf_op jit(solution)/shard_map/ppermute | solution.py:439
  52.7 0.0 collective-permute-done.6.m2
  52.7 0.0 collective-permute-done.7.m3
  52.7 1.0 %shard_map.71 = (f32[8,128]{1,0:T(8,128)S(1)}, f32[8,768]{1,0:T(8,128)S(1)}) custom-call(s32[3]{0:T(128)S(1)} %pad_add_fusion.place, f32[8,128]{1,0:T(8,128)S(1)} %get-tuple-element.18.info, f32[8,768]{1,0:T(8,128)S(1)} %shard_map.69.refs_5_.stat, f32[8,768]{1,0:T(8,128)S(1)} %collective-permute-done.4.refs_6_.their_stat, ...), custom_call_target="tpu_custom_call" | custom-call | flops 1000000000 | tf_op jit(solution)/shard_map/pallas_call | solution.py:380
  53.6 0.5 collective-permute-done.10.m1
  54.1 0.9 %collective-permute-done.11.m2 = s16[48,896]{1,0:T(8,128)(2,1)S(1)} collective-permute-done((s16[48,896]{1,0:T(8,128)(2,1)S(1)}, s16[48,896]{1,0:T(8,128)(2,1)S(1)}, u32[]{:S(2)}, u32[]{:S(2)}) %collective-permute-start.11) | collective-permute-done | bytes 86048 | tf_op jit(solution)/shard_map/ppermute | solution.py:439
  55.0 0.9 %collective-permute-done.12.m3 = s16[48,896]{1,0:T(8,128)(2,1)S(1)} collective-permute-done((s16[48,896]{1,0:T(8,128)(2,1)S(1)}, s16[48,896]{1,0:T(8,128)(2,1)S(1)}, u32[]{:S(2)}, u32[]{:S(2)}) %collective-permute-start.12) | collective-permute-done | bytes 86048 | tf_op jit(solution)/shard_map/ppermute | solution.py:439
  55.9 0.0 copy-start.4
  55.9 0.9 %shard_map.74 = f32[128,128]{1,0:T(8,128)S(1)} custom-call(s32[3]{0:T(128)S(1)} %pad_add_fusion.place, f32[8,128]{1,0:T(8,128)S(1)} %get-tuple-element.18.info, f32[8,768]{1,0:T(8,128)S(1)} %get-tuple-element.23.aux, f32[8,128]{1,0:T(8,128)S(1)} %get-tuple-element.24.tile, f32[48,768]{1,0:T(8,128)S(1)} %get-tuple-element.26.own, ...), custom_call_target="tpu_custom_call" | custom-call | flops 2000000000 | tf_op jit(solution)/shard_map/pallas_call | solution.py:380
  56.8 18.5 %all_to_all.10 = f32[128,1,128]{2,1,0:T(1,128)S(1)} all-to-all(f32[128,1,128]{2,1,0:T(1,128)S(1)} %bitcast.9), channel_id=1, replica_groups=mesh['gene'=16,'z'=4,'core'=2] {'gene','z','core'}, dimensions={0} | all-to-all | bytes 131072 | tf_op jit(solution)/shard_map/all_to_all | solution.py:449
  75.3 0.0 copy-done.4
  75.3 1.5 %shard_map.75 = (f32[2,128]{1,0:T(2,128)}, f32[1,2]{1,0:T(1,128)}) custom-call(s32[3]{0:T(128)S(1)} %pad_add_fusion.place, s32[32]{0:T(128)S(1)} %copy-done.4, f32[128,128]{1,0:T(8,128)S(1)} %bitcast.10), custom_call_target="tpu_custom_call" | custom-call | flops 2000000000 | tf_op jit(solution)/shard_map/pallas_call | solution.py:380
Async XLA Ops:
  0.6 12.7 %collective-permute-start = (s32[128,1280]{1,0:T(8,128)}, s32[128,1280]{1,0:T(8,128)S(1)}, u32[]{:S(2)}, u32[]{:S(2)}) collective-permute-start(s32[128,1280]{1,0:T(8,128)} %perms.3), channel_id=1, source_target_pairs={{0,1},{1,0},{2,3},{3,2},{4,5},{5,4},{6,7},{7,6},{8,9},{9,8},{10,11... | collective-permute-start | bytes 1966088 | tf_op jit(solution)/shard_map/ppermute | solution.py:397
  2.1 11.2 %all-to-all-start = ((f32[8,2,1280]{2,1,0:T(2,128)}), f32[8,2,1280]{2,1,0:T(2,128)S(1)}, u32[]{:S(2)}, u32[]{:S(2)}) async-start(f32[8,2,1280]{2,1,0:T(2,128)} %broadcast_in_dim.2), calls=%async_computation | async-start | bytes 163840 | tf_op jit(solution)/shard_map/all_to_all | solution.py:395
  7.6 32.2 %collective-permute-start.3 = (bf16[768,1280]{1,0:T(8,128)(2,1)}, bf16[768,1280]{1,0:T(8,128)(2,1)S(1)}, u32[]{:S(2)}, u32[]{:S(2)}) collective-permute-start(bf16[768,1280]{1,0:T(8,128)(2,1)} %refs_3_.3), channel_id=1, source_target_pairs={{0,1},{1,0},{2,3},{3,2},{4,5},{5,4},{6,7},{7,6},{8,9},{9,8},{10,11... | collective-permute-start | bytes 5898248 | tf_op jit(solution)/shard_map/ppermute | solution.py:398
  8.1 1.5 %copy-start = (bf16[768,1280]{1,0:T(8,128)(2,1)S(1)}, bf16[768,1280]{1,0:T(8,128)(2,1)}, u32[]{:S(2)}) copy-start(bf16[768,1280]{1,0:T(8,128)(2,1)} %refs_3_.3) | copy-start | bytes 5898244
  9.6 3.7 %copy-start.2 = (s32[128,1280]{1,0:T(8,128)S(1)}, s32[128,1280]{1,0:T(8,128)}, u32[]{:S(2)}) copy-start(s32[128,1280]{1,0:T(8,128)} %perms.3) | copy-start | bytes 1966084
  9.6 3.7 %copy-start.3 = (s32[2,2]{1,0:T(2,128)S(1)}, s32[2,2]{1,0:T(2,128)}, u32[]{:S(2)}) copy-start(s32[2,2]{1,0:T(2,128)} %windows.1) | copy-start | bytes 52
  10.9 23.5 %collective-permute-start.4 = (f32[8,768]{1,0:T(8,128)S(1)}, f32[8,768]{1,0:T(8,128)S(1)}, u32[]{:S(2)}, u32[]{:S(2)}) collective-permute-start(f32[8,768]{1,0:T(8,128)S(1)} %shard_map.69.refs_5_.stat), channel_id=1, source_target_pairs={{0,1},{1,0},{2,3},{3,2},{4,5},{5,4},{6,7},{7,6},{8,9},{9,8},{10,11... | collective-permute-start | bytes 73736 | tf_op jit(solution)/shard_map/ppermute | solution.py:406
  21.4 18.4 %collective-permute-start.1 = (bf16[64,2688]{1,0:T(8,128)(2,1)S(1)}, bf16[64,2688]{1,0:T(8,128)(2,1)S(1)}, u32[]{:S(2)}, u32[]{:S(2)}) collective-permute-start(bf16[64,2688]{1,0:T(8,128)(2,1)S(1)} %get-tuple-element.17.refs_1_), channel_id=1, source_target_pairs={{0,8},{8,16},{16,24},{24,32},{32,40},{40,48},{48,56},{56,64},{64,7... | collective-permute-start | bytes 1032200 | tf_op jit(solution)/shard_map/ppermute | solution.py:425
  22.9 16.8 %collective-permute-start.2 = (bf16[64,2688]{1,0:T(8,128)(2,1)S(1)}, bf16[64,2688]{1,0:T(8,128)(2,1)S(1)}, u32[]{:S(2)}, u32[]{:S(2)}) collective-permute-start(bf16[64,2688]{1,0:T(8,128)(2,1)S(1)} %get-tuple-element.17.refs_1_), channel_id=1, source_target_pairs={{8,0},{16,8},{24,16},{32,24},{40,32},{48,40},{56,48},{64,56},{72,6... | collective-permute-start | bytes 1032200 | tf_op jit(solution)/shard_map/ppermute | solution.py:426
  26.8 13.0 %copy-start.1 = (bf16[768,1280]{1,0:T(8,128)(2,1)S(1)}, bf16[768,1280]{1,0:T(8,128)(2,1)}, u32[]{:S(2)}) copy-start(bf16[768,1280]{1,0:T(8,128)(2,1)} %refs_3_.3) | copy-start | bytes 5898244
  34.3 12.4 %collective-permute-start.8 = (bf16[64,2560]{1,0:T(8,128)(2,1)S(1)}, bf16[64,2560]{1,0:T(8,128)(2,1)S(1)}, u32[]{:S(2)}, u32[]{:S(2)}) collective-permute-start(bf16[64,2560]{1,0:T(8,128)(2,1)S(1)} %shard_map.72.refs_1_), channel_id=1, source_target_pairs={{0,8},{8,16},{16,24},{24,32},{32,40},{40,48},{48,56},{56,64},{64,7... | collective-permute-start | bytes 983048 | tf_op jit(solution)/shard_map/ppermute | solution.py:425
  34.4 12.3 %collective-permute-start.9 = (bf16[64,2560]{1,0:T(8,128)(2,1)S(1)}, bf16[64,2560]{1,0:T(8,128)(2,1)S(1)}, u32[]{:S(2)}, u32[]{:S(2)}) collective-permute-start(bf16[64,2560]{1,0:T(8,128)(2,1)S(1)} %shard_map.72.refs_1_), channel_id=1, source_target_pairs={{8,0},{16,8},{24,16},{32,24},{40,32},{48,40},{56,48},{64,56},{72,6... | collective-permute-start | bytes 983048 | tf_op jit(solution)/shard_map/ppermute | solution.py:426
  41.4 9.8 %collective-permute-start.5 = (s16[64,896]{1,0:T(8,128)(2,1)S(1)}, s16[64,896]{1,0:T(8,128)(2,1)S(1)}, u32[]{:S(2)}, u32[]{:S(2)}) collective-permute-start(s16[64,896]{1,0:T(8,128)(2,1)S(1)} %get-tuple-element.20), channel_id=1, source_target_pairs={{0,2},{2,4},{4,6},{6,0},{1,3},{3,5},{5,7},{7,1},{8,10},{10,12},{12... | collective-permute-start | bytes 344072 | tf_op jit(solution)/shard_map/ppermute | solution.py:439
  42.0 10.6 %collective-permute-start.6 = (s16[64,896]{1,0:T(8,128)(2,1)S(1)}, s16[64,896]{1,0:T(8,128)(2,1)S(1)}, u32[]{:S(2)}, u32[]{:S(2)}) collective-permute-start(s16[64,896]{1,0:T(8,128)(2,1)S(1)} %get-tuple-element.21), channel_id=1, source_target_pairs={{0,4},{2,6},{4,0},{6,2},{1,5},{3,7},{5,1},{7,3},{8,12},{10,14},{12... | collective-permute-start | bytes 344072 | tf_op jit(solution)/shard_map/ppermute | solution.py:439
  44.1 8.6 %collective-permute-start.7 = (s16[64,896]{1,0:T(8,128)(2,1)S(1)}, s16[64,896]{1,0:T(8,128)(2,1)S(1)}, u32[]{:S(2)}, u32[]{:S(2)}) collective-permute-start(s16[64,896]{1,0:T(8,128)(2,1)S(1)} %get-tuple-element.22), channel_id=1, source_target_pairs={{0,6},{2,0},{4,2},{6,4},{1,7},{3,1},{5,3},{7,5},{8,14},{10,8},{12,... | collective-permute-start | bytes 344072 | tf_op jit(solution)/shard_map/ppermute | solution.py:439
  48.3 5.8 %collective-permute-start.10 = (s16[48,896]{1,0:T(8,128)(2,1)S(1)}, s16[48,896]{1,0:T(8,128)(2,1)S(1)}, u32[]{:S(2)}, u32[]{:S(2)}) collective-permute-start(s16[48,896]{1,0:T(8,128)(2,1)S(1)} %get-tuple-element.27), channel_id=1, source_target_pairs={{0,2},{2,4},{4,6},{6,0},{1,3},{3,5},{5,7},{7,1},{8,10},{10,12},{12... | collective-permute-start | bytes 258056 | tf_op jit(solution)/shard_map/ppermute | solution.py:439
  49.0 6.1 %collective-permute-start.11 = (s16[48,896]{1,0:T(8,128)(2,1)S(1)}, s16[48,896]{1,0:T(8,128)(2,1)S(1)}, u32[]{:S(2)}, u32[]{:S(2)}) collective-permute-start(s16[48,896]{1,0:T(8,128)(2,1)S(1)} %get-tuple-element.28), channel_id=1, source_target_pairs={{0,4},{2,6},{4,0},{6,2},{1,5},{3,7},{5,1},{7,3},{8,12},{10,14},{12... | collective-permute-start | bytes 258056 | tf_op jit(solution)/shard_map/ppermute | solution.py:439
  51.2 4.7 %collective-permute-start.12 = (s16[48,896]{1,0:T(8,128)(2,1)S(1)}, s16[48,896]{1,0:T(8,128)(2,1)S(1)}, u32[]{:S(2)}, u32[]{:S(2)}) collective-permute-start(s16[48,896]{1,0:T(8,128)(2,1)S(1)} %get-tuple-element.29), channel_id=1, source_target_pairs={{0,6},{2,0},{4,2},{6,4},{1,7},{3,1},{5,3},{7,5},{8,14},{10,8},{12,... | collective-permute-start | bytes 258056 | tf_op jit(solution)/shard_map/ppermute | solution.py:439
  55.9 19.4 %copy-start.4 = (s32[32]{0:T(128)S(1)}, s32[32]{0:T(128)}, u32[]{:S(2)}) copy-start(s32[32]{0:T(128)} %order.1) | copy-start | bytes 388

commit v8 on v7

--- a/solution.py
+++ b/solution.py
@@ -36,34 +36,46 @@
     )
 
 
-def look_up(chunk, genes, place, perms, theirs, table, out):
+def look_up(chunk, place, perms, theirs, table, out):
     z, c = place[1], place[2]
-    table_rows = table.shape[1]
+    genes, table_rows = table.shape[:2]
     width = perms.shape[1]
-
-    def step(pair, carry):
-        first = []
-        for k in range(2):
-            d = lax.rem(z + pair * 2 + k, 4) * 2 + c
-            first.append(pl.multiple_of(d * 2 * HALF + chunk * HALF, HALF))
-        for u in range(2 * width // LANES):
-            source = perms if u < width // LANES else theirs
-            lane = u % (width // LANES) * LANES
-            rows = [source[pl.ds(f, HALF), lane : lane + LANES] for f in first]
-            index = jnp.concatenate(rows, axis=0)
-            low = (index & (LANES - 1)).astype(jnp.int16)
-            high = (index >> 7).astype(jnp.int16)
-            found = [jnp.zeros((TILE, LANES), jnp.bfloat16) for _ in genes]
-            for r in range(table_rows):
-                here = high == jnp.int16(r)
-                for n, j in enumerate(genes):
-                    found[n] = jnp.where(here, lane_gather(table[j, r], low), found[n])
-            for n in range(len(genes)):
-                row = pl.multiple_of(n * 2 * TILE + pair * TILE, TILE)
-                out[pl.ds(row, TILE), u * LANES : (u + 1) * LANES] = found[n]
-        return carry
-
-    lax.fori_loop(0, 2, step, 0)
+    group = 5
+    steps = width // LANES // group
+    zero = jnp.zeros((TILE, LANES), jnp.bfloat16)
+    for s, source in enumerate((perms, theirs)):
+
+        def step(t, carry, s=s, source=source):
+            pair, part = t // steps, t % steps
+            first = []
+            for k in range(2):
+                d = lax.rem(z + pair * 2 + k, 4) * 2 + c
+                first.append(pl.multiple_of(d * 2 * HALF + chunk * HALF, HALF))
+            found = [zero] * genes
+            for u in range(group):
+                lane = pl.multiple_of((part * group + u) * LANES, LANES)
+                index = jnp.concatenate(
+                    [source[pl.ds(f, HALF), pl.ds(lane, LANES)] for f in first], axis=0
+                )
+                low = (index & (LANES - 1)).astype(jnp.int16)
+                high = (index >> 7).astype(jnp.int16)
+                never = high < jnp.int16(0)
+                found = [jnp.where(never, f, zero) for f in found]
+                for r in range(table_rows):
+                    here = high == jnp.int16(r)
+                    for j in range(genes):
+                        found[j] = jnp.where(here, lane_gather(table[j, r], low), found[j])
+                    if r % 16 == 0:
+                        found = [
+                            jnp.where(never, found[genes - 1 - j], found[j]) for j in range(genes)
+                        ]
+                for j in range(genes):
+                    row = pl.multiple_of(j * 2 * TILE + pair * TILE, TILE)
+                    to = pl.multiple_of(lane + s * width, LANES)
+                    out[pl.ds(row, TILE), pl.ds(to, LANES)] = found[j]
+            return carry
+
+        lax.fori_loop(0, 2 * steps, step, 0)
 
 
 def lane_sums(rows):
@@ -74,6 +86,12 @@
         precision=lax.Precision.HIGHEST,
         preferred_element_type=jnp.float32,
     )[:1]
+
+
+def fetch_kernel(source, out, done):
+    copy = pltpu.make_async_copy(source, out, done)
+    copy.start()
+    copy.wait()
 
 
 def moments_kernel(dosage, out, sums):
@@ -129,11 +147,11 @@
         lines.append(line)
     lines.append(jnp.zeros((4 * TILE - len(lines), LANES), jnp.float32))
     out[:, 2 * width :] = jnp.concatenate(lines, axis=0).astype(jnp.bfloat16)
-    look_up(0, (0, 1), place, perms, theirs, table, out)
+    look_up(0, place, perms, theirs, table, out)
 
 
 def later_kernel(chunk, place, perms, theirs, table, out):
-    look_up(chunk, (0, 1), place, perms, theirs, table, out)
+    look_up(chunk, place, perms, theirs, table, out)
 
 
 def times(rows, dosage):
@@ -362,11 +380,7 @@
             pl.BlockSpec(memory_space=pltpu.HBM) if i in remote else SM if k else VM
             for i, k in enumerate(scalar)
         ],
-        out_specs=tuple([VM] * len(outs))
-        if many
-        else pl.BlockSpec(memory_space=pltpu.HBM)
-        if remote
-        else VM,
+        out_specs=tuple([VM] * len(outs)) if many else VM,
         scratch_shapes=scratch,
         compiler_params=pltpu.CompilerParams(vmem_limit_bytes=24 << 20),
         cost_estimate=pl.CostEstimate(flops=int(us * 1e9), bytes_accessed=0, transcendentals=0),
@@ -396,6 +410,14 @@
     mates = [(0, 1), (1, 0)]
     their_perms = lax.ppermute(perms, "core", mates)
     theirs = lax.ppermute(dosage, "core", mates)
+    near_perms = call(
+        fetch_kernel,
+        shape(perms.shape, jnp.int32),
+        [perms],
+        1,
+        [pltpu.SemaphoreType.DMA],
+        remote=(0,),
+    )
     stat = call(
         moments_kernel,
         shape((8, variants)),
@@ -409,13 +431,13 @@
     first, table = call(
         first_kernel,
         [shape((4 * TILE, 2 * width + LANES), jnp.bfloat16), table_shape],
-        [place, windows, every, perms, their_perms],
+        [place, windows, every, near_perms, their_perms],
         9,
     )
     second = call(
         functools.partial(later_kernel, 1),
         shape((4 * TILE, 2 * width), jnp.bfloat16),
-        [place, perms, their_perms, table],
+        [place, near_perms, their_perms, table],
         8,
     )
     ahead = [(i, (i + 1) % owners) for i in range(owners)]

time: 77.2 us -> 79.2 us (1.026)
  waiting for transfers between devices: 5.94 us -> 3.47 us
  starting transfers between devices: 25.2 us -> 27.5 us
  Pallas kernels: 23.4 us -> 25.5 us
    ppermute x6, starting transfers between devices: 8.28 us -> 10.6 us  [on_device(): lax.ppermute(parts[k - 1], 'z', [(i, (i + k) % 4) for i in range(4)])]
    pallas_call x8 -> x9, Pallas kernels: 23.4 us -> 25.5 us  [call(): return made(*args)]
    ppermute x2, waiting for transfers between devices: 1.38 us -> 0.24 us  [on_device(): left = lax.ppermute(own, 'gene', ahead)]
    all_to_all x1, waiting for transfers between devices: 2.3 us -> 1.16 us  [on_device(): every = lax.all_to_all(copies, ('z', 'core'), 0, 0, tiled=True)]
  transfers between devices with their start and end apart: 14 -> 14, of which waited for: 5 -> 4; matrix products, arithmetic and copies ran while one was open for 2% -> 2% of each run, Pallas kernels for 27% -> 29%
where the time goes in v8:
time: 79.2 us; the launch traced here: 78.7 us
  starting transfers between devices  27.5 us (35%)
  Pallas kernels  25.5 us (32%)
  blocking collectives  18.5 us (23%)
  waiting for transfers between devices  3.47 us (4%)
  local copies, waits for them, and re-layouts  2.91 us (4%)
    pallas_call x9, Pallas kernels, call(): return made(*args)  25.5 us
    all_to_all x1, blocking collectives, on_device(): lax.all_to_all(lines.reshape(everyone, 1, LANES), ('gene', 'z', 'core'),...  18.5 us
    ppermute x6, starting transfers between devices, on_device(): lax.ppermute(parts[k - 1], 'z', [(i, (i + k) % 4) for i in range(4)])  10.6 us
    ppermute x2, starting transfers between devices, on_device(): right = lax.ppermute(own, 'gene', back)  9.18 us
    all_to_all x1, starting transfers between devices, on_device(): every = lax.all_to_all(copies, ('z', 'core'), 0, 0, tiled=True)  5.52 us
    ppermute x6, waiting for transfers between devices, on_device(): lax.ppermute(parts[k - 1], 'z', [(i, (i + k) % 4) for i in range(4)])  2.06 us
    ppermute x2, starting transfers between devices, on_device(): left = lax.ppermute(own, 'gene', ahead)  1.63 us
  transfers between devices with their start and end apart: 14, of which 4 were waited for; matrix products, arithmetic and copies ran while one was open for 2% of the time, Pallas kernels for 29%

profile of v8, /device:TPU:0, one launch (start us, length us, event | category | flops | bytes accessed | tf_op | source)
XLA Modules:
  0.0 78.7 jit_solution(12026160294247511784)
XLA Ops:
  0.6 0.1 collective-permute-start
  0.7 1.4 %broadcast_in_dim.2 = f32[8,2,1280]{2,1,0:T(2,128)} broadcast(f32[2,1280]{1,0:T(2,128)} %bitcast.11), dimensions={1,2} | broadcast | bytes 92160 | tf_op jit(solution)/shard_map/broadcast_in_dim | solution.py:408
  2.1 5.5 %all-to-all-start = ((f32[8,2,1280]{2,1,0:T(2,128)}), f32[8,2,1280]{2,1,0:T(2,128)S(1)}, u32[]{:S(2)}, u32[]{:S(2)}) async-start(f32[8,2,1280]{2,1,0:T(2,128)} %broadcast_in_dim.2), calls=%async_computation | async-start | bytes 163840 | tf_op jit(solution)/shard_map/all_to_all | solution.py:409
  7.6 0.5 collective-permute-start.3
  8.1 0.0 copy-start
  8.1 1.5 %copy-done = bf16[768,1280]{1,0:T(8,128)(2,1)S(1)} copy-done((bf16[768,1280]{1,0:T(8,128)(2,1)S(1)}, bf16[768,1280]{1,0:T(8,128)(2,1)}, u32[]{:S(2)}) %copy-start) | copy-done | bytes 1966104
  9.7 1.3 %shard_map.70.refs_5_.stat = f32[8,768]{1,0:T(8,128)S(1)} custom-call(bf16[768,1280]{1,0:T(8,128)(2,1)S(1)} %copy-done), custom_call_target="tpu_custom_call" | custom-call | flops 2000000000 | tf_op jit(solution)/shard_map/pallas_call | solution.py:394
  10.9 0.0 copy-start.2
  10.9 0.0 collective-permute-start.4
  11.0 0.1 pad_add_fusion.place
  11.0 1.1 %shard_map.68.perms = s32[128,1280]{1,0:T(8,128)S(1)} custom-call(s32[128,1280]{1,0:T(8,128)} %source.1), custom_call_target="tpu_custom_call" | custom-call | flops 1000000000 | tf_op jit(solution)/shard_map/pallas_call | solution.py:394
  12.2 1.2 %all-to-all-done.every = f32[8,2,1280]{2,1,0:T(2,128)S(1)} async-done(((f32[8,2,1280]{2,1,0:T(2,128)}), f32[8,2,1280]{2,1,0:T(2,128)S(1)}, u32[]{:S(2)}, u32[]{:S(2)}) %all-to-all-start) | async-done | bytes 81952 | tf_op jit(solution)/shard_map/all_to_all | solution.py:409
  13.3 0.0 collective-permute-done.theirs
  13.3 0.0 copy-done.2
  13.3 8.5 %shard_map.69 = (bf16[64,2688]{1,0:T(8,128)(2,1)S(1)}, bf16[2,80,16,128]{3,2,1,0:T(8,128)(2,1)S(1)}) custom-call(s32[3]{0:T(128)S(1)} %pad_add_fusion.place, s32[2,2]{1,0:T(2,128)S(1)} %copy-done.2, f32[8,2,1280]{2,1,0:T(2,128)S(1)} %all-to-all-done.every, s32[128,1280]{1,0:T(8,128)S(1)} %shard_map.68.perms, s32[128,1280]{1,0:T(8,128)S(1)} %collective-permute-done.theirs), custom_call_target="tpu_custom_call" | custom-call | flops 8999999488 | tf_op jit(solution)/shard_map/pallas_call | solution.py:394
  21.8 1.6 %collective-permute-start.1 = (bf16[64,2688]{1,0:T(8,128)(2,1)S(1)}, bf16[64,2688]{1,0:T(8,128)(2,1)S(1)}, u32[]{:S(2)}, u32[]{:S(2)}) collective-permute-start(bf16[64,2688]{1,0:T(8,128)(2,1)S(1)} %get-tuple-element.17.refs_1_), channel_id=1, source_target_pairs={{0,8},{8,16},{16,24},{24,32},{32,40},{40,48},{48,56},{56,64},{64,7... | collective-permute-start | bytes 1032200 | tf_op jit(solution)/shard_map/ppermute | solution.py:447
  23.4 3.9 %collective-permute-start.2 = (bf16[64,2688]{1,0:T(8,128)(2,1)S(1)}, bf16[64,2688]{1,0:T(8,128)(2,1)S(1)}, u32[]{:S(2)}, u32[]{:S(2)}) collective-permute-start(bf16[64,2688]{1,0:T(8,128)(2,1)S(1)} %get-tuple-element.17.refs_1_), channel_id=1, source_target_pairs={{8,0},{16,8},{24,16},{32,24},{40,32},{48,40},{56,48},{64,56},{72,6... | collective-permute-start | bytes 1032200 | tf_op jit(solution)/shard_map/ppermute | solution.py:448
  27.3 0.0 copy-start.1
  27.3 8.0 %shard_map.73.refs_1_ = bf16[64,2560]{1,0:T(8,128)(2,1)S(1)} custom-call(s32[3]{0:T(128)S(1)} %pad_add_fusion.place, s32[128,1280]{1,0:T(8,128)S(1)} %shard_map.68.perms, s32[128,1280]{1,0:T(8,128)S(1)} %collective-permute-done.theirs, bf16[2,80,16,128]{3,2,1,0:T(8,128)(2,1)S(1)} %get-tuple-element.25.table), custom_call_target="tpu_custom_call" | custom-call | flops 8000000000 | tf_op jit(solution)/shard_map/pallas_call | solution.py:394
  35.3 0.1 collective-permute-start.8
  35.4 0.0 collective-permute-done.4.refs_6_.their_stat
  35.4 5.3 %collective-permute-start.9 = (bf16[64,2560]{1,0:T(8,128)(2,1)S(1)}, bf16[64,2560]{1,0:T(8,128)(2,1)S(1)}, u32[]{:S(2)}, u32[]{:S(2)}) collective-permute-start(bf16[64,2560]{1,0:T(8,128)(2,1)S(1)} %shard_map.73.refs_1_), channel_id=1, source_target_pairs={{8,0},{16,8},{24,16},{32,24},{40,32},{48,40},{56,48},{64,56},{72,6... | collective-permute-start | bytes 983048 | tf_op jit(solution)/shard_map/ppermute | solution.py:448
  40.7 0.0 collective-permute-done.1.refs_0_
  40.7 0.0 collective-permute-done.2.refs_2_
  40.7 0.0 collective-permute-done.3.refs_4_
  40.7 0.0 copy-done.1
  40.8 1.6 %shard_map.71 = (f32[56,768]{1,0:T(8,128)S(1)}, s16[64,896]{1,0:T(8,128)(2,1)S(1)}, s16[64,896]{1,0:T(8,128)(2,1)S(1)}, s16[64,896]{1,0:T(8,128)(2,1)S(1)}, f32[8,128]{1,0:T(8,128)S(1)}) custom-call(bf16[64,2688]{1,0:T(8,128)(2,1)S(1)} %collective-permute-done.1.refs_0_, bf16[64,2688]{1,0:T(8,128)(2,1)S(1)} %get-tuple-element.17.refs_1_, ...), custom_call_target="tpu_custom_call" | custom-call | flops 2000000000 | tf_op jit(solution)/shard_map/pallas_call | solution.py:394
  42.4 0.9 %collective-permute-start.5 = (s16[64,896]{1,0:T(8,128)(2,1)S(1)}, s16[64,896]{1,0:T(8,128)(2,1)S(1)}, u32[]{:S(2)}, u32[]{:S(2)}) collective-permute-start(s16[64,896]{1,0:T(8,128)(2,1)S(1)} %get-tuple-element.20), channel_id=1, source_target_pairs={{0,2},{2,4},{4,6},{6,0},{1,3},{3,5},{5,7},{7,1},{8,10},{10,12},{12... | collective-permute-start | bytes 344072 | tf_op jit(solution)/shard_map/ppermute | solution.py:461
  43.3 2.7 %collective-permute-start.6 = (s16[64,896]{1,0:T(8,128)(2,1)S(1)}, s16[64,896]{1,0:T(8,128)(2,1)S(1)}, u32[]{:S(2)}, u32[]{:S(2)}) collective-permute-start(s16[64,896]{1,0:T(8,128)(2,1)S(1)} %get-tuple-element.21), channel_id=1, source_target_pairs={{0,4},{2,6},{4,0},{6,2},{1,5},{3,7},{5,1},{7,3},{8,12},{10,14},{12... | collective-permute-start | bytes 344072 | tf_op jit(solution)/shard_map/ppermute | solution.py:461
  46.0 1.5 %collective-permute-start.7 = (s16[64,896]{1,0:T(8,128)(2,1)S(1)}, s16[64,896]{1,0:T(8,128)(2,1)S(1)}, u32[]{:S(2)}, u32[]{:S(2)}) collective-permute-start(s16[64,896]{1,0:T(8,128)(2,1)S(1)} %get-tuple-element.22), channel_id=1, source_target_pairs={{0,6},{2,0},{4,2},{6,4},{1,7},{3,1},{5,3},{7,5},{8,14},{10,8},{12,... | collective-permute-start | bytes 344072 | tf_op jit(solution)/shard_map/ppermute | solution.py:461
  47.5 0.2 collective-permute-done.8.refs_0_
  47.7 0.0 collective-permute-done.9.refs_2_
  47.7 1.6 %shard_map.74 = (f32[48,768]{1,0:T(8,128)S(1)}, s16[48,896]{1,0:T(8,128)(2,1)S(1)}, s16[48,896]{1,0:T(8,128)(2,1)S(1)}, s16[48,896]{1,0:T(8,128)(2,1)S(1)}) custom-call(bf16[64,2560]{1,0:T(8,128)(2,1)S(1)} %collective-permute-done.8.refs_0_, bf16[64,2560]{1,0:T(8,128)(2,1)S(1)} %shard_map.73.refs_1_, bf16[64,2560]{1,0:T(8,128)(2,1)S(1)} %collective-permute-done.9.refs_2_, ...), custom_call_target="tpu_custom_call" | custom-call | flops 2000000000 | tf_op jit(solution)/shard_map/pallas_call | solution.py:394
  49.3 1.3 %collective-permute-start.10 = (s16[48,896]{1,0:T(8,128)(2,1)S(1)}, s16[48,896]{1,0:T(8,128)(2,1)S(1)}, u32[]{:S(2)}, u32[]{:S(2)}) collective-permute-start(s16[48,896]{1,0:T(8,128)(2,1)S(1)} %get-tuple-element.27), channel_id=1, source_target_pairs={{0,2},{2,4},{4,6},{6,0},{1,3},{3,5},{5,7},{7,1},{8,10},{10,12},{12... | collective-permute-start | bytes 258056 | tf_op jit(solution)/shard_map/ppermute | solution.py:461
  50.7 2.7 %collective-permute-start.11 = (s16[48,896]{1,0:T(8,128)(2,1)S(1)}, s16[48,896]{1,0:T(8,128)(2,1)S(1)}, u32[]{:S(2)}, u32[]{:S(2)}) collective-permute-start(s16[48,896]{1,0:T(8,128)(2,1)S(1)} %get-tuple-element.28), channel_id=1, source_target_pairs={{0,4},{2,6},{4,0},{6,2},{1,5},{3,7},{5,1},{7,3},{8,12},{10,14},{12... | collective-permute-start | bytes 258056 | tf_op jit(solution)/shard_map/ppermute | solution.py:461
  53.3 0.0 collective-permute-done.5.m1
  53.3 1.5 %collective-permute-start.12 = (s16[48,896]{1,0:T(8,128)(2,1)S(1)}, s16[48,896]{1,0:T(8,128)(2,1)S(1)}, u32[]{:S(2)}, u32[]{:S(2)}) collective-permute-start(s16[48,896]{1,0:T(8,128)(2,1)S(1)} %get-tuple-element.29), channel_id=1, source_target_pairs={{0,6},{2,0},{4,2},{6,4},{1,7},{3,1},{5,3},{7,5},{8,14},{10,8},{12,... | collective-permute-start | bytes 258056 | tf_op jit(solution)/shard_map/ppermute | solution.py:461
  54.8 0.0 collective-permute-done.6.m2
  54.8 0.0 collective-permute-done.7.m3
  54.8 1.0 %shard_map.72 = (f32[8,128]{1,0:T(8,128)S(1)}, f32[8,768]{1,0:T(8,128)S(1)}) custom-call(s32[3]{0:T(128)S(1)} %pad_add_fusion.place, f32[8,128]{1,0:T(8,128)S(1)} %get-tuple-element.18.info, f32[8,768]{1,0:T(8,128)S(1)} %shard_map.70.refs_5_.stat, f32[8,768]{1,0:T(8,128)S(1)} %collective-permute-done.4.refs_6_.their_stat, ...), custom_call_target="tpu_custom_call" | custom-call | flops 1000000000 | tf_op jit(solution)/shard_map/pallas_call | solution.py:394
  55.8 0.0 collective-permute-done.10.m1
  55.8 0.9 %collective-permute-done.11.m2 = s16[48,896]{1,0:T(8,128)(2,1)S(1)} collective-permute-done((s16[48,896]{1,0:T(8,128)(2,1)S(1)}, s16[48,896]{1,0:T(8,128)(2,1)S(1)}, u32[]{:S(2)}, u32[]{:S(2)}) %collective-permute-start.11) | collective-permute-done | bytes 86048 | tf_op jit(solution)/shard_map/ppermute | solution.py:461
  56.7 1.1 %collective-permute-done.12.m3 = s16[48,896]{1,0:T(8,128)(2,1)S(1)} collective-permute-done((s16[48,896]{1,0:T(8,128)(2,1)S(1)}, s16[48,896]{1,0:T(8,128)(2,1)S(1)}, u32[]{:S(2)}, u32[]{:S(2)}) %collective-permute-start.12) | collective-permute-done | bytes 86048 | tf_op jit(solution)/shard_map/ppermute | solution.py:461
  57.8 0.0 copy-start.3
  57.8 0.9 %shard_map.75 = f32[128,128]{1,0:T(8,128)S(1)} custom-call(s32[3]{0:T(128)S(1)} %pad_add_fusion.place, f32[8,128]{1,0:T(8,128)S(1)} %get-tuple-element.18.info, f32[8,768]{1,0:T(8,128)S(1)} %get-tuple-element.23.aux, f32[8,128]{1,0:T(8,128)S(1)} %get-tuple-element.24.tile, f32[48,768]{1,0:T(8,128)S(1)} %get-tuple-element.26.own, ...), custom_call_target="tpu_custom_call" | custom-call | flops 2000000000 | tf_op jit(solution)/shard_map/pallas_call | solution.py:394
  58.8 18.5 %all_to_all.10 = f32[128,1,128]{2,1,0:T(1,128)S(1)} all-to-all(f32[128,1,128]{2,1,0:T(1,128)S(1)} %bitcast.9), channel_id=1, replica_groups=mesh['gene'=16,'z'=4,'core'=2] {'gene','z','core'}, dimensions={0} | all-to-all | bytes 131072 | tf_op jit(solution)/shard_map/all_to_all | solution.py:471
  77.2 0.0 copy-done.3
  77.2 1.5 %shard_map.76 = (f32[2,128]{1,0:T(2,128)}, f32[1,2]{1,0:T(1,128)}) custom-call(s32[3]{0:T(128)S(1)} %pad_add_fusion.place, s32[32]{0:T(128)S(1)} %copy-done.3, f32[128,128]{1,0:T(8,128)S(1)} %bitcast.10), custom_call_target="tpu_custom_call" | custom-call | flops 2000000000 | tf_op jit(solution)/shard_map/pallas_call | solution.py:394
Async XLA Ops:
  0.6 12.7 %collective-permute-start = (s32[128,1280]{1,0:T(8,128)}, s32[128,1280]{1,0:T(8,128)S(1)}, u32[]{:S(2)}, u32[]{:S(2)}) collective-permute-start(s32[128,1280]{1,0:T(8,128)} %source.1), channel_id=1, source_target_pairs={{0,1},{1,0},{2,3},{3,2},{4,5},{5,4},{6,7},{7,6},{8,9},{9,8},{10,11... | collective-permute-start | bytes 1966088 | tf_op jit(solution)/shard_map/ppermute | solution.py:411
  2.1 11.2 %all-to-all-start = ((f32[8,2,1280]{2,1,0:T(2,128)}), f32[8,2,1280]{2,1,0:T(2,128)S(1)}, u32[]{:S(2)}, u32[]{:S(2)}) async-start(f32[8,2,1280]{2,1,0:T(2,128)} %broadcast_in_dim.2), calls=%async_computation | async-start | bytes 163840 | tf_op jit(solution)/shard_map/all_to_all | solution.py:409
  7.6 33.1 %collective-permute-start.3 = (bf16[768,1280]{1,0:T(8,128)(2,1)}, bf16[768,1280]{1,0:T(8,128)(2,1)S(1)}, u32[]{:S(2)}, u32[]{:S(2)}) collective-permute-start(bf16[768,1280]{1,0:T(8,128)(2,1)} %refs_3_.3), channel_id=1, source_target_pairs={{0,1},{1,0},{2,3},{3,2},{4,5},{5,4},{6,7},{7,6},{8,9},{9,8},{10,11... | collective-permute-start | bytes 5898248 | tf_op jit(solution)/shard_map/ppermute | solution.py:412
  8.1 1.5 %copy-start = (bf16[768,1280]{1,0:T(8,128)(2,1)S(1)}, bf16[768,1280]{1,0:T(8,128)(2,1)}, u32[]{:S(2)}) copy-start(bf16[768,1280]{1,0:T(8,128)(2,1)} %refs_3_.3) | copy-start | bytes 5898244
  10.9 2.4 %copy-start.2 = (s32[2,2]{1,0:T(2,128)S(1)}, s32[2,2]{1,0:T(2,128)}, u32[]{:S(2)}) copy-start(s32[2,2]{1,0:T(2,128)} %windows.1) | copy-start | bytes 52
  10.9 24.5 %collective-permute-start.4 = (f32[8,768]{1,0:T(8,128)S(1)}, f32[8,768]{1,0:T(8,128)S(1)}, u32[]{:S(2)}, u32[]{:S(2)}) collective-permute-start(f32[8,768]{1,0:T(8,128)S(1)} %shard_map.70.refs_5_.stat), channel_id=1, source_target_pairs={{0,1},{1,0},{2,3},{3,2},{4,5},{5,4},{6,7},{7,6},{8,9},{9,8},{10,11... | collective-permute-start | bytes 73736 | tf_op jit(solution)/shard_map/ppermute | solution.py:428
  21.8 18.9 %collective-permute-start.1 = (bf16[64,2688]{1,0:T(8,128)(2,1)S(1)}, bf16[64,2688]{1,0:T(8,128)(2,1)S(1)}, u32[]{:S(2)}, u32[]{:S(2)}) collective-permute-start(bf16[64,2688]{1,0:T(8,128)(2,1)S(1)} %get-tuple-element.17.refs_1_), channel_id=1, source_target_pairs={{0,8},{8,16},{16,24},{24,32},{32,40},{40,48},{48,56},{56,64},{64,7... | collective-permute-start | bytes 1032200 | tf_op jit(solution)/shard_map/ppermute | solution.py:447
  23.4 17.3 %collective-permute-start.2 = (bf16[64,2688]{1,0:T(8,128)(2,1)S(1)}, bf16[64,2688]{1,0:T(8,128)(2,1)S(1)}, u32[]{:S(2)}, u32[]{:S(2)}) collective-permute-start(bf16[64,2688]{1,0:T(8,128)(2,1)S(1)} %get-tuple-element.17.refs_1_), channel_id=1, source_target_pairs={{8,0},{16,8},{24,16},{32,24},{40,32},{48,40},{56,48},{64,56},{72,6... | collective-permute-start | bytes 1032200 | tf_op jit(solution)/shard_map/ppermute | solution.py:448
  27.3 13.5 %copy-start.1 = (bf16[768,1280]{1,0:T(8,128)(2,1)S(1)}, bf16[768,1280]{1,0:T(8,128)(2,1)}, u32[]{:S(2)}) copy-start(bf16[768,1280]{1,0:T(8,128)(2,1)} %refs_3_.3) | copy-start | bytes 5898244
  35.3 12.4 %collective-permute-start.8 = (bf16[64,2560]{1,0:T(8,128)(2,1)S(1)}, bf16[64,2560]{1,0:T(8,128)(2,1)S(1)}, u32[]{:S(2)}, u32[]{:S(2)}) collective-permute-start(bf16[64,2560]{1,0:T(8,128)(2,1)S(1)} %shard_map.73.refs_1_), channel_id=1, source_target_pairs={{0,8},{8,16},{16,24},{24,32},{32,40},{40,48},{48,56},{56,64},{64,7... | collective-permute-start | bytes 983048 | tf_op jit(solution)/shard_map/ppermute | solution.py:447
  35.4 12.3 %collective-permute-start.9 = (bf16[64,2560]{1,0:T(8,128)(2,1)S(1)}, bf16[64,2560]{1,0:T(8,128)(2,1)S(1)}, u32[]{:S(2)}, u32[]{:S(2)}) collective-permute-start(bf16[64,2560]{1,0:T(8,128)(2,1)S(1)} %shard_map.73.refs_1_), channel_id=1, source_target_pairs={{8,0},{16,8},{24,16},{32,24},{40,32},{48,40},{56,48},{64,56},{72,6... | collective-permute-start | bytes 983048 | tf_op jit(solution)/shard_map/ppermute | solution.py:448
  42.4 11.0 %collective-permute-start.5 = (s16[64,896]{1,0:T(8,128)(2,1)S(1)}, s16[64,896]{1,0:T(8,128)(2,1)S(1)}, u32[]{:S(2)}, u32[]{:S(2)}) collective-permute-start(s16[64,896]{1,0:T(8,128)(2,1)S(1)} %get-tuple-element.20), channel_id=1, source_target_pairs={{0,2},{2,4},{4,6},{6,0},{1,3},{3,5},{5,7},{7,1},{8,10},{10,12},{12... | collective-permute-start | bytes 344072 | tf_op jit(solution)/shard_map/ppermute | solution.py:461
  43.3 11.5 %collective-permute-start.6 = (s16[64,896]{1,0:T(8,128)(2,1)S(1)}, s16[64,896]{1,0:T(8,128)(2,1)S(1)}, u32[]{:S(2)}, u32[]{:S(2)}) collective-permute-start(s16[64,896]{1,0:T(8,128)(2,1)S(1)} %get-tuple-element.21), channel_id=1, source_target_pairs={{0,4},{2,6},{4,0},{6,2},{1,5},{3,7},{5,1},{7,3},{8,12},{10,14},{12... | collective-permute-start | bytes 344072 | tf_op jit(solution)/shard_map/ppermute | solution.py:461
  46.0 8.8 %collective-permute-start.7 = (s16[64,896]{1,0:T(8,128)(2,1)S(1)}, s16[64,896]{1,0:T(8,128)(2,1)S(1)}, u32[]{:S(2)}, u32[]{:S(2)}) collective-permute-start(s16[64,896]{1,0:T(8,128)(2,1)S(1)} %get-tuple-element.22), channel_id=1, source_target_pairs={{0,6},{2,0},{4,2},{6,4},{1,7},{3,1},{5,3},{7,5},{8,14},{10,8},{12,... | collective-permute-start | bytes 344072 | tf_op jit(solution)/shard_map/ppermute | solution.py:461
  49.3 6.5 %collective-permute-start.10 = (s16[48,896]{1,0:T(8,128)(2,1)S(1)}, s16[48,896]{1,0:T(8,128)(2,1)S(1)}, u32[]{:S(2)}, u32[]{:S(2)}) collective-permute-start(s16[48,896]{1,0:T(8,128)(2,1)S(1)} %get-tuple-element.27), channel_id=1, source_target_pairs={{0,2},{2,4},{4,6},{6,0},{1,3},{3,5},{5,7},{7,1},{8,10},{10,12},{12... | collective-permute-start | bytes 258056 | tf_op jit(solution)/shard_map/ppermute | solution.py:461
  50.7 6.1 %collective-permute-start.11 = (s16[48,896]{1,0:T(8,128)(2,1)S(1)}, s16[48,896]{1,0:T(8,128)(2,1)S(1)}, u32[]{:S(2)}, u32[]{:S(2)}) collective-permute-start(s16[48,896]{1,0:T(8,128)(2,1)S(1)} %get-tuple-element.28), channel_id=1, source_target_pairs={{0,4},{2,6},{4,0},{6,2},{1,5},{3,7},{5,1},{7,3},{8,12},{10,14},{12... | collective-permute-start | bytes 258056 | tf_op jit(solution)/shard_map/ppermute | solution.py:461
  53.3 4.5 %collective-permute-start.12 = (s16[48,896]{1,0:T(8,128)(2,1)S(1)}, s16[48,896]{1,0:T(8,128)(2,1)S(1)}, u32[]{:S(2)}, u32[]{:S(2)}) collective-permute-start(s16[48,896]{1,0:T(8,128)(2,1)S(1)} %get-tuple-element.29), channel_id=1, source_target_pairs={{0,6},{2,0},{4,2},{6,4},{1,7},{3,1},{5,3},{7,5},{8,14},{10,8},{12,... | collective-permute-start | bytes 258056 | tf_op jit(solution)/shard_map/ppermute | solution.py:461
  57.8 19.4 %copy-start.3 = (s32[32]{0:T(128)S(1)}, s32[32]{0:T(128)}, u32[]{:S(2)}) copy-start(s32[32]{0:T(128)} %order.1) | copy-start | bytes 388

commit v9 on v7

--- a/solution.py
+++ b/solution.py
@@ -74,6 +74,12 @@
         precision=lax.Precision.HIGHEST,
         preferred_element_type=jnp.float32,
     )[:1]
+
+
+def fetch_kernel(source, out, done):
+    copy = pltpu.make_async_copy(source, out, done)
+    copy.start()
+    copy.wait()
 
 
 def moments_kernel(dosage, out, sums):
@@ -175,13 +181,16 @@
     return mean, jnp.sqrt(jnp.maximum(square - total * mean, 0.0) + count * epsilon)
 
 
-def sums_kernel(chunk, *refs):
-    blocks = refs[:3]
-    dosage, theirs, stat, their_stat, own, m1, m2, m3 = refs[3:11]
+def sums_kernel(count, with_direct, held, *refs):
+    blocks = refs[:count]
+    dosage, theirs, stat, their_stat = refs[count : count + 4]
+    earlier = refs[count + 4 : count + 4 + held]
+    own, m1, m2, m3 = refs[count + 4 + held : count + 8 + held]
+    start = earlier[0].shape[0] if held else 0
     variants, width = dosage.shape
     stat = stat[...] + their_stat[...]
     rows = jnp.concatenate([block[:, : 2 * width] for block in blocks], axis=0)
-    if chunk == 0:
+    if with_direct:
         tiles = 2 * width // LANES
         extra = [block[:, 2 * width :].astype(jnp.float32) for block in blocks]
         direct = [
@@ -197,10 +206,10 @@
     got = (both - column * mean) * (1.0 / size)
     column = jnp.broadcast_to(column, (column.shape[0], LANES))
     at = lambda n, kz: slice(n * 2 * TILE + kz * HALF, n * 2 * TILE + (kz + 1) * HALF)
-    for n in range(6):
+    for n in range(2 * count):
         own[n * HALF : (n + 1) * HALF, :] = both[at(n, 0)]
     largest = jnp.abs(got[at(0, 1)])
-    for n in range(6):
+    for n in range(2 * count):
         for kz in range(1, 4):
             largest = jnp.maximum(largest, jnp.abs(got[at(n, kz)]))
 
@@ -211,15 +220,17 @@
         return to_int16(jnp.where(lane == 0, code, line))
 
     code = bound_code(jnp.max(largest, keepdims=True))
+    for message, before in zip((m1, m2, m3), earlier):
+        message[:start, :] = before[...]
     for k, message in enumerate((m1, m2, m3)):
-        for t in range(3):
+        for t in range(count):
             pair = [at(2 * t, k + 1), at(2 * t + 1, k + 1)]
             values = jnp.concatenate([got[p] for p in pair], axis=0)
             columns = jnp.concatenate([column[p] for p in pair], axis=0)
-            message[t * TILE : (t + 1) * TILE, :variants] = to_int16(coded(values, code))
-            message[t * TILE : (t + 1) * TILE, variants:] = beside(code, columns)
-    if chunk == 0:
-        spots = slice(12 * TILE, 12 * TILE + HALF)
+            message[start + t * TILE : start + (t + 1) * TILE, :variants] = to_int16(coded(values, code))
+            message[start + t * TILE : start + (t + 1) * TILE, variants:] = beside(code, columns)
+    if with_direct:
+        spots = slice(4 * count * TILE, 4 * count * TILE + HALF)
         own[48:56, :] = both[spots]
         values, columns = got[spots], column[spots]
         code = bound_code(jnp.max(jnp.abs(values), keepdims=True))
@@ -236,8 +247,8 @@
             info[o : o + 1, :] = e[2 * tiles : 2 * tiles + 1] * 128.0 + e[2 * tiles + 1 : 2 * tiles + 2]
 
 
-def added(own, messages, means, sizes):
-    total = own[...]
+def added(owns, messages, means, sizes):
+    total = jnp.concatenate([own[...] for own in owns], axis=0)
     rows, variants = total.shape
     for message, mean, size in zip(messages, means, sizes):
         side = message[:rows, variants:].astype(jnp.int32).astype(jnp.float32)
@@ -290,7 +301,7 @@
         aux[1 + q : 2 + q, :] = means[q]
         aux[4 + q : 5 + q, :] = sizes[q]
     aux[7:8, :] = jnp.zeros_like(scale)
-    sums = added(own, (m1, m2, m3), means, sizes) * scale
+    sums = added((own,), (m1, m2, m3), means, sizes) * scale
     inside = list(inside_rows(place, info, variants))
     tile = best_tile(jnp.zeros((HALF, LANES), jnp.float32), 0, sums, inside)
     lane = lax.broadcasted_iota(jnp.int32, (HALF, LANES), 1)
@@ -301,11 +312,11 @@
     out[...] = tile
 
 
-def maxima_kernel(place, info, aux, tile, own, m1, m2, m3, out):
-    variants = own.shape[1]
+def maxima_kernel(place, info, aux, tile, near, far, m1, m2, m3, out):
+    variants = near.shape[1]
     means = [aux[1 + q : 2 + q, :] for q in range(3)]
     sizes = [aux[4 + q : 5 + q, :] for q in range(3)]
-    sums = added(own, (m1, m2, m3), means, sizes) * aux[0:1, :]
+    sums = added((near, far), (m1, m2, m3), means, sizes) * aux[0:1, :]
     tile = best_tile(tile[...], 1, sums, inside_rows(place, info, variants))
     lane = lax.broadcasted_iota(jnp.int32, (HALF, LANES), 1)
     row = lax.broadcasted_iota(jnp.int32, (HALF, LANES), 0)
@@ -362,11 +373,7 @@
             pl.BlockSpec(memory_space=pltpu.HBM) if i in remote else SM if k else VM
             for i, k in enumerate(scalar)
         ],
-        out_specs=tuple([VM] * len(outs))
-        if many
-        else pl.BlockSpec(memory_space=pltpu.HBM)
-        if remote
-        else VM,
+        out_specs=tuple([VM] * len(outs)) if many else VM,
         scratch_shapes=scratch,
         compiler_params=pltpu.CompilerParams(vmem_limit_bytes=24 << 20),
         cost_estimate=pl.CostEstimate(flops=int(us * 1e9), bytes_accessed=0, transcendentals=0),
@@ -396,6 +403,14 @@
     mates = [(0, 1), (1, 0)]
     their_perms = lax.ppermute(perms, "core", mates)
     theirs = lax.ppermute(dosage, "core", mates)
+    near_perms = call(
+        fetch_kernel,
+        shape(perms.shape, jnp.int32),
+        [perms],
+        1,
+        [pltpu.SemaphoreType.DMA],
+        remote=(0,),
+    )
     stat = call(
         moments_kernel,
         shape((8, variants)),
@@ -409,13 +424,13 @@
     first, table = call(
         first_kernel,
         [shape((4 * TILE, 2 * width + LANES), jnp.bfloat16), table_shape],
-        [place, windows, every, perms, their_perms],
+        [place, windows, every, near_perms, their_perms],
         9,
     )
     second = call(
         functools.partial(later_kernel, 1),
         shape((4 * TILE, 2 * width), jnp.bfloat16),
-        [place, perms, their_perms, table],
+        [place, near_perms, their_perms, table],
         8,
     )
     ahead = [(i, (i + 1) % owners) for i in range(owners)]
@@ -424,17 +439,31 @@
     for h, own in enumerate((first, second)):
         left = lax.ppermute(own, "gene", ahead)
         right = lax.ppermute(own, "gene", back)
-        depth, deep = (56, 64) if h == 0 else (48, 48)
-        outs = [shape((depth, variants))] + [shape((deep, variants + LANES), jnp.int16)] * 3
-        own, *parts = call(
-            functools.partial(sums_kernel, h),
-            outs + ([shape((8, LANES))] if h == 0 else []),
-            [left, own, right, dosage, theirs, stat, their_stat],
-            2,
-        )
+        common = [dosage, theirs, stat, their_stat]
+        wide = variants + LANES
+        codes = lambda rows: [shape((rows, wide), jnp.int16)] * 3
         if h == 0:
-            info = parts.pop()
-        group = [own]
+            mine, *parts, info = call(
+                functools.partial(sums_kernel, 3, True, 0),
+                [shape((56, variants)), *codes(64), shape((8, LANES))],
+                [left, own, right, *common],
+                2,
+            )
+            group = [mine]
+        else:
+            near, *parts = call(
+                functools.partial(sums_kernel, 2, False, 0),
+                [shape((32, variants)), *codes(32)],
+                [left, own, *common],
+                1,
+            )
+            far, *parts = call(
+                functools.partial(sums_kernel, 1, False, 3),
+                [shape((16, variants)), *codes(48)],
+                [right, *common, *parts],
+                1,
+            )
+            group = [near, far]
         for k in range(1, 4):
             group.append(lax.ppermute(parts[k - 1], "z", [(i, (i + k) % 4) for i in range(4)]))
         sums.append(group)

time: 77.2 us -> 80.8 us (1.047)
  Pallas kernels: 23.4 us -> 25.9 us
  local copies, waits for them, and re-layouts: 2.91 us -> 1.37 us
  waiting for transfers between devices: 5.94 us -> 7.39 us
    pallas_call x8 -> x10, Pallas kernels: 23.4 us -> 25.9 us  [call(): return made(*args)]
    all_to_all x1, waiting for transfers between devices: 2.3 us -> 4.02 us  [on_device(): every = lax.all_to_all(copies, ('z', 'core'), 0, 0, tiled=True)]
    unnamed x10 -> x6, local copies, waits for them, and re-layouts: 1.56 us -> 0.01 us
    ppermute x2, waiting for transfers between devices: 1.38 us -> 0.01 us  [on_device(): left = lax.ppermute(own, 'gene', ahead)]
    ppermute x1, waiting for transfers between devices: 0.01 us -> 1.2 us  [on_device(): their_stat = lax.ppermute(stat, 'core', mates)]
  transfers between devices with their start and end apart: 14 -> 14, of which waited for: 5 -> 5; matrix products, arithmetic and copies ran while one was open for 2% -> 2% of each run, Pallas kernels for 27% -> 29%
where the time goes in v9:
time: 80.8 us; the launch traced here: 80.2 us
  Pallas kernels  25.9 us (32%)
  starting transfers between devices  25.6 us (32%)
  blocking collectives  19.2 us (24%)
  waiting for transfers between devices  7.39 us (9%)
  local copies, waits for them, and re-layouts  1.37 us (2%)
    pallas_call x10, Pallas kernels, call(): return made(*args)  25.9 us
    all_to_all x1, blocking collectives, on_device(): lax.all_to_all(lines.reshape(everyone, 1, LANES), ('gene', 'z', 'core'),...  19.2 us
    ppermute x2, starting transfers between devices, on_device(): right = lax.ppermute(own, 'gene', back)  9.17 us
    ppermute x6, starting transfers between devices, on_device(): lax.ppermute(parts[k - 1], 'z', [(i, (i + k) % 4) for i in range(4)])  8.52 us
    all_to_all x1, starting transfers between devices, on_device(): every = lax.all_to_all(copies, ('z', 'core'), 0, 0, tiled=True)  5.65 us
    all_to_all x1, waiting for transfers between devices, on_device(): every = lax.all_to_all(copies, ('z', 'core'), 0, 0, tiled=True)  4.02 us
    ppermute x6, waiting for transfers between devices, on_device(): lax.ppermute(parts[k - 1], 'z', [(i, (i + k) % 4) for i in range(4)])  1.73 us
    ppermute x2, starting transfers between devices, on_device(): left = lax.ppermute(own, 'gene', ahead)  1.63 us
  transfers between devices with their start and end apart: 14, of which 5 were waited for; matrix products, arithmetic and copies ran while one was open for 2% of the time, Pallas kernels for 29%

profile of v9, /device:TPU:0, one launch (start us, length us, event | category | flops | bytes accessed | tf_op | source)
XLA Modules:
  0.0 80.2 jit_solution(8867343760206849480)
XLA Ops:
  0.6 0.1 collective-permute-start
  0.7 1.4 %broadcast_in_dim.2 = f32[8,2,1280]{2,1,0:T(2,128)} broadcast(f32[2,1280]{1,0:T(2,128)} %bitcast.11), dimensions={1,2} | broadcast | bytes 92160 | tf_op jit(solution)/shard_map/broadcast_in_dim | solution.py:401
  2.1 0.0 copy-start.1
  2.1 5.7 %all-to-all-start = ((f32[8,2,1280]{2,1,0:T(2,128)}), f32[8,2,1280]{2,1,0:T(2,128)S(1)}, u32[]{:S(2)}, u32[]{:S(2)}) async-start(f32[8,2,1280]{2,1,0:T(2,128)} %broadcast_in_dim.2), calls=%async_computation | async-start | bytes 163840 | tf_op jit(solution)/shard_map/all_to_all | solution.py:402
  7.7 0.5 collective-permute-start.3
  8.2 0.1 pad_add_fusion.place
  8.3 1.1 %shard_map.68.perms = s32[128,1280]{1,0:T(8,128)S(1)} custom-call(s32[128,1280]{1,0:T(8,128)} %source.1), custom_call_target="tpu_custom_call" | custom-call | flops 1000000000 | tf_op jit(solution)/shard_map/pallas_call | solution.py:387
  9.4 4.0 %all-to-all-done.every = f32[8,2,1280]{2,1,0:T(2,128)S(1)} async-done(((f32[8,2,1280]{2,1,0:T(2,128)}), f32[8,2,1280]{2,1,0:T(2,128)S(1)}, u32[]{:S(2)}, u32[]{:S(2)}) %all-to-all-start) | async-done | bytes 81952 | tf_op jit(solution)/shard_map/all_to_all | solution.py:402
  13.4 0.0 collective-permute-done.theirs
  13.5 0.0 copy-done.1
  13.5 8.0 %shard_map.69 = (bf16[64,2688]{1,0:T(8,128)(2,1)S(1)}, bf16[2,80,16,128]{3,2,1,0:T(8,128)(2,1)S(1)}) custom-call(s32[3]{0:T(128)S(1)} %pad_add_fusion.place, s32[2,2]{1,0:T(2,128)S(1)} %copy-done.1, f32[8,2,1280]{2,1,0:T(2,128)S(1)} %all-to-all-done.every, s32[128,1280]{1,0:T(8,128)S(1)} %shard_map.68.perms, s32[128,1280]{1,0:T(8,128)S(1)} %collective-permute-done.theirs), custom_call_target="tpu_custom_call" | custom-call | flops 8999999488 | tf_op jit(solution)/shard_map/pallas_call | solution.py:387
  21.5 1.6 %collective-permute-start.1 = (bf16[64,2688]{1,0:T(8,128)(2,1)S(1)}, bf16[64,2688]{1,0:T(8,128)(2,1)S(1)}, u32[]{:S(2)}, u32[]{:S(2)}) collective-permute-start(bf16[64,2688]{1,0:T(8,128)(2,1)S(1)} %get-tuple-element.21.refs_1_), channel_id=1, source_target_pairs={{0,8},{8,16},{16,24},{24,32},{32,40},{40,48},{48,56},{56,64},{64,7... | collective-permute-start | bytes 1032200 | tf_op jit(solution)/shard_map/ppermute | solution.py:440
  23.1 3.9 %collective-permute-start.2 = (bf16[64,2688]{1,0:T(8,128)(2,1)S(1)}, bf16[64,2688]{1,0:T(8,128)(2,1)S(1)}, u32[]{:S(2)}, u32[]{:S(2)}) collective-permute-start(bf16[64,2688]{1,0:T(8,128)(2,1)S(1)} %get-tuple-element.21.refs_1_), channel_id=1, source_target_pairs={{8,0},{16,8},{24,16},{32,24},{40,32},{48,40},{56,48},{64,56},{72,6... | collective-permute-start | bytes 1032200 | tf_op jit(solution)/shard_map/ppermute | solution.py:441
  26.9 0.0 copy-start
  26.9 7.6 %shard_map.73.refs_1_ = bf16[64,2560]{1,0:T(8,128)(2,1)S(1)} custom-call(s32[3]{0:T(128)S(1)} %pad_add_fusion.place, s32[128,1280]{1,0:T(8,128)S(1)} %shard_map.68.perms, s32[128,1280]{1,0:T(8,128)S(1)} %collective-permute-done.theirs, bf16[2,80,16,128]{3,2,1,0:T(8,128)(2,1)S(1)} %get-tuple-element.29.table), custom_call_target="tpu_custom_call" | custom-call | flops 8000000000 | tf_op jit(solution)/shard_map/pallas_call | solution.py:387
  34.5 0.1 collective-permute-start.8
  34.5 0.0 copy-done
  34.6 1.3 %shard_map.70.refs_5_.stat.refs_4_.refs_3_ = f32[8,768]{1,0:T(8,128)S(1)} custom-call(bf16[768,1280]{1,0:T(8,128)(2,1)S(1)} %copy-done), custom_call_target="tpu_custom_call" | custom-call | flops 2000000000 | tf_op jit(solution)/shard_map/pallas_call | solution.py:387
  35.8 0.0 collective-permute-start.4
  35.8 1.2 %collective-permute-done.4.refs_6_.their_stat.refs_5_.refs_4_ = f32[8,768]{1,0:T(8,128)S(1)} collective-permute-done((f32[8,768]{1,0:T(8,128)S(1)}, f32[8,768]{1,0:T(8,128)S(1)}, u32[]{:S(2)}, u32[]{:S(2)}) %collective-permute-start.4) | collective-permute-done | bytes 24608 | tf_op jit(solution)/shard_map/ppermute | solution.py:421
  37.0 5.3 %collective-permute-start.9 = (bf16[64,2560]{1,0:T(8,128)(2,1)S(1)}, bf16[64,2560]{1,0:T(8,128)(2,1)S(1)}, u32[]{:S(2)}, u32[]{:S(2)}) collective-permute-start(bf16[64,2560]{1,0:T(8,128)(2,1)S(1)} %shard_map.73.refs_1_), channel_id=1, source_target_pairs={{8,0},{16,8},{24,16},{32,24},{40,32},{48,40},{56,48},{64,56},{72,6... | collective-permute-start | bytes 983048 | tf_op jit(solution)/shard_map/ppermute | solution.py:441
  42.3 0.0 collective-permute-done.1.refs_0_
  42.4 0.0 collective-permute-done.2.refs_2_
  42.4 0.0 collective-permute-done.3.refs_4_.refs_3_.refs_2_
  42.4 1.6 %shard_map.71 = (f32[56,768]{1,0:T(8,128)S(1)}, s16[64,896]{1,0:T(8,128)(2,1)S(1)}, s16[64,896]{1,0:T(8,128)(2,1)S(1)}, s16[64,896]{1,0:T(8,128)(2,1)S(1)}, f32[8,128]{1,0:T(8,128)S(1)}) custom-call(bf16[64,2688]{1,0:T(8,128)(2,1)S(1)} %collective-permute-done.1.refs_0_, bf16[64,2688]{1,0:T(8,128)(2,1)S(1)} %get-tuple-element.21.refs_1_, ...), custom_call_target="tpu_custom_call" | custom-call | flops 2000000000 | tf_op jit(solution)/shard_map/pallas_call | solution.py:387
  44.0 0.7 collective-permute-start.5
  44.6 2.0 %collective-permute-start.6 = (s16[64,896]{1,0:T(8,128)(2,1)S(1)}, s16[64,896]{1,0:T(8,128)(2,1)S(1)}, u32[]{:S(2)}, u32[]{:S(2)}) collective-permute-start(s16[64,896]{1,0:T(8,128)(2,1)S(1)} %get-tuple-element.25), channel_id=1, source_target_pairs={{0,4},{2,6},{4,0},{6,2},{1,5},{3,7},{5,1},{7,3},{8,12},{10,14},{12... | collective-permute-start | bytes 344072 | tf_op jit(solution)/shard_map/ppermute | solution.py:468
  46.7 1.0 %collective-permute-start.7 = (s16[64,896]{1,0:T(8,128)(2,1)S(1)}, s16[64,896]{1,0:T(8,128)(2,1)S(1)}, u32[]{:S(2)}, u32[]{:S(2)}) collective-permute-start(s16[64,896]{1,0:T(8,128)(2,1)S(1)} %get-tuple-element.26), channel_id=1, source_target_pairs={{0,6},{2,0},{4,2},{6,4},{1,7},{3,1},{5,3},{7,5},{8,14},{10,8},{12,... | collective-permute-start | bytes 344072 | tf_op jit(solution)/shard_map/ppermute | solution.py:468
  47.7 0.0 collective-permute-done.8.refs_0_
  47.7 1.6 %shard_map.74 = (f32[32,768]{1,0:T(8,128)S(1)}, s16[32,896]{1,0:T(8,128)(2,1)S(1)}, s16[32,896]{1,0:T(8,128)(2,1)S(1)}, s16[32,896]{1,0:T(8,128)(2,1)S(1)}) custom-call(bf16[64,2560]{1,0:T(8,128)(2,1)S(1)} %collective-permute-done.8.refs_0_, bf16[64,2560]{1,0:T(8,128)(2,1)S(1)} %shard_map.73.refs_1_, bf16[768,1280]{1,0:T(8,128)(2,1)S(1)} %copy-done, ...), custom_call_target="tpu_custom_call" | custom-call | flops 1000000000 | tf_op jit(solution)/shard_map/pallas_call | solution.py:387
  49.2 0.4 collective-permute-done.9.refs_0_
  49.6 1.5 %shard_map.75 = (f32[16,768]{1,0:T(8,128)S(1)}, s16[48,896]{1,0:T(8,128)(2,1)S(1)}, s16[48,896]{1,0:T(8,128)(2,1)S(1)}, s16[48,896]{1,0:T(8,128)(2,1)S(1)}) custom-call(bf16[64,2560]{1,0:T(8,128)(2,1)S(1)} %collective-permute-done.9.refs_0_, bf16[768,1280]{1,0:T(8,128)(2,1)S(1)} %copy-done, ...), custom_call_target="tpu_custom_call" | custom-call | flops 1000000000 | tf_op jit(solution)/shard_map/pallas_call | solution.py:387
  51.1 0.7 collective-permute-start.10
  51.8 2.0 %collective-permute-start.11 = (s16[48,896]{1,0:T(8,128)(2,1)S(1)}, s16[48,896]{1,0:T(8,128)(2,1)S(1)}, u32[]{:S(2)}, u32[]{:S(2)}) collective-permute-start(s16[48,896]{1,0:T(8,128)(2,1)S(1)} %get-tuple-element.36), channel_id=1, source_target_pairs={{0,4},{2,6},{4,0},{6,2},{1,5},{3,7},{5,1},{7,3},{8,12},{10,14},{12... | collective-permute-start | bytes 258056 | tf_op jit(solution)/shard_map/ppermute | solution.py:468
  53.8 0.0 collective-permute-done.5.m1
  53.8 2.2 %collective-permute-start.12 = (s16[48,896]{1,0:T(8,128)(2,1)S(1)}, s16[48,896]{1,0:T(8,128)(2,1)S(1)}, u32[]{:S(2)}, u32[]{:S(2)}) collective-permute-start(s16[48,896]{1,0:T(8,128)(2,1)S(1)} %get-tuple-element.37), channel_id=1, source_target_pairs={{0,6},{2,0},{4,2},{6,4},{1,7},{3,1},{5,3},{7,5},{8,14},{10,8},{12,... | collective-permute-start | bytes 258056 | tf_op jit(solution)/shard_map/ppermute | solution.py:468
  56.0 0.0 collective-permute-done.6.m2
  56.0 0.0 collective-permute-done.7.m3
  56.0 1.0 %shard_map.72 = (f32[8,128]{1,0:T(8,128)S(1)}, f32[8,768]{1,0:T(8,128)S(1)}) custom-call(s32[3]{0:T(128)S(1)} %pad_add_fusion.place, f32[8,128]{1,0:T(8,128)S(1)} %get-tuple-element.22.info, f32[8,768]{1,0:T(8,128)S(1)} %shard_map.70.refs_5_.stat.refs_4_.refs_3_, f32[8,768]{1,0:T(8,128)S(1)} %collective-permute-done.4.refs_6_.their_stat.refs_5_.refs_4_, ...), custom_call_target="tpu_custom_call" | custom-call | flops 1000000000 | tf_op jit(solution)/shard_map/pallas_call | solution.py:387
  56.9 1.0 %collective-permute-done.10.m1 = s16[48,896]{1,0:T(8,128)(2,1)S(1)} collective-permute-done((s16[48,896]{1,0:T(8,128)(2,1)S(1)}, s16[48,896]{1,0:T(8,128)(2,1)S(1)}, u32[]{:S(2)}, u32[]{:S(2)}) %collective-permute-start.10) | collective-permute-done | bytes 86048 | tf_op jit(solution)/shard_map/ppermute | solution.py:468
  58.0 0.0 collective-permute-done.11.m2
  58.0 0.7 collective-permute-done.12.m3
  58.7 0.0 copy-start.2
  58.7 0.9 %shard_map.76 = f32[128,128]{1,0:T(8,128)S(1)} custom-call(s32[3]{0:T(128)S(1)} %pad_add_fusion.place, f32[8,128]{1,0:T(8,128)S(1)} %get-tuple-element.22.info, f32[8,768]{1,0:T(8,128)S(1)} %get-tuple-element.27.aux, f32[8,128]{1,0:T(8,128)S(1)} %get-tuple-element.28.tile, f32[32,768]{1,0:T(8,128)S(1)} %get-tuple-element.30.near, ...), custom_call_target="tpu_custom_call" | custom-call | flops 2000000000 | tf_op jit(solution)/shard_map/pallas_call | solution.py:387
  59.6 19.2 %all_to_all.10 = f32[128,1,128]{2,1,0:T(1,128)S(1)} all-to-all(f32[128,1,128]{2,1,0:T(1,128)S(1)} %bitcast.9), channel_id=1, replica_groups=mesh['gene'=16,'z'=4,'core'=2] {'gene','z','core'}, dimensions={0} | all-to-all | bytes 131072 | tf_op jit(solution)/shard_map/all_to_all | solution.py:478
  78.8 0.0 copy-done.2
  78.8 1.5 %shard_map.77 = (f32[2,128]{1,0:T(2,128)}, f32[1,2]{1,0:T(1,128)}) custom-call(s32[3]{0:T(128)S(1)} %pad_add_fusion.place, s32[32]{0:T(128)S(1)} %copy-done.2, f32[128,128]{1,0:T(8,128)S(1)} %bitcast.10), custom_call_target="tpu_custom_call" | custom-call | flops 2000000000 | tf_op jit(solution)/shard_map/pallas_call | solution.py:387
Async XLA Ops:
  0.6 12.8 %collective-permute-start = (s32[128,1280]{1,0:T(8,128)}, s32[128,1280]{1,0:T(8,128)S(1)}, u32[]{:S(2)}, u32[]{:S(2)}) collective-permute-start(s32[128,1280]{1,0:T(8,128)} %source.1), channel_id=1, source_target_pairs={{0,1},{1,0},{2,3},{3,2},{4,5},{5,4},{6,7},{7,6},{8,9},{9,8},{10,11... | collective-permute-start | bytes 1966088 | tf_op jit(solution)/shard_map/ppermute | solution.py:404
  2.1 11.4 %copy-start.1 = (s32[2,2]{1,0:T(2,128)S(1)}, s32[2,2]{1,0:T(2,128)}, u32[]{:S(2)}) copy-start(s32[2,2]{1,0:T(2,128)} %windows.1) | copy-start | bytes 52
  2.1 11.4 %all-to-all-start = ((f32[8,2,1280]{2,1,0:T(2,128)}), f32[8,2,1280]{2,1,0:T(2,128)S(1)}, u32[]{:S(2)}, u32[]{:S(2)}) async-start(f32[8,2,1280]{2,1,0:T(2,128)} %broadcast_in_dim.2), calls=%async_computation | async-start | bytes 163840 | tf_op jit(solution)/shard_map/all_to_all | solution.py:402
  7.7 34.6 %collective-permute-start.3 = (bf16[768,1280]{1,0:T(8,128)(2,1)}, bf16[768,1280]{1,0:T(8,128)(2,1)S(1)}, u32[]{:S(2)}, u32[]{:S(2)}) collective-permute-start(bf16[768,1280]{1,0:T(8,128)(2,1)} %refs_1_.1), channel_id=1, source_target_pairs={{0,1},{1,0},{2,3},{3,2},{4,5},{5,4},{6,7},{7,6},{8,9},{9,8},{10,11... | collective-permute-start | bytes 5898248 | tf_op jit(solution)/shard_map/ppermute | solution.py:405
  21.5 20.9 %collective-permute-start.1 = (bf16[64,2688]{1,0:T(8,128)(2,1)S(1)}, bf16[64,2688]{1,0:T(8,128)(2,1)S(1)}, u32[]{:S(2)}, u32[]{:S(2)}) collective-permute-start(bf16[64,2688]{1,0:T(8,128)(2,1)S(1)} %get-tuple-element.21.refs_1_), channel_id=1, source_target_pairs={{0,8},{8,16},{16,24},{24,32},{32,40},{40,48},{48,56},{56,64},{64,7... | collective-permute-start | bytes 1032200 | tf_op jit(solution)/shard_map/ppermute | solution.py:440
  23.1 19.3 %collective-permute-start.2 = (bf16[64,2688]{1,0:T(8,128)(2,1)S(1)}, bf16[64,2688]{1,0:T(8,128)(2,1)S(1)}, u32[]{:S(2)}, u32[]{:S(2)}) collective-permute-start(bf16[64,2688]{1,0:T(8,128)(2,1)S(1)} %get-tuple-element.21.refs_1_), channel_id=1, source_target_pairs={{8,0},{16,8},{24,16},{32,24},{40,32},{48,40},{56,48},{64,56},{72,6... | collective-permute-start | bytes 1032200 | tf_op jit(solution)/shard_map/ppermute | solution.py:441
  26.9 7.6 %copy-start = (bf16[768,1280]{1,0:T(8,128)(2,1)S(1)}, bf16[768,1280]{1,0:T(8,128)(2,1)}, u32[]{:S(2)}) copy-start(bf16[768,1280]{1,0:T(8,128)(2,1)} %refs_1_.1) | copy-start | bytes 5898244
  34.5 13.2 %collective-permute-start.8 = (bf16[64,2560]{1,0:T(8,128)(2,1)S(1)}, bf16[64,2560]{1,0:T(8,128)(2,1)S(1)}, u32[]{:S(2)}, u32[]{:S(2)}) collective-permute-start(bf16[64,2560]{1,0:T(8,128)(2,1)S(1)} %shard_map.73.refs_1_), channel_id=1, source_target_pairs={{0,8},{8,16},{16,24},{24,32},{32,40},{40,48},{48,56},{56,64},{64,7... | collective-permute-start | bytes 983048 | tf_op jit(solution)/shard_map/ppermute | solution.py:440
  35.8 1.2 %collective-permute-start.4 = (f32[8,768]{1,0:T(8,128)S(1)}, f32[8,768]{1,0:T(8,128)S(1)}, u32[]{:S(2)}, u32[]{:S(2)}) collective-permute-start(f32[8,768]{1,0:T(8,128)S(1)} %shard_map.70.refs_5_.stat.refs_4_.refs_3_), channel_id=1, source_target_pairs={{0,1},{1,0},{2,3},{3,2},{4,5},{5,4},{6,7},{7,6},{8,9},{9,8},{10,11... | collective-permute-start | bytes 73736 | tf_op jit(solution)/shard_map/ppermute | solution.py:421
  37.0 12.6 %collective-permute-start.9 = (bf16[64,2560]{1,0:T(8,128)(2,1)S(1)}, bf16[64,2560]{1,0:T(8,128)(2,1)S(1)}, u32[]{:S(2)}, u32[]{:S(2)}) collective-permute-start(bf16[64,2560]{1,0:T(8,128)(2,1)S(1)} %shard_map.73.refs_1_), channel_id=1, source_target_pairs={{8,0},{16,8},{24,16},{32,24},{40,32},{48,40},{56,48},{64,56},{72,6... | collective-permute-start | bytes 983048 | tf_op jit(solution)/shard_map/ppermute | solution.py:441
  44.0 9.8 %collective-permute-start.5 = (s16[64,896]{1,0:T(8,128)(2,1)S(1)}, s16[64,896]{1,0:T(8,128)(2,1)S(1)}, u32[]{:S(2)}, u32[]{:S(2)}) collective-permute-start(s16[64,896]{1,0:T(8,128)(2,1)S(1)} %get-tuple-element.24), channel_id=1, source_target_pairs={{0,2},{2,4},{4,6},{6,0},{1,3},{3,5},{5,7},{7,1},{8,10},{10,12},{12... | collective-permute-start | bytes 344072 | tf_op jit(solution)/shard_map/ppermute | solution.py:468
  44.6 11.3 %collective-permute-start.6 = (s16[64,896]{1,0:T(8,128)(2,1)S(1)}, s16[64,896]{1,0:T(8,128)(2,1)S(1)}, u32[]{:S(2)}, u32[]{:S(2)}) collective-permute-start(s16[64,896]{1,0:T(8,128)(2,1)S(1)} %get-tuple-element.25), channel_id=1, source_target_pairs={{0,4},{2,6},{4,0},{6,2},{1,5},{3,7},{5,1},{7,3},{8,12},{10,14},{12... | collective-permute-start | bytes 344072 | tf_op jit(solution)/shard_map/ppermute | solution.py:468
  46.7 9.3 %collective-permute-start.7 = (s16[64,896]{1,0:T(8,128)(2,1)S(1)}, s16[64,896]{1,0:T(8,128)(2,1)S(1)}, u32[]{:S(2)}, u32[]{:S(2)}) collective-permute-start(s16[64,896]{1,0:T(8,128)(2,1)S(1)} %get-tuple-element.26), channel_id=1, source_target_pairs={{0,6},{2,0},{4,2},{6,4},{1,7},{3,1},{5,3},{7,5},{8,14},{10,8},{12,... | collective-permute-start | bytes 344072 | tf_op jit(solution)/shard_map/ppermute | solution.py:468
  51.1 6.9 %collective-permute-start.10 = (s16[48,896]{1,0:T(8,128)(2,1)S(1)}, s16[48,896]{1,0:T(8,128)(2,1)S(1)}, u32[]{:S(2)}, u32[]{:S(2)}) collective-permute-start(s16[48,896]{1,0:T(8,128)(2,1)S(1)} %get-tuple-element.35), channel_id=1, source_target_pairs={{0,2},{2,4},{4,6},{6,0},{1,3},{3,5},{5,7},{7,1},{8,10},{10,12},{12... | collective-permute-start | bytes 258056 | tf_op jit(solution)/shard_map/ppermute | solution.py:468
  51.8 6.2 %collective-permute-start.11 = (s16[48,896]{1,0:T(8,128)(2,1)S(1)}, s16[48,896]{1,0:T(8,128)(2,1)S(1)}, u32[]{:S(2)}, u32[]{:S(2)}) collective-permute-start(s16[48,896]{1,0:T(8,128)(2,1)S(1)} %get-tuple-element.36), channel_id=1, source_target_pairs={{0,4},{2,6},{4,0},{6,2},{1,5},{3,7},{5,1},{7,3},{8,12},{10,14},{12... | collective-permute-start | bytes 258056 | tf_op jit(solution)/shard_map/ppermute | solution.py:468
  53.8 4.8 %collective-permute-start.12 = (s16[48,896]{1,0:T(8,128)(2,1)S(1)}, s16[48,896]{1,0:T(8,128)(2,1)S(1)}, u32[]{:S(2)}, u32[]{:S(2)}) collective-permute-start(s16[48,896]{1,0:T(8,128)(2,1)S(1)} %get-tuple-element.37), channel_id=1, source_target_pairs={{0,6},{2,0},{4,2},{6,4},{1,7},{3,1},{5,3},{7,5},{8,14},{10,8},{12,... | collective-permute-start | bytes 258056 | tf_op jit(solution)/shard_map/ppermute | solution.py:468
  58.7 20.1 %copy-start.2 = (s32[32]{0:T(128)S(1)}, s32[32]{0:T(128)}, u32[]{:S(2)}) copy-start(s32[32]{0:T(128)} %order.1) | copy-start | bytes 388

commit v10 on v9

--- a/solution.py
+++ b/solution.py
@@ -76,31 +76,31 @@
     )[:1]
 
 
-def fetch_kernel(source, out, done):
-    copy = pltpu.make_async_copy(source, out, done)
-    copy.start()
-    copy.wait()
-
-
-def moments_kernel(dosage, out, sums):
+def fetch_kernel(perms, dosage, near, out, kept, sums, done):
     variants, width = dosage.shape
-
-    def step(i, carry):
-        rows = pl.ds(pl.multiple_of(i * LANES, LANES), LANES)
+    pieces = variants // LANES
+    copies = []
+    for i in range(pieces):
+        rows = pl.ds(i * LANES, LANES)
+        copies.append(pltpu.make_async_copy(dosage.at[rows], kept.at[rows], done.at[i]))
+    copies.append(pltpu.make_async_copy(perms, near, done.at[pieces]))
+    for copy in copies:
+        copy.start()
+    for i in range(pieces):
+        copies[i].wait()
+        rows = slice(i * LANES, (i + 1) * LANES)
         total = jnp.zeros((LANES, LANES), jnp.float32)
         square = jnp.zeros((LANES, LANES), jnp.float32)
         for k in range(width // LANES):
-            v = dosage[rows, k * LANES : (k + 1) * LANES].astype(jnp.float32)
+            v = kept[rows, k * LANES : (k + 1) * LANES].astype(jnp.float32)
             total = total + v
             square = square + v * v
         sums[0, rows, :] = total
         sums[1, rows, :] = square
-        return carry
-
-    lax.fori_loop(0, variants // LANES, step, 0)
     out[...] = jnp.zeros_like(out)
     for j in range(2):
         out[j : j + 1, :] = lane_sums(sums[j])
+    copies[pieces].wait()
 
 
 def first_kernel(place, windows, every, perms, theirs, out, table):
@@ -181,12 +181,10 @@
     return mean, jnp.sqrt(jnp.maximum(square - total * mean, 0.0) + count * epsilon)
 
 
-def sums_kernel(count, with_direct, held, *refs):
+def sums_kernel(count, with_direct, *refs):
     blocks = refs[:count]
     dosage, theirs, stat, their_stat = refs[count : count + 4]
-    earlier = refs[count + 4 : count + 4 + held]
-    own, m1, m2, m3 = refs[count + 4 + held : count + 8 + held]
-    start = earlier[0].shape[0] if held else 0
+    own, m1, m2, m3 = refs[count + 4 : count + 8]
     variants, width = dosage.shape
     stat = stat[...] + their_stat[...]
     rows = jnp.concatenate([block[:, : 2 * width] for block in blocks], axis=0)
@@ -220,15 +218,13 @@
         return to_int16(jnp.where(lane == 0, code, line))
 
     code = bound_code(jnp.max(largest, keepdims=True))
-    for message, before in zip((m1, m2, m3), earlier):
-        message[:start, :] = before[...]
     for k, message in enumerate((m1, m2, m3)):
         for t in range(count):
             pair = [at(2 * t, k + 1), at(2 * t + 1, k + 1)]
             values = jnp.concatenate([got[p] for p in pair], axis=0)
             columns = jnp.concatenate([column[p] for p in pair], axis=0)
-            message[start + t * TILE : start + (t + 1) * TILE, :variants] = to_int16(coded(values, code))
-            message[start + t * TILE : start + (t + 1) * TILE, variants:] = beside(code, columns)
+            message[t * TILE : (t + 1) * TILE, :variants] = to_int16(coded(values, code))
+            message[t * TILE : (t + 1) * TILE, variants:] = beside(code, columns)
     if with_direct:
         spots = slice(4 * count * TILE, 4 * count * TILE + HALF)
         own[48:56, :] = both[spots]
@@ -247,8 +243,8 @@
             info[o : o + 1, :] = e[2 * tiles : 2 * tiles + 1] * 128.0 + e[2 * tiles + 1 : 2 * tiles + 2]
 
 
-def added(owns, messages, means, sizes):
-    total = jnp.concatenate([own[...] for own in owns], axis=0)
+def added(own, messages, means, sizes):
+    total = own[...]
     rows, variants = total.shape
     for message, mean, size in zip(messages, means, sizes):
         side = message[:rows, variants:].astype(jnp.int32).astype(jnp.float32)
@@ -301,7 +297,7 @@
         aux[1 + q : 2 + q, :] = means[q]
         aux[4 + q : 5 + q, :] = sizes[q]
     aux[7:8, :] = jnp.zeros_like(scale)
-    sums = added((own,), (m1, m2, m3), means, sizes) * scale
+    sums = added(own, (m1, m2, m3), means, sizes) * scale
     inside = list(inside_rows(place, info, variants))
     tile = best_tile(jnp.zeros((HALF, LANES), jnp.float32), 0, sums, inside)
     lane = lax.broadcasted_iota(jnp.int32, (HALF, LANES), 1)
@@ -312,11 +308,11 @@
     out[...] = tile
 
 
-def maxima_kernel(place, info, aux, tile, near, far, m1, m2, m3, out):
-    variants = near.shape[1]
+def maxima_kernel(place, info, aux, tile, own, m1, m2, m3, out):
+    variants = own.shape[1]
     means = [aux[1 + q : 2 + q, :] for q in range(3)]
     sizes = [aux[4 + q : 5 + q, :] for q in range(3)]
-    sums = added((near, far), (m1, m2, m3), means, sizes) * aux[0:1, :]
+    sums = added(own, (m1, m2, m3), means, sizes) * aux[0:1, :]
     tile = best_tile(tile[...], 1, sums, inside_rows(place, info, variants))
     lane = lax.broadcasted_iota(jnp.int32, (HALF, LANES), 1)
     row = lax.broadcasted_iota(jnp.int32, (HALF, LANES), 0)
@@ -403,20 +399,17 @@
     mates = [(0, 1), (1, 0)]
     their_perms = lax.ppermute(perms, "core", mates)
     theirs = lax.ppermute(dosage, "core", mates)
-    near_perms = call(
+    near_perms, stat = call(
         fetch_kernel,
-        shape(perms.shape, jnp.int32),
-        [perms],
-        1,
-        [pltpu.SemaphoreType.DMA],
-        remote=(0,),
-    )
-    stat = call(
-        moments_kernel,
-        shape((8, variants)),
-        [dosage],
+        [shape(perms.shape, jnp.int32), shape((8, variants))],
+        [perms, dosage],
         2,
-        [pltpu.VMEM((2, variants, LANES), jnp.float32)],
+        [
+            pltpu.VMEM((variants, width), jnp.bfloat16),
+            pltpu.VMEM((2, variants, LANES), jnp.float32),
+            pltpu.SemaphoreType.DMA((variants // LANES + 1,)),
+        ],
+        remote=(0, 1),
     )
     their_stat = lax.ppermute(stat, "core", mates)
 
@@ -444,26 +437,19 @@
         codes = lambda rows: [shape((rows, wide), jnp.int16)] * 3
         if h == 0:
             mine, *parts, info = call(
-                functools.partial(sums_kernel, 3, True, 0),
+                functools.partial(sums_kernel, 3, True),
                 [shape((56, variants)), *codes(64), shape((8, LANES))],
                 [left, own, right, *common],
                 2,
             )
-            group = [mine]
         else:
-            near, *parts = call(
-                functools.partial(sums_kernel, 2, False, 0),
-                [shape((32, variants)), *codes(32)],
-                [left, own, *common],
-                1,
+            mine, *parts = call(
+                functools.partial(sums_kernel, 3, False),
+                [shape((48, variants)), *codes(48)],
+                [left, own, right, *common],
+                2,
             )
-            far, *parts = call(
-                functools.partial(sums_kernel, 1, False, 3),
-                [shape((16, variants)), *codes(48)],
-                [right, *common, *parts],
-                1,
-            )
-            group = [near, far]
+        group = [mine]
         for k in range(1, 4):
             group.append(lax.ppermute(parts[k - 1], "z", [(i, (i + k) % 4) for i in range(4)]))
         sums.append(group)

time: 80.8 us -> 77.3 us (0.957)
  Pallas kernels: 25.9 us -> 24.4 us
  starting transfers between devices: 25.6 us -> 24.6 us
    ppermute x2, waiting for transfers between devices: 0.01 us -> 1.64 us  [on_device(): left = lax.ppermute(own, 'gene', ahead)]
    pallas_call x10 -> x8, Pallas kernels: 25.9 us -> 24.4 us  [call(): return made(*args)]
    all_to_all x1, waiting for transfers between devices: 4.02 us -> 2.7 us  [on_device(): every = lax.all_to_all(copies, ('z', 'core'), 0, 0, tiled=True)]
    ppermute x1, waiting for transfers between devices: 1.2 us -> 0.01 us  [on_device(): their_stat = lax.ppermute(stat, 'core', mates)]
    ppermute x6, waiting for transfers between devices: 1.73 us -> 2.73 us  [on_device(): lax.ppermute(parts[k - 1], 'z', [(i, (i + k) % 4) for i in range(4)])]
    ppermute x6, starting transfers between devices: 8.52 us -> 7.52 us  [on_device(): lax.ppermute(parts[k - 1], 'z', [(i, (i + k) % 4) for i in range(4)])]
where the time goes in v10:
time: 77.3 us; the launch traced here: 76.8 us
  starting transfers between devices  24.6 us (32%)
  Pallas kernels  24.4 us (32%)
  blocking collectives  18.5 us (24%)
  waiting for transfers between devices  7.08 us (9%)
  local copies, waits for them, and re-layouts  1.37 us (2%)
    pallas_call x8, Pallas kernels, call(): return made(*args)  24.4 us
    all_to_all x1, blocking collectives, on_device(): lax.all_to_all(lines.reshape(everyone, 1, LANES), ('gene', 'z', 'core'),...  18.5 us
    ppermute x2, starting transfers between devices, on_device(): right = lax.ppermute(own, 'gene', back)  9.18 us
    ppermute x6, starting transfers between devices, on_device(): lax.ppermute(parts[k - 1], 'z', [(i, (i + k) % 4) for i in range(4)])  7.52 us
    all_to_all x1, starting transfers between devices, on_device(): every = lax.all_to_all(copies, ('z', 'core'), 0, 0, tiled=True)  5.52 us
    ppermute x6, waiting for transfers between devices, on_device(): lax.ppermute(parts[k - 1], 'z', [(i, (i + k) % 4) for i in range(4)])  2.73 us
    all_to_all x1, waiting for transfers between devices, on_device(): every = lax.all_to_all(copies, ('z', 'core'), 0, 0, tiled=True)  2.7 us
    ppermute x2, waiting for transfers between devices, on_device(): left = lax.ppermute(own, 'gene', ahead)  1.64 us
  transfers between devices with their start and end apart: 14, of which 5 were waited for; matrix products, arithmetic and copies ran while one was open for 2% of the time, Pallas kernels for 29%

profile of v10, /device:TPU:0, one launch (start us, length us, event | category | flops | bytes accessed | tf_op | source)
XLA Modules:
  0.0 76.8 jit_solution(6370518950245439910)
XLA Ops:
  0.6 0.1 collective-permute-start
  0.7 1.4 %broadcast_in_dim.2 = f32[8,2,1280]{2,1,0:T(2,128)} broadcast(f32[2,1280]{1,0:T(2,128)} %bitcast.11), dimensions={1,2} | broadcast | bytes 92160 | tf_op jit(solution)/shard_map/broadcast_in_dim | solution.py:397
  2.1 5.5 %all-to-all-start = ((f32[8,2,1280]{2,1,0:T(2,128)}), f32[8,2,1280]{2,1,0:T(2,128)S(1)}, u32[]{:S(2)}, u32[]{:S(2)}) async-start(f32[8,2,1280]{2,1,0:T(2,128)} %broadcast_in_dim.2), calls=%async_computation | async-start | bytes 163840 | tf_op jit(solution)/shard_map/all_to_all | solution.py:398
  7.6 0.0 copy-start.1
  7.6 0.5 collective-permute-start.3
  8.1 2.3 %shard_map.68 = (s32[128,1280]{1,0:T(8,128)S(1)}, f32[8,768]{1,0:T(8,128)S(1)}) custom-call(s32[128,1280]{1,0:T(8,128)} %perms.1, bf16[768,1280]{1,0:T(8,128)(2,1)} %refs_3_.3), custom_call_target="tpu_custom_call" | custom-call | flops 2000000000 | tf_op jit(solution)/shard_map/pallas_call | solution.py:383
  10.4 0.2 collective-permute-start.4
  10.5 0.1 pad_add_fusion.place
  10.6 2.7 %all-to-all-done.every = f32[8,2,1280]{2,1,0:T(2,128)S(1)} async-done(((f32[8,2,1280]{2,1,0:T(2,128)}), f32[8,2,1280]{2,1,0:T(2,128)S(1)}, u32[]{:S(2)}, u32[]{:S(2)}) %all-to-all-start) | async-done | bytes 81952 | tf_op jit(solution)/shard_map/all_to_all | solution.py:398
  13.3 0.0 collective-permute-done.theirs
  13.3 0.0 copy-done.1
  13.3 8.0 %shard_map.69 = (bf16[64,2688]{1,0:T(8,128)(2,1)S(1)}, bf16[2,80,16,128]{3,2,1,0:T(8,128)(2,1)S(1)}) custom-call(s32[3]{0:T(128)S(1)} %pad_add_fusion.place, s32[2,2]{1,0:T(2,128)S(1)} %copy-done.1, f32[8,2,1280]{2,1,0:T(2,128)S(1)} %all-to-all-done.every, s32[128,1280]{1,0:T(8,128)S(1)} %get-tuple-element.19.perms, s32[128,1280]{1,0:T(8,128)S(1)} %collective-permute-done.theirs), custom_call_target="tpu_custom_call" | custom-call | flops 8999999488 | tf_op jit(solution)/shard_map/pallas_call | solution.py:383
  21.4 1.6 %collective-permute-start.1 = (bf16[64,2688]{1,0:T(8,128)(2,1)S(1)}, bf16[64,2688]{1,0:T(8,128)(2,1)S(1)}, u32[]{:S(2)}, u32[]{:S(2)}) collective-permute-start(bf16[64,2688]{1,0:T(8,128)(2,1)S(1)} %get-tuple-element.20.refs_1_), channel_id=1, source_target_pairs={{0,8},{8,16},{16,24},{24,32},{32,40},{40,48},{48,56},{56,64},{64,7... | collective-permute-start | bytes 1032200 | tf_op jit(solution)/shard_map/ppermute | solution.py:433
  22.9 3.9 %collective-permute-start.2 = (bf16[64,2688]{1,0:T(8,128)(2,1)S(1)}, bf16[64,2688]{1,0:T(8,128)(2,1)S(1)}, u32[]{:S(2)}, u32[]{:S(2)}) collective-permute-start(bf16[64,2688]{1,0:T(8,128)(2,1)S(1)} %get-tuple-element.20.refs_1_), channel_id=1, source_target_pairs={{8,0},{16,8},{24,16},{32,24},{40,32},{48,40},{56,48},{64,56},{72,6... | collective-permute-start | bytes 1032200 | tf_op jit(solution)/shard_map/ppermute | solution.py:434
  26.8 0.0 copy-start
  26.8 7.6 %shard_map.72.refs_1_ = bf16[64,2560]{1,0:T(8,128)(2,1)S(1)} custom-call(s32[3]{0:T(128)S(1)} %pad_add_fusion.place, s32[128,1280]{1,0:T(8,128)S(1)} %get-tuple-element.19.perms, s32[128,1280]{1,0:T(8,128)S(1)} %collective-permute-done.theirs, bf16[2,80,16,128]{3,2,1,0:T(8,128)(2,1)S(1)} %get-tuple-element.29.table), custom_call_target="tpu_custom_call" | custom-call | flops 8000000000 | tf_op jit(solution)/shard_map/pallas_call | solution.py:383
  34.3 0.1 collective-permute-start.8
  34.4 0.0 collective-permute-done.4.refs_6_.their_stat
  34.4 5.3 %collective-permute-start.9 = (bf16[64,2560]{1,0:T(8,128)(2,1)S(1)}, bf16[64,2560]{1,0:T(8,128)(2,1)S(1)}, u32[]{:S(2)}, u32[]{:S(2)}) collective-permute-start(bf16[64,2560]{1,0:T(8,128)(2,1)S(1)} %shard_map.72.refs_1_), channel_id=1, source_target_pairs={{8,0},{16,8},{24,16},{32,24},{40,32},{48,40},{56,48},{64,56},{72,6... | collective-permute-start | bytes 983048 | tf_op jit(solution)/shard_map/ppermute | solution.py:434
  39.7 0.0 collective-permute-done.1.refs_0_
  39.8 0.0 collective-permute-done.2.refs_2_
  39.8 0.0 collective-permute-done.3.refs_4_
  39.8 0.0 copy-done
  39.8 1.6 %shard_map.70 = (f32[56,768]{1,0:T(8,128)S(1)}, s16[64,896]{1,0:T(8,128)(2,1)S(1)}, s16[64,896]{1,0:T(8,128)(2,1)S(1)}, s16[64,896]{1,0:T(8,128)(2,1)S(1)}, f32[8,128]{1,0:T(8,128)S(1)}) custom-call(bf16[64,2688]{1,0:T(8,128)(2,1)S(1)} %collective-permute-done.1.refs_0_, bf16[64,2688]{1,0:T(8,128)(2,1)S(1)} %get-tuple-element.20.refs_1_, ...), custom_call_target="tpu_custom_call" | custom-call | flops 2000000000 | tf_op jit(solution)/shard_map/pallas_call | solution.py:383
  41.4 0.6 collective-permute-start.5
  42.0 2.1 %collective-permute-start.6 = (s16[64,896]{1,0:T(8,128)(2,1)S(1)}, s16[64,896]{1,0:T(8,128)(2,1)S(1)}, u32[]{:S(2)}, u32[]{:S(2)}) collective-permute-start(s16[64,896]{1,0:T(8,128)(2,1)S(1)} %get-tuple-element.25), channel_id=1, source_target_pairs={{0,4},{2,6},{4,0},{6,2},{1,5},{3,7},{5,1},{7,3},{8,12},{10,14},{12... | collective-permute-start | bytes 344072 | tf_op jit(solution)/shard_map/ppermute | solution.py:454
  44.1 1.0 %collective-permute-start.7 = (s16[64,896]{1,0:T(8,128)(2,1)S(1)}, s16[64,896]{1,0:T(8,128)(2,1)S(1)}, u32[]{:S(2)}, u32[]{:S(2)}) collective-permute-start(s16[64,896]{1,0:T(8,128)(2,1)S(1)} %get-tuple-element.26), channel_id=1, source_target_pairs={{0,6},{2,0},{4,2},{6,4},{1,7},{3,1},{5,3},{7,5},{8,14},{10,8},{12,... | collective-permute-start | bytes 344072 | tf_op jit(solution)/shard_map/ppermute | solution.py:454
  45.1 1.6 %collective-permute-done.8.refs_0_ = bf16[64,2560]{1,0:T(8,128)(2,1)S(1)} collective-permute-done((bf16[64,2560]{1,0:T(8,128)(2,1)S(1)}, bf16[64,2560]{1,0:T(8,128)(2,1)S(1)}, u32[]{:S(2)}, u32[]{:S(2)}) %collective-permute-start.8) | collective-permute-done | bytes 327712 | tf_op jit(solution)/shard_map/ppermute | solution.py:433
  46.7 0.0 collective-permute-done.9.refs_2_
  46.7 1.6 %shard_map.73 = (f32[48,768]{1,0:T(8,128)S(1)}, s16[48,896]{1,0:T(8,128)(2,1)S(1)}, s16[48,896]{1,0:T(8,128)(2,1)S(1)}, s16[48,896]{1,0:T(8,128)(2,1)S(1)}) custom-call(bf16[64,2560]{1,0:T(8,128)(2,1)S(1)} %collective-permute-done.8.refs_0_, bf16[64,2560]{1,0:T(8,128)(2,1)S(1)} %shard_map.72.refs_1_, bf16[64,2560]{1,0:T(8,128)(2,1)S(1)} %collective-permute-done.9.refs_2_, ...), custom_call_target="tpu_custom_call" | custom-call | flops 2000000000 | tf_op jit(solution)/shard_map/pallas_call | solution.py:383
  48.4 0.6 collective-permute-start.10
  49.0 2.1 %collective-permute-start.11 = (s16[48,896]{1,0:T(8,128)(2,1)S(1)}, s16[48,896]{1,0:T(8,128)(2,1)S(1)}, u32[]{:S(2)}, u32[]{:S(2)}) collective-permute-start(s16[48,896]{1,0:T(8,128)(2,1)S(1)} %get-tuple-element.32), channel_id=1, source_target_pairs={{0,4},{2,6},{4,0},{6,2},{1,5},{3,7},{5,1},{7,3},{8,12},{10,14},{12... | collective-permute-start | bytes 258056 | tf_op jit(solution)/shard_map/ppermute | solution.py:454
  51.1 0.0 collective-permute-done.5.m1
  51.1 1.2 %collective-permute-start.12 = (s16[48,896]{1,0:T(8,128)(2,1)S(1)}, s16[48,896]{1,0:T(8,128)(2,1)S(1)}, u32[]{:S(2)}, u32[]{:S(2)}) collective-permute-start(s16[48,896]{1,0:T(8,128)(2,1)S(1)} %get-tuple-element.33), channel_id=1, source_target_pairs={{0,6},{2,0},{4,2},{6,4},{1,7},{3,1},{5,3},{7,5},{8,14},{10,8},{12,... | collective-permute-start | bytes 258056 | tf_op jit(solution)/shard_map/ppermute | solution.py:454
  52.2 0.0 collective-permute-done.6.m2
  52.2 0.0 collective-permute-done.7.m3
  52.2 1.0 %shard_map.71 = (f32[8,128]{1,0:T(8,128)S(1)}, f32[8,768]{1,0:T(8,128)S(1)}) custom-call(s32[3]{0:T(128)S(1)} %pad_add_fusion.place, f32[8,128]{1,0:T(8,128)S(1)} %get-tuple-element.22.info, f32[8,768]{1,0:T(8,128)S(1)} %get-tuple-element.21.refs_5_.stat, f32[8,768]{1,0:T(8,128)S(1)} %collective-permute-done.4.refs_6_.their_stat, ...), custom_call_target="tpu_custom_call" | custom-call | flops 1000000000 | tf_op jit(solution)/shard_map/pallas_call | solution.py:383
  53.2 1.0 %collective-permute-done.10.m1 = s16[48,896]{1,0:T(8,128)(2,1)S(1)} collective-permute-done((s16[48,896]{1,0:T(8,128)(2,1)S(1)}, s16[48,896]{1,0:T(8,128)(2,1)S(1)}, u32[]{:S(2)}, u32[]{:S(2)}) %collective-permute-start.10) | collective-permute-done | bytes 86048 | tf_op jit(solution)/shard_map/ppermute | solution.py:454
  54.1 0.9 %collective-permute-done.11.m2 = s16[48,896]{1,0:T(8,128)(2,1)S(1)} collective-permute-done((s16[48,896]{1,0:T(8,128)(2,1)S(1)}, s16[48,896]{1,0:T(8,128)(2,1)S(1)}, u32[]{:S(2)}, u32[]{:S(2)}) %collective-permute-start.11) | collective-permute-done | bytes 86048 | tf_op jit(solution)/shard_map/ppermute | solution.py:454
  55.0 0.9 %collective-permute-done.12.m3 = s16[48,896]{1,0:T(8,128)(2,1)S(1)} collective-permute-done((s16[48,896]{1,0:T(8,128)(2,1)S(1)}, s16[48,896]{1,0:T(8,128)(2,1)S(1)}, u32[]{:S(2)}, u32[]{:S(2)}) %collective-permute-start.12) | collective-permute-done | bytes 86048 | tf_op jit(solution)/shard_map/ppermute | solution.py:454
  55.9 0.0 copy-start.2
  55.9 0.9 %shard_map.74 = f32[128,128]{1,0:T(8,128)S(1)} custom-call(s32[3]{0:T(128)S(1)} %pad_add_fusion.place, f32[8,128]{1,0:T(8,128)S(1)} %get-tuple-element.22.info, f32[8,768]{1,0:T(8,128)S(1)} %get-tuple-element.27.aux, f32[8,128]{1,0:T(8,128)S(1)} %get-tuple-element.28.tile, f32[48,768]{1,0:T(8,128)S(1)} %get-tuple-element.30.own, ...), custom_call_target="tpu_custom_call" | custom-call | flops 2000000000 | tf_op jit(solution)/shard_map/pallas_call | solution.py:383
  56.8 18.5 %all_to_all.10 = f32[128,1,128]{2,1,0:T(1,128)S(1)} all-to-all(f32[128,1,128]{2,1,0:T(1,128)S(1)} %bitcast.9), channel_id=1, replica_groups=mesh['gene'=16,'z'=4,'core'=2] {'gene','z','core'}, dimensions={0} | all-to-all | bytes 131072 | tf_op jit(solution)/shard_map/all_to_all | solution.py:464
  75.3 0.0 copy-done.2
  75.3 1.5 %shard_map.75 = (f32[2,128]{1,0:T(2,128)}, f32[1,2]{1,0:T(1,128)}) custom-call(s32[3]{0:T(128)S(1)} %pad_add_fusion.place, s32[32]{0:T(128)S(1)} %copy-done.2, f32[128,128]{1,0:T(8,128)S(1)} %bitcast.10), custom_call_target="tpu_custom_call" | custom-call | flops 2000000000 | tf_op jit(solution)/shard_map/pallas_call | solution.py:383
Async XLA Ops:
  0.6 12.7 %collective-permute-start = (s32[128,1280]{1,0:T(8,128)}, s32[128,1280]{1,0:T(8,128)S(1)}, u32[]{:S(2)}, u32[]{:S(2)}) collective-permute-start(s32[128,1280]{1,0:T(8,128)} %perms.1), channel_id=1, source_target_pairs={{0,1},{1,0},{2,3},{3,2},{4,5},{5,4},{6,7},{7,6},{8,9},{9,8},{10,11... | collective-permute-start | bytes 1966088 | tf_op jit(solution)/shard_map/ppermute | solution.py:400
  2.1 11.2 %all-to-all-start = ((f32[8,2,1280]{2,1,0:T(2,128)}), f32[8,2,1280]{2,1,0:T(2,128)S(1)}, u32[]{:S(2)}, u32[]{:S(2)}) async-start(f32[8,2,1280]{2,1,0:T(2,128)} %broadcast_in_dim.2), calls=%async_computation | async-start | bytes 163840 | tf_op jit(solution)/shard_map/all_to_all | solution.py:398
  7.6 5.7 %copy-start.1 = (s32[2,2]{1,0:T(2,128)S(1)}, s32[2,2]{1,0:T(2,128)}, u32[]{:S(2)}) copy-start(s32[2,2]{1,0:T(2,128)} %windows.1) | copy-start | bytes 52
  7.6 32.1 %collective-permute-start.3 = (bf16[768,1280]{1,0:T(8,128)(2,1)}, bf16[768,1280]{1,0:T(8,128)(2,1)S(1)}, u32[]{:S(2)}, u32[]{:S(2)}) collective-permute-start(bf16[768,1280]{1,0:T(8,128)(2,1)} %refs_3_.3), channel_id=1, source_target_pairs={{0,1},{1,0},{2,3},{3,2},{4,5},{5,4},{6,7},{7,6},{8,9},{9,8},{10,11... | collective-permute-start | bytes 5898248 | tf_op jit(solution)/shard_map/ppermute | solution.py:401
  10.4 24.0 %collective-permute-start.4 = (f32[8,768]{1,0:T(8,128)S(1)}, f32[8,768]{1,0:T(8,128)S(1)}, u32[]{:S(2)}, u32[]{:S(2)}) collective-permute-start(f32[8,768]{1,0:T(8,128)S(1)} %get-tuple-element.21.refs_5_.stat), channel_id=1, source_target_pairs={{0,1},{1,0},{2,3},{3,2},{4,5},{5,4},{6,7},{7,6},{8,9},{9,8},{10,11... | collective-permute-start | bytes 73736 | tf_op jit(solution)/shard_map/ppermute | solution.py:414
  21.4 18.4 %collective-permute-start.1 = (bf16[64,2688]{1,0:T(8,128)(2,1)S(1)}, bf16[64,2688]{1,0:T(8,128)(2,1)S(1)}, u32[]{:S(2)}, u32[]{:S(2)}) collective-permute-start(bf16[64,2688]{1,0:T(8,128)(2,1)S(1)} %get-tuple-element.20.refs_1_), channel_id=1, source_target_pairs={{0,8},{8,16},{16,24},{24,32},{32,40},{40,48},{48,56},{56,64},{64,7... | collective-permute-start | bytes 1032200 | tf_op jit(solution)/shard_map/ppermute | solution.py:433
  22.9 16.8 %collective-permute-start.2 = (bf16[64,2688]{1,0:T(8,128)(2,1)S(1)}, bf16[64,2688]{1,0:T(8,128)(2,1)S(1)}, u32[]{:S(2)}, u32[]{:S(2)}) collective-permute-start(bf16[64,2688]{1,0:T(8,128)(2,1)S(1)} %get-tuple-element.20.refs_1_), channel_id=1, source_target_pairs={{8,0},{16,8},{24,16},{32,24},{40,32},{48,40},{56,48},{64,56},{72,6... | collective-permute-start | bytes 1032200 | tf_op jit(solution)/shard_map/ppermute | solution.py:434
  26.8 13.0 %copy-start = (bf16[768,1280]{1,0:T(8,128)(2,1)S(1)}, bf16[768,1280]{1,0:T(8,128)(2,1)}, u32[]{:S(2)}) copy-start(bf16[768,1280]{1,0:T(8,128)(2,1)} %refs_3_.3) | copy-start | bytes 5898244
  34.3 12.4 %collective-permute-start.8 = (bf16[64,2560]{1,0:T(8,128)(2,1)S(1)}, bf16[64,2560]{1,0:T(8,128)(2,1)S(1)}, u32[]{:S(2)}, u32[]{:S(2)}) collective-permute-start(bf16[64,2560]{1,0:T(8,128)(2,1)S(1)} %shard_map.72.refs_1_), channel_id=1, source_target_pairs={{0,8},{8,16},{16,24},{24,32},{32,40},{40,48},{48,56},{56,64},{64,7... | collective-permute-start | bytes 983048 | tf_op jit(solution)/shard_map/ppermute | solution.py:433
  34.4 12.3 %collective-permute-start.9 = (bf16[64,2560]{1,0:T(8,128)(2,1)S(1)}, bf16[64,2560]{1,0:T(8,128)(2,1)S(1)}, u32[]{:S(2)}, u32[]{:S(2)}) collective-permute-start(bf16[64,2560]{1,0:T(8,128)(2,1)S(1)} %shard_map.72.refs_1_), channel_id=1, source_target_pairs={{8,0},{16,8},{24,16},{32,24},{40,32},{48,40},{56,48},{64,56},{72,6... | collective-permute-start | bytes 983048 | tf_op jit(solution)/shard_map/ppermute | solution.py:434
  41.4 9.6 %collective-permute-start.5 = (s16[64,896]{1,0:T(8,128)(2,1)S(1)}, s16[64,896]{1,0:T(8,128)(2,1)S(1)}, u32[]{:S(2)}, u32[]{:S(2)}) collective-permute-start(s16[64,896]{1,0:T(8,128)(2,1)S(1)} %get-tuple-element.24), channel_id=1, source_target_pairs={{0,2},{2,4},{4,6},{6,0},{1,3},{3,5},{5,7},{7,1},{8,10},{10,12},{12... | collective-permute-start | bytes 344072 | tf_op jit(solution)/shard_map/ppermute | solution.py:454
  42.0 10.2 %collective-permute-start.6 = (s16[64,896]{1,0:T(8,128)(2,1)S(1)}, s16[64,896]{1,0:T(8,128)(2,1)S(1)}, u32[]{:S(2)}, u32[]{:S(2)}) collective-permute-start(s16[64,896]{1,0:T(8,128)(2,1)S(1)} %get-tuple-element.25), channel_id=1, source_target_pairs={{0,4},{2,6},{4,0},{6,2},{1,5},{3,7},{5,1},{7,3},{8,12},{10,14},{12... | collective-permute-start | bytes 344072 | tf_op jit(solution)/shard_map/ppermute | solution.py:454
  44.1 8.1 %collective-permute-start.7 = (s16[64,896]{1,0:T(8,128)(2,1)S(1)}, s16[64,896]{1,0:T(8,128)(2,1)S(1)}, u32[]{:S(2)}, u32[]{:S(2)}) collective-permute-start(s16[64,896]{1,0:T(8,128)(2,1)S(1)} %get-tuple-element.26), channel_id=1, source_target_pairs={{0,6},{2,0},{4,2},{6,4},{1,7},{3,1},{5,3},{7,5},{8,14},{10,8},{12,... | collective-permute-start | bytes 344072 | tf_op jit(solution)/shard_map/ppermute | solution.py:454
  48.4 5.8 %collective-permute-start.10 = (s16[48,896]{1,0:T(8,128)(2,1)S(1)}, s16[48,896]{1,0:T(8,128)(2,1)S(1)}, u32[]{:S(2)}, u32[]{:S(2)}) collective-permute-start(s16[48,896]{1,0:T(8,128)(2,1)S(1)} %get-tuple-element.31), channel_id=1, source_target_pairs={{0,2},{2,4},{4,6},{6,0},{1,3},{3,5},{5,7},{7,1},{8,10},{10,12},{12... | collective-permute-start | bytes 258056 | tf_op jit(solution)/shard_map/ppermute | solution.py:454
  49.0 6.1 %collective-permute-start.11 = (s16[48,896]{1,0:T(8,128)(2,1)S(1)}, s16[48,896]{1,0:T(8,128)(2,1)S(1)}, u32[]{:S(2)}, u32[]{:S(2)}) collective-permute-start(s16[48,896]{1,0:T(8,128)(2,1)S(1)} %get-tuple-element.32), channel_id=1, source_target_pairs={{0,4},{2,6},{4,0},{6,2},{1,5},{3,7},{5,1},{7,3},{8,12},{10,14},{12... | collective-permute-start | bytes 258056 | tf_op jit(solution)/shard_map/ppermute | solution.py:454
  51.1 4.8 %collective-permute-start.12 = (s16[48,896]{1,0:T(8,128)(2,1)S(1)}, s16[48,896]{1,0:T(8,128)(2,1)S(1)}, u32[]{:S(2)}, u32[]{:S(2)}) collective-permute-start(s16[48,896]{1,0:T(8,128)(2,1)S(1)} %get-tuple-element.33), channel_id=1, source_target_pairs={{0,6},{2,0},{4,2},{6,4},{1,7},{3,1},{5,3},{7,5},{8,14},{10,8},{12,... | collective-permute-start | bytes 258056 | tf_op jit(solution)/shard_map/ppermute | solution.py:454
  55.9 19.4 %copy-start.2 = (s32[32]{0:T(128)S(1)}, s32[32]{0:T(128)}, u32[]{:S(2)}) copy-start(s32[32]{0:T(128)} %order.1) | copy-start | bytes 388
